TPU v7x, 128 devices: a whole 4x4x4 slice. The times are simulated.
128 devices in a mesh: gx: 16 (over y_hi, z, core), gy: 8 (over y_lo, x).
Axes of the slice: x: 4, y: 4 (y_hi: 2, y_lo: 2; y = y_hi * 2 + y_lo), z: 4, core: 2. Of those that a mesh axis runs over, the one named last changes fastest.
Arguments:
- prev_wave: float32 [32, 512, 4096], P(None, 'gy', 'gx'), may hold values from -6 to 6
- source: float32 [32, 512, 4096], P(None, 'gy', 'gx'), may hold values from -6 to 6
- start_state: float32 [512, 4096], P('gy', 'gx'), may hold values from -6 to 6
- storage: float32 [512, 4096], P('gy', 'gx'), may hold values from 0.5 to 4
- leakage: float32 [512, 4096], P('gy', 'gx'), may hold values from 0.1 to 1
- cond_east: float32 [512, 4096], P('gy', 'gx'), may hold values from 0.5 to 2
- cond_south: float32 [512, 4096], P('gy', 'gx'), may hold values from 0.5 to 2
- owner_weight: int32 [512, 4096], P('gy', 'gx'), may hold values from 1 to 3
- aggregate: int32 [512, 4096], P('gy', 'gx'), may hold values from 0 to 8191, as said below
- coarse_inverse: float32 [8192, 8192], P(('gx', 'gy')), as said below
Outputs:
- relaxed: float32 [32, 512, 4096], P(None, 'gy', 'gx')
Inputs may be any that keep to these rules, and one draw needn't show every extreme that they name: coarse_inverse is exactly symmetric, with diagonal entries from 1 / 256 to 4 / 256. `aggregate`: the nodes of tile (a, b) carry exactly the aggregates (b * 8 + a) * 64 to (b * 8 + a + 1) * 64 - 1, each of them inside that tile.
All inputs are finite; a program needn't handle non-finite values.
Results may differ from a plain program's by a relative error of at most 0.0003.
Values sent between devices are 32-bit elements; how exact they have to be, the bound alone decides.
No kernel may reach another device: no remote copies, remote signals or barrier semaphores. Data moves between devices by JAX's collectives and lax.ppermute only.
A program may use at most 128 MiB of HBM per device.

v0:
```python
import jax
import jax.numpy as jnp
from jax import lax
from jax.sharding import PartitionSpec as P

DEG = 8
OV = 2


cheb_theta = 1.0
cheb_delta = 0.95


def padded_2(block, sides, width):
    for axis, dim in sides:
        count = lax.axis_size(axis)
        forward = [(i, i + 1) for i in range(count - 1)]
        backward = [(target, source) for source, target in forward]
        low = lax.ppermute(
            lax.slice_in_dim(block, block.shape[dim] - width, None, axis=dim), axis, forward
        )
        high = lax.ppermute(lax.slice_in_dim(block, 0, width, axis=dim), axis, backward)
        block = jnp.concatenate([low, block, high], axis=dim)
    return block


def apply_operator(full, diagonal_mid, east_mid, east_west, south_mid, south_north):
    centre = full[1:-1, 1:-1]
    return (
        diagonal_mid * centre
        - east_mid * full[1:-1, 2:]
        - east_west * full[1:-1, :-2]
        - south_mid * full[2:, 1:-1]
        - south_north * full[:-2, 1:-1]
    )


def local_sweep(stack, steps_count):
    prev_full = stack[:steps_count]
    source_mid = stack[steps_count : 2 * steps_count, 1:-1, 1:-1]
    start_mid = stack[2 * steps_count, 1:-1, 1:-1]
    storage_full = stack[2 * steps_count + 1]
    leakage_full = stack[2 * steps_count + 2]
    east_full = stack[2 * steps_count + 3]
    south_full = stack[2 * steps_count + 4]
    present_full = stack[2 * steps_count + 5]
    east_mid = east_full[1:-1, 1:-1]
    east_west = east_full[1:-1, :-2]
    south_mid = south_full[1:-1, 1:-1]
    south_north = south_full[:-2, 1:-1]
    storage_mid = storage_full[1:-1, 1:-1]
    diagonal_mid = (
        storage_mid
        + leakage_full[1:-1, 1:-1]
        + east_mid
        + east_west
        + south_mid
        + south_north
        + (1.0 - present_full[1:-1, 1:-1])
    )
    inner_mask = jnp.pad(jnp.ones_like(storage_mid), 1) > 0.5
    sigma = cheb_theta / cheb_delta

    def advance(carried, inputs):
        cycle_full, source_now = inputs
        rhs = source_now + storage_mid * carried

        def residual_of(interior):
            full = jnp.where(inner_mask, jnp.pad(interior, 1), cycle_full)
            return rhs - apply_operator(
                full, diagonal_mid, east_mid, east_west, south_mid, south_north
            )

        iterate = cycle_full[1:-1, 1:-1]
        update = residual_of(iterate) / diagonal_mid / cheb_theta
        iterate = iterate + update
        rho_prev = 1.0 / sigma
        for degree in range(1, DEG):
            rho_now = 1.0 / (2.0 * sigma - rho_prev)
            update = rho_now * rho_prev * update + 2.0 * rho_now / cheb_delta * (
                residual_of(iterate) / diagonal_mid
            )
            iterate = iterate + update
            rho_prev = rho_now
        return (iterate, iterate)

    final_state, waves = lax.scan(advance, start_mid, (prev_full, source_mid), unroll=8)
    return waves


def collect_rims(returned, rows_dev, cols_dev):
    lower = rows_dev + 3 * OV
    rightmost = cols_dev + 3 * OV
    incoming = jnp.zeros((returned.shape[0], rows_dev, cols_dev), returned.dtype)
    incoming = incoming.at[:, :OV, :].add(returned[:, :OV, 2 * OV : 2 * OV + cols_dev])
    incoming = incoming.at[:, rows_dev - OV :, :].add(
        returned[:, lower:, 2 * OV : 2 * OV + cols_dev]
    )
    incoming = incoming.at[:, :, :OV].add(returned[:, 2 * OV : 2 * OV + rows_dev, :OV])
    incoming = incoming.at[:, :, cols_dev - OV :].add(
        returned[:, 2 * OV : 2 * OV + rows_dev, rightmost:]
    )
    incoming = incoming.at[:, :OV, :OV].add(returned[:, :OV, :OV])
    incoming = incoming.at[:, :OV, cols_dev - OV :].add(returned[:, :OV, rightmost:])
    incoming = incoming.at[:, rows_dev - OV :, :OV].add(returned[:, lower:, :OV])
    incoming = incoming.at[:, rows_dev - OV :, cols_dev - OV :].add(returned[:, lower:, rightmost:])
    return incoming


def shards(
    prev_wave,
    source,
    start_state,
    storage,
    leakage,
    cond_east,
    cond_south,
    owner_weight,
    aggregate,
    coarse_inverse,
):
    steps_count, rows_dev, cols_dev = prev_wave.shape
    rows_all = rows_dev * lax.axis_size("gy")
    cols_all = cols_dev * lax.axis_size("gx")
    col_ids = lax.axis_index("gx") * cols_dev + lax.broadcasted_iota(
        jnp.int32, (rows_dev, cols_dev), 1
    )
    row_ids = lax.axis_index("gy") * rows_dev + lax.broadcasted_iota(
        jnp.int32, (rows_dev, cols_dev), 0
    )
    east = jnp.where(col_ids < cols_all - 1, cond_east, jnp.zeros_like(cond_east))
    south = jnp.where(row_ids < rows_all - 1, cond_south, jnp.zeros_like(cond_south))
    cycle = OV + 1
    stack = jnp.concatenate(
        [
            prev_wave,
            source,
            start_state[None],
            storage[None],
            leakage[None],
            east[None],
            south[None],
            jnp.ones_like(storage)[None],
        ],
        0,
    )
    padded = padded_2(stack, (("gx", 2), ("gy", 1)), cycle)
    waves = local_sweep(padded, steps_count)
    folded = jnp.concatenate([waves, jnp.ones_like(waves[:1])], 0)
    returned = padded_2(folded, (("gx", 2), ("gy", 1)), OV)
    incoming = collect_rims(returned, rows_dev, cols_dev)
    own = waves[:, OV : OV + rows_dev, OV : OV + cols_dev]
    weight = owner_weight.astype(jnp.float32)
    settled = (weight * own + incoming[:steps_count]) / (weight + incoming[steps_count])
    upad = padded_2(settled, (("gx", 2), ("gy", 1)), 1)
    east_west = padded[
        2 * steps_count + 3, cycle : cycle + rows_dev, cycle - 1 : cycle - 1 + cols_dev
    ]
    south_north = padded[
        2 * steps_count + 4, cycle - 1 : cycle - 1 + rows_dev, cycle : cycle + cols_dev
    ]
    diagonal_entries = storage + leakage + east + east_west + south + south_north
    image = (
        diagonal_entries * settled
        - east * upad[:, 1:-1, 2:]
        - east_west * upad[:, 1:-1, :-2]
        - south * upad[:, 2:, 1:-1]
        - south_north * upad[:, :-2, 1:-1]
    )
    before = jnp.concatenate([start_state[None], settled[:-1]], 0)
    resid = source + storage * before - image
    own_aggs = coarse_inverse.shape[0]
    tile_number = lax.axis_index("gx") * lax.axis_size("gy") + lax.axis_index("gy")
    local_ids = aggregate.reshape(-1) - tile_number * own_aggs
    one_hot = jnp.where(
        local_ids[:, None] == lax.broadcasted_iota(jnp.int32, (1, own_aggs), 1),
        jnp.float32(1.0),
        jnp.float32(0.0),
    )
    own_coarse = lax.dot_general(
        one_hot,
        resid.reshape(steps_count, -1),
        (((0,), (1,)), ((), ())),
        precision=lax.Precision.HIGHEST,
        preferred_element_type=jnp.float32,
    )
    correction = jnp.dot(
        coarse_inverse,
        lax.all_gather(own_coarse, ("gx", "gy"), axis=0, tiled=True),
        precision=lax.Precision.HIGHEST,
        preferred_element_type=jnp.float32,
    )
    prolonged = jnp.dot(
        one_hot, correction, precision=lax.Precision.HIGHEST, preferred_element_type=jnp.float32
    )
    return settled + prolonged.T.reshape(steps_count, rows_dev, cols_dev)


def solution(mesh):
    return jax.shard_map(
        shards,
        mesh=mesh,
        in_specs=(
            P(None, "gy", "gx"),
            P(None, "gy", "gx"),
            P("gy", "gx"),
            P("gy", "gx"),
            P("gy", "gx"),
            P("gy", "gx"),
            P("gy", "gx"),
            P("gy", "gx"),
            P("gy", "gx"),
            P(("gx", "gy"), None),
        ),
        out_specs=P(None, "gy", "gx"),
        check_vma=False,
    )
```

profile of v0, /device:TPU:0, one launch (start us, length us, event | category | flops | bytes accessed | tf_op | source)
XLA Modules:
  0.0 926.9 jit_solution(2154771409516820878)
XLA Ops:
  10.5 3.5 fusion.665
  32.2 3.7 collective-permute-start.2
  37.8 6.0 collective-permute-done.2
  43.8 4.7 collective-permute-done.3
  48.5 3.8 pad_maximum_fusion
  58.2 309.7 %while.22 = (s32[]{:T(128)}, f32[68,260]{1,0:T(8,128)S(1)}, f32[4,8,68,260]{3,2,1,0:T(8,128)}, f32[4,8,70,262]{3,2,1,0:T(8,128)}, f32[4,8,68,260]{3,2,1,0:T(8,12...) while((s32[]{:T(128)}, f32[68,260]{1,0:T(8,128)S(1)}, ...), condition=%wide.region_1.2_spmd, body=%wide.region_0.1_spmd.sunk | while | flops 19737768 | bytes 98721776 | solution.py:87
  367.9 5.6 copy.99
  374.3 3.8 collective-permute-start.4
  385.3 5.8 fusion.664
  391.0 5.0 copy.100
  400.1 5.0 copy.102
  407.2 4.7 collective-permute-done.7
  419.1 5.1 scatter-add.26
  424.2 47.5 %scatter-add.29 = f32[33,64,256]{1,0,2:T(8,128)} dynamic-update-slice(f32[33,64,256]{1,0,2:T(8,128)} %scatter-add.26, f32[33,2,256]{1,0,2:T(8,128)} %copy.126, s32[]{:T(128)} %constant.335.clone.1, s32[]{:T(128)} %constant.346.clone.1, s32[]{:T(128)} %constant.335.clone.1) | dynamic-update-slice | bytes 135172 | tf_op jit(solution)/shard_map/scatter-add | solution.py:96
  488.6 4.9 fusion.525
  495.5 3.6 collective-permute-start.9
  500.6 5.6 copy.110
  509.9 4.8 fusion.666
  514.8 4.4 copy.116
  519.2 4.3 copy.119
  523.5 5.6 collective-permute-start.11
  531.7 3.7 collective-permute-done.10
  535.3 4.8 copy.117
  540.1 4.6 copy.120
  544.7 22.2 %fusion.672 = f32[4,8,64,256]{2,1,0,3:T(8,128)} fusion(f32[32,64,1]{1,0,2:T(8,128)S(1)} %collective-permute-done.8, f32[32,64,256]{1,0,2:T(8,128)} %copy-done.4, f32[32,64,1]{1,0,2:T(8,128)S(1)} %collective-permute-done.9, f32[32,1,258]{1,0,2:T(8,128)} %copy.120, f32[64,256]{0,1:T(8,128)S(1)} %copy.118, f32[32,1,258]{1,0,2:T(8,128)} %copy.117, ...), kind=kLoop, calls=%fused_computation.1076 | loop fusion | flops 11010048 | bytes 8864256
  566.9 4.8 copy.132
  571.7 5.9 fusion.533
  577.7 310.7 %all-gather.3.cloned.1.call-done = f32[128,64,32]{1,2,0:T(8,128)} async-done(((f32[1,64,32]{1,2,0:T(8,128)}), f32[128,64,32]{1,2,0:T(8,128)}) %all-gather.3.cloned.1.call-update) | async-done | bytes 1048592 | tf_op jit(solution)/shard_map/all_gather | solution.py:189
  888.3 4.1 copy.122
  903.0 5.6 copy.123
  908.6 6.5 add.1047
  915.1 4.6 copy.124
  (663 shorter events, 382.3 us)
Async XLA Ops:
  6.5 889.1 %copy-start = (f32[64,8192]{1,0:T(8,128)S(1)}, f32[64,8192]{1,0:T(8,128)}, u32[]{:S(2)}) copy-start(f32[64,8192]{1,0:T(8,128)} %param.37) | copy-start | bytes 6291460
  6.5 881.8 %all-gather.3.cloned.1.call-start = ((), (), s32[]{:S(2)}) async-start(), calls=%async_computation | async-start | bytes 2113536 | tf_op jit(solution)/shard_map/all_gather | solution.py:189
  6.6 3.2 copy-start.17
  10.5 3.7 copy-start.1
  17.0 5.5 collective-permute-start
  21.2 5.4 collective-permute-start.1
  26.6 21.9 %slice-start = ((s8[4587520]{0:T(1024)(128)(4,1)}), s8[393216]{0:T(1024)(128)(4,1)S(1)}, s32[]{:S(2)}) async-start(s8[4587520]{0:T(1024)(128)(4,1)} %bitcast.308), calls=%async_computation.1 | async-start | bytes 786432
  29.8 18.7 %slice-start.1 = ((s8[4587520]{0:T(1024)(128)(4,1)}), s8[4194304]{0:T(1024)(128)(4,1)S(1)}, s32[]{:S(2)}) async-start(s8[4587520]{0:T(1024)(128)(4,1)} %bitcast.308), calls=%async_computation.2 | async-start | bytes 8388608
  29.8 18.7 %copy-start.2 = (f32[70,64,3]{2,1,0:T(8,128)S(1)}, f32[70,64,3]{2,1,0:T(8,128)}, u32[]{:S(2)}) copy-start(f32[70,64,3]{2,1,0:T(8,128)} %copy.97) | copy-start | bytes 161284
  29.8 18.7 %copy-start.3 = (f32[70,64,3]{2,1,0:T(8,128)S(1)}, f32[70,64,3]{2,1,0:T(8,128)}, u32[]{:S(2)}) copy-start(f32[70,64,3]{2,1,0:T(8,128)} %copy.98) | copy-start | bytes 161284
  32.2 11.6 %collective-permute-start.2 = (f32[70,3,262]{2,1,0:T(4,128)S(1)}, f32[70,3,262]{2,1,0:T(4,128)S(1)}, u32[]{:S(2)}, u32[]{:S(2)}) collective-permute-start(f32[70,3,262]{2,1,0:T(4,128)S(1)} %get-tuple-element.450), channel_id=1, source_target_pairs={{0,1},{1,2},{2,3},{3,4},{4,5},{5,6},{6,7},{8,9},{9,10},{10,11},{11... | collective-permute-start | bytes 660248 | tf_op jit(solution)/shard_map/ppermute | solution.py:19
  35.9 12.6 %collective-permute-start.3 = (f32[70,3,262]{2,1,0:T(4,128)S(1)}, f32[70,3,262]{2,1,0:T(4,128)S(1)}, u32[]{:S(2)}, u32[]{:S(2)}) collective-permute-start(f32[70,3,262]{2,1,0:T(4,128)S(1)} %get-tuple-element.451), channel_id=1, source_target_pairs={{1,0},{2,1},{3,2},{4,3},{5,4},{6,5},{7,6},{9,8},{10,9},{11,10},{12... | collective-permute-start | bytes 660248 | tf_op jit(solution)/shard_map/ppermute | solution.py:22
  43.8 14.3 %copy-start.5 = (f32[70,3,262]{2,1,0:T(4,128)}, f32[70,3,262]{2,1,0:T(4,128)S(1)}, u32[]{:S(2)}) copy-start(f32[70,3,262]{2,1,0:T(4,128)S(1)} %collective-permute-done.2) | copy-start | bytes 660244
  367.9 11.5 %copy-start.21 = (s32[2]{0:T(128)S(1)}, s32[2]{0:T(128)}, u32[]{:S(2)}) copy-start(s32[2]{0:T(128)} %iota_multiply_fusion) | copy-start | bytes 28
  367.9 11.5 %copy-start.22 = (s32[3]{0:T(128)S(1)}, s32[3]{0:T(128)}, u32[]{:S(2)}) copy-start(s32[3]{0:T(128)} %constant.349.clone.1) | copy-start | bytes 40
  367.9 12.3 %copy-start.18 = (s32[64,256]{1,0:T(8,128)S(1)}, s32[64,256]{1,0:T(8,128)}, u32[]{:S(2)}) copy-start(s32[64,256]{1,0:T(8,128)} %param.35) | copy-start | bytes 196612
  374.3 8.8 collective-permute-start.4
  378.1 6.8 collective-permute-start.5
  396.0 10.3 %collective-permute-start.6 = (f32[33,2,264]{2,0,1:T(8,128)S(1)}, f32[33,2,264]{2,0,1:T(8,128)S(1)}, u32[]{:S(2)}, u32[]{:S(2)}) collective-permute-start(f32[33,2,264]{2,0,1:T(8,128)S(1)} %copy.100), channel_id=1, source_target_pairs={{0,1},{1,2},{2,3},{3,4},{4,5},{5,6},{6,7},{8,9},{9,10},{10,11},{11... | collective-permute-start | bytes 209096 | tf_op jit(solution)/shard_map/ppermute | solution.py:19
  405.1 6.8 collective-permute-start.7
  488.5 11.9 %copy-start.19 = (s32[64,256]{1,0:T(8,128)S(1)}, s32[64,256]{1,0:T(8,128)}, u32[]{:S(2)}) copy-start(s32[64,256]{1,0:T(8,128)} %param.36) | copy-start | bytes 196612
  488.6 12.0 %copy-start.11 = (f32[64,256]{1,0:T(8,128)S(1)}, f32[64,256]{1,0:T(8,128)}, u32[]{:S(2)}) copy-start(f32[64,256]{1,0:T(8,128)} %param.31) | copy-start | bytes 196612
  495.5 11.4 %copy-start.15 = (f32[64,256]{1,0:T(8,128)S(1)}, f32[64,256]{1,0:T(8,128)}, u32[]{:S(2)}) copy-start(f32[64,256]{1,0:T(8,128)} %param.30) | copy-start | bytes 196612
  495.5 11.5 %copy-start.9 = (f32[64,256]{1,0:T(8,128)S(1)}, f32[64,256]{1,0:T(8,128)}, u32[]{:S(2)}) copy-start(f32[64,256]{1,0:T(8,128)} %get-tuple-element.420) | copy-start | bytes 196612
  495.5 11.6 %copy-start.8 = (f32[64,256]{1,0:T(8,128)S(1)}, f32[64,256]{1,0:T(8,128)}, u32[]{:S(2)}) copy-start(f32[64,256]{1,0:T(8,128)} %get-tuple-element.422) | copy-start | bytes 196612
  495.5 11.7 %collective-permute-start.9 = (f32[32,64,1]{1,0,2:T(8,128)S(1)}, f32[32,64,1]{1,0,2:T(8,128)S(1)}, u32[]{:S(2)}, u32[]{:S(2)}) collective-permute-start(f32[32,64,1]{1,0,2:T(8,128)S(1)} %get-tuple-element.460), channel_id=1, source_target_pairs={{0,8},{8,16},{16,24},{24,32},{32,40},{40,48},{48,56},{56,64},{64,7... | collective-permute-start | bytes 24584 | tf_op jit(solution)/shard_map/ppermute | solution.py:19
  499.2 8.0 collective-permute-start.8
  514.7 15.6 %copy-start.6 = (f32[70,3,262]{2,1,0:T(4,128)S(1)}, f32[70,3,262]{2,1,0:T(4,128)}, u32[]{:S(2)}) copy-start(f32[70,3,262]{2,1,0:T(4,128)} %copy-done.5) | copy-start | bytes 660244
  514.8 15.6 %copy-start.13 = (f32[64,256]{1,0:T(8,128)S(1)}, f32[64,256]{1,0:T(8,128)}, u32[]{:S(2)}) copy-start(f32[64,256]{1,0:T(8,128)} %param.32) | copy-start | bytes 196612
  523.5 16.6 %collective-permute-start.11 = (f32[32,1,258]{2,0,1:T(8,128)}, f32[32,1,258]{2,0,1:T(8,128)}, u32[]{:S(2)}, u32[]{:S(2)}) collective-permute-start(f32[32,1,258]{2,0,1:T(8,128)} %copy.119), channel_id=1, source_target_pairs={{0,1},{1,2},{2,3},{3,4},{4,5},{5,6},{6,7},{8,9},{9,10},{10,11},{11... | collective-permute-start | bytes 99080 | tf_op jit(solution)/shard_map/ppermute | solution.py:19
  529.1 6.3 collective-permute-start.10
  566.9 4.8 copy-start.20
  (6 other events, 14.5 us)
Sparse Core Ops, SparseCore 0:
  577.8 310.5 all-gather.2
where the time goes:
time: 945 us; the launch traced here: 927 us
  other arithmetic  338 us (36%)
  waiting for transfers between devices  332 us (35%)
  local copies, waits for them, and re-layouts  187 us (20%)
  starting transfers between devices  29.1 us (3%)
  loops' own time  15.2 us (2%)
  between operations  14.5 us (2%)
  matrix products  11.3 us (1%)
    all_gather x1, waiting for transfers between devices, shards(): lax.all_gather(own_coarse, ('gx', 'gy'), axis=0, tiled=True)  311 us
    add x224, other arithmetic, advance(): iterate = iterate + update  228 us
    scatter-add x1, local copies, waits for them, and re-layouts, collect_rims(): incoming.at[:, rows_dev - OV:, :]  47.5 us
    unnamed x68, local copies, waits for them, and re-layouts  28.8 us
    while x28, other arithmetic  27.6 us
    unnamed x5, other arithmetic  23.6 us
    slice x5, local copies, waits for them, and re-layouts, padded_2(): lax.slice_in_dim(block, 0, width, axis=dim)  22.9 us
    select_n x228, other arithmetic, residual_of(): full = jnp.where(inner_mask, jnp.pad(interior, 1), cycle_full)  22.2 us
  transfers between devices with their start and end apart: 13, of which 7 were waited for; matrix products, arithmetic and copies ran while one was open for 3% of the time, Pallas kernels for 0%

commit v1 on v0

--- a/solution.py
+++ b/solution.py
@@ -1,14 +1,73 @@
+import functools
+import math
+
 import jax
 import jax.numpy as jnp
+import numpy as np
 from jax import lax
+from jax.experimental import pallas as pl
+from jax.experimental.pallas import tpu as pltpu
 from jax.sharding import PartitionSpec as P
 
 DEG = 8
 OV = 2
+STRIDE = 9
+LANES = 128
+SUB = 8
 
 
 cheb_theta = 1.0
 cheb_delta = 0.95
+
+
+def horner_coefficients():
+    t8 = np.array([1.0, -32.0, 160.0, -256.0, 128.0])
+    u_scale = 1.0 / cheb_delta**2
+    at_one = sum(c * u_scale**k for k, c in enumerate(t8))
+    g = -np.array([c * u_scale**k for k, c in enumerate(t8)]) / at_one
+    g[0] += 1.0
+    q = np.zeros(4)
+    total = 0.0
+    for k in range(4):
+        total += g[k]
+        q[k] = total
+    return q
+
+
+Q_COEF = horner_coefficients()
+
+
+def lane_ids():
+    return lax.broadcasted_iota(jnp.int32, (SUB, LANES), 1)
+
+
+def row_ids_of(j):
+    return lax.broadcasted_iota(jnp.int32, (SUB, LANES), 0) * STRIDE + j
+
+
+def east_of(x):
+    return pltpu.roll(x, LANES - 1, 1)
+
+
+def west_of(x):
+    return pltpu.roll(x, 1, 1)
+
+
+def south_list(xs):
+    return xs[1:] + [pltpu.roll(xs[0], SUB - 1, 0)]
+
+
+def north_list(xs):
+    return [pltpu.roll(xs[-1], 1, 0)] + xs[:-1]
+
+
+def off_diagonal(xs, east, south):
+    from_north = north_list([s * x for s, x in zip(south, xs)])
+    from_south = [s * x for s, x in zip(south, south_list(xs))]
+    out = []
+    for j, x in enumerate(xs):
+        out.append((west_of(east[j] * x) + east[j] * east_of(x)) + (from_north[j] + from_south[j]))
+    return out
 
 
 def padded_2(block, sides, width):
@@ -24,68 +83,136 @@
     return block
 
 
-def apply_operator(full, diagonal_mid, east_mid, east_west, south_mid, south_north):
-    centre = full[1:-1, 1:-1]
+def windows_of(left, right, halo_left, halo_right, lanes):
     return (
-        diagonal_mid * centre
-        - east_mid * full[1:-1, 2:]
-        - east_west * full[1:-1, :-2]
-        - south_mid * full[2:, 1:-1]
-        - south_north * full[:-2, 1:-1]
-    )
+        jnp.where(lanes < LANES - 3, left, halo_left),
+        jnp.where(lanes < LANES // 2, right, left),
+        jnp.where(lanes < 3, halo_right, right),
+    )
+
+
+def sweep_kernel(pT, sT, cT, pX, sX, cX, out, rims, coef, carry):
+    step0 = pl.program_id(0)
+    block_steps = pT.shape[0]
+    lanes = lane_ids()
+    rows = lambda j: pl.ds(j, SUB, stride=STRIDE)
+
+    def window_set(j, tile_left, tile_right, xref, slot):
+        left = pltpu.roll(xref[0, rows(j), :], (2 * LANES - 3 - 4 * slot) % LANES, 1)
+        right = pltpu.roll(xref[1, rows(j), :], (2 * LANES - 4 * slot) % LANES, 1)
+        return windows_of(tile_left, tile_right, left, right, lanes)
+
+    breaks = (LANES - 4, LANES // 2 - 1, 2)
+    outer = (LANES - 3, -1, 2)
+
+    @pl.when(step0 == 0)
+    def _():
+        planes = [[window_set(j, cT[p, 0, rows(j), :], cT[p, 1, rows(j), :], cX, p) for j in range(STRIDE)] for p in range(5)]
+        for w in range(3):
+            start, storage, leakage, east, south = [[planes[p][j][w] for j in range(STRIDE)] for p in range(5)]
+            east = [jnp.where(lanes == breaks[w], 0.0, e) for e in east]
+            north = north_list(south)
+            diag, scale = [], []
+            for j in range(STRIDE):
+                d = storage[j] + leakage[j] + east[j] + west_of(east[j]) + south[j] + north[j]
+                row = row_ids_of(j)
+                inner = ((row < 66) | (row > 69)) & (lanes != outer[w]) & (d > 0.0)
+                diag.append(d)
+                scale.append(jnp.where(inner, 1.0 / jnp.sqrt(jnp.where(inner, d, 1.0)), 0.0))
+            scale_south = south_list(scale)
+            for j in range(STRIDE):
+                carry[w, j] = start[j]
+                coef[0, w, j] = east[j] * scale[j] * east_of(scale[j])
+                coef[1, w, j] = south[j] * scale[j] * scale_south[j]
+                coef[2, w, j] = storage[j]
+                coef[3, w, j] = diag[j]
+                coef[4, w, j] = east[j]
+                coef[5, w, j] = south[j]
+                coef[6, w, j] = scale[j]
+                coef[7, w, j] = scale[j] * np.float32(Q_COEF[3])
+        for side in range(2):
+            rims[side] = jnp.zeros_like(rims[side])
+
+    def step(i, _):
+        t = step0 * block_steps + i
+        prev = [window_set(j, pT[i, 0, rows(j), :], pT[i, 1, rows(j), :], pX, t) for j in range(STRIDE)]
+        srcs = [window_set(j, sT[i, 0, rows(j), :], sT[i, 1, rows(j), :], sX, t) for j in range(STRIDE)]
+        result = []
+        for w in range(3):
+            x0 = [prev[j][w] for j in range(STRIDE)]
+            full = off_diagonal(x0, [coef[4, w, j] for j in range(STRIDE)], [coef[5, w, j] for j in range(STRIDE)])
+            z = [
+                coef[6, w, j] * ((srcs[j][w] + coef[2, w, j] * carry[w, j]) + (full[j] - coef[3, w, j] * x0[j]))
+                for j in range(STRIDE)
+            ]
+            east = [coef[0, w, j] for j in range(STRIDE)]
+            south = [coef[1, w, j] for j in range(STRIDE)]
+            base = [a + b for a, b in zip(z, off_diagonal(z, east, south))]
+            y = base
+            for k in (2, 1, 0):
+                y = off_diagonal(off_diagonal(y, east, south), east, south)
+                ratio = np.float32(Q_COEF[k] / Q_COEF[3])
+                y = [a + ratio * b for a, b in zip(y, base)]
+            result.append([x0[j] + coef[7, w, j] * y[j] for j in range(STRIDE)])
+        for j in range(STRIDE):
+            a, b, c = result[0][j], result[1][j], result[2][j]
+            left = jnp.where(lanes < 96, a, b)
+            right = jnp.where(lanes < 32, b, c)
+            out[i, 0, rows(j), :] = left
+            out[i, 1, rows(j), :] = right
+            fresh = windows_of(left, right, a, c, lanes)
+            for w in range(3):
+                carry[w, j] = fresh[w]
+            slot = 4 * t
+            here = (lanes >= slot) & (lanes < slot + 3)
+            rims[0, rows(j), :] = jnp.where(here, pltpu.roll(a, (slot + 2) % LANES, 1), rims[0, rows(j), :])
+            rims[1, rows(j), :] = jnp.where(here, pltpu.roll(c, (slot + 1) % LANES, 1), rims[1, rows(j), :])
+        return 0
+
+    lax.fori_loop(0, block_steps, step, 0)
+
+
+def sweep(pT, sT, cT, pX, sX, cX):
+    steps = pT.shape[0]
+    block = 4
+    rows = pT.shape[2]
+    big = pl.BlockSpec((block, 2, rows, LANES), lambda i: (i, 0, 0, 0))
+    const = lambda a: pl.BlockSpec(a.shape, lambda i: (0,) * a.ndim)
+    return pl.pallas_call(
+        sweep_kernel,
+        grid=(steps // block,),
+        in_specs=[big, big, const(cT), const(pX), const(sX), const(cX)],
+        out_specs=[big, pl.BlockSpec((2, rows, LANES), lambda i: (0, 0, 0))],
+        out_shape=[jax.ShapeDtypeStruct(pT.shape, jnp.float32), jax.ShapeDtypeStruct((2, rows, LANES), jnp.float32)],
+        scratch_shapes=[pltpu.VMEM((8, 3, STRIDE, SUB, LANES), jnp.float32), pltpu.VMEM((3, STRIDE, SUB, LANES), jnp.float32)],
+        compiler_params=pltpu.CompilerParams(vmem_limit_bytes=48 * 1024 * 1024),
+        name="sweep",
+    )(pT, sT, cT, pX, sX, cX)
+
+
+def circular(x):
+    pad = jnp.zeros(x.shape[:-2] + (2,) + x.shape[-1:], x.dtype)
+    return jnp.concatenate([x[..., 3:, :], pad, x[..., :3, :]], axis=-2)
+
+
+def tiles_and_sides(x):
+    x = circular(x)
+    tiles = jnp.stack([x[..., 3:131], x[..., 131:259]], 1)
+    sides = []
+    for s in (x[..., 0:3], x[..., 259:262]):
+        s = jnp.pad(s, ((0, 32 - s.shape[0]), (0, 0), (0, 1)))
+        sides.append(jnp.transpose(s, (1, 0, 2)).reshape(72, LANES))
+    return tiles, jnp.stack(sides)
 
 
 def local_sweep(stack, steps_count):
-    prev_full = stack[:steps_count]
-    source_mid = stack[steps_count : 2 * steps_count, 1:-1, 1:-1]
-    start_mid = stack[2 * steps_count, 1:-1, 1:-1]
-    storage_full = stack[2 * steps_count + 1]
-    leakage_full = stack[2 * steps_count + 2]
-    east_full = stack[2 * steps_count + 3]
-    south_full = stack[2 * steps_count + 4]
-    present_full = stack[2 * steps_count + 5]
-    east_mid = east_full[1:-1, 1:-1]
-    east_west = east_full[1:-1, :-2]
-    south_mid = south_full[1:-1, 1:-1]
-    south_north = south_full[:-2, 1:-1]
-    storage_mid = storage_full[1:-1, 1:-1]
-    diagonal_mid = (
-        storage_mid
-        + leakage_full[1:-1, 1:-1]
-        + east_mid
-        + east_west
-        + south_mid
-        + south_north
-        + (1.0 - present_full[1:-1, 1:-1])
-    )
-    inner_mask = jnp.pad(jnp.ones_like(storage_mid), 1) > 0.5
-    sigma = cheb_theta / cheb_delta
-
-    def advance(carried, inputs):
-        cycle_full, source_now = inputs
-        rhs = source_now + storage_mid * carried
-
-        def residual_of(interior):
-            full = jnp.where(inner_mask, jnp.pad(interior, 1), cycle_full)
-            return rhs - apply_operator(
-                full, diagonal_mid, east_mid, east_west, south_mid, south_north
-            )
-
-        iterate = cycle_full[1:-1, 1:-1]
-        update = residual_of(iterate) / diagonal_mid / cheb_theta
-        iterate = iterate + update
-        rho_prev = 1.0 / sigma
-        for degree in range(1, DEG):
-            rho_now = 1.0 / (2.0 * sigma - rho_prev)
-            update = rho_now * rho_prev * update + 2.0 * rho_now / cheb_delta * (
-                residual_of(iterate) / diagonal_mid
-            )
-            iterate = iterate + update
-            rho_prev = rho_now
-        return (iterate, iterate)
-
-    final_state, waves = lax.scan(advance, start_mid, (prev_full, source_mid), unroll=8)
-    return waves
+    pT, pX = tiles_and_sides(stack[:steps_count])
+    sT, sX = tiles_and_sides(stack[steps_count : 2 * steps_count])
+    cT, cX = tiles_and_sides(stack[2 * steps_count : 2 * steps_count + 5])
+    out, rims = sweep(pT, sT, cT, pX, sX, cX)
+    rims = jnp.transpose(rims.reshape(2, 72, 32, 4), (0, 2, 1, 3))
+    full = jnp.concatenate([rims[0, :, :, 0:2], out[:, 0], out[:, 1], rims[1, :, :, 1:3]], axis=-1)
+    return jnp.concatenate([full[:, 70:72], full[:, :66]], axis=1)
 
 
 def collect_rims(returned, rows_dev, cols_dev):
@@ -105,6 +232,15 @@
     incoming = incoming.at[:, rows_dev - OV :, :OV].add(returned[:, lower:, :OV])
     incoming = incoming.at[:, rows_dev - OV :, cols_dev - OV :].add(returned[:, lower:, rightmost:])
     return incoming
+
+
+def gather_all(own):
+    count = lax.axis_size("gx") * lax.axis_size("gy")
+    block = own.reshape(1, 1, own.size)
+    every = lax.all_to_all(
+        jnp.broadcast_to(block, (count,) + block.shape[1:]), ("gx", "gy"), 0, 0
+    )
+    return every.reshape(count * own.shape[0], own.shape[1])
 
 
 def shards(
@@ -186,7 +322,7 @@
     )
     correction = jnp.dot(
         coarse_inverse,
-        lax.all_gather(own_coarse, ("gx", "gy"), axis=0, tiled=True),
+        gather_all(own_coarse),
         precision=lax.Precision.HIGHEST,
         preferred_element_type=jnp.float32,
     )

time: 945 us -> 344 us (0.36); the launches traced: 927 us -> 342 us
  waiting for transfers between devices: 332 us -> 12.4 us
  other arithmetic: 338 us -> 42.1 us
  blocking collectives: 0 us -> 45.4 us
  local copies, waits for them, and re-layouts: 187 us -> 144 us
  Pallas kernels: 0 us -> 35.8 us
  starting transfers between devices: 29.1 us -> 46.1 us
  loops' own time: 15.2 us -> 0 us
  between operations: 14.5 us -> 1.04 us
    all_gather x1 -> x0, waiting for transfers between devices: 311 us -> none  [shards(): lax.all_gather(own_coarse, ('gx', 'gy'), axis=0, tiled=True)]
    add x224 -> x2, other arithmetic: 228 us -> 4.04 us  [the longest x1 2.89 us: collect_rims(): incoming.at[:, :, cols_dev - OV:]]
    scatter-add x1, local copies, waits for them, and re-layouts: 47.5 us -> 1.05 us  [collect_rims(): incoming.at[:, rows_dev - OV:, :]]
    all_to_all x0 -> x1, blocking collectives: none -> 45.4 us  [gather_all(): lax.all_to_all(jnp.broadcast_to(block, (count,) + block.shape[1:]), ('gx'...]
    pallas_call x0 -> x1, Pallas kernels: none -> 35.8 us  [sweep(): pl.pallas_call(sweep_kernel, grid=(steps // block,), in_specs=[big, big,...]
    while x28 -> x0, other arithmetic: 27.6 us -> none
    unnamed x5 -> x4, other arithmetic: 23.6 us -> 0.74 us
    select_n x228 -> x0, other arithmetic: 22.2 us -> none  [residual_of(): full = jnp.where(inner_mask, jnp.pad(interior, 1), cycle_full)]
  transfers between devices with their start and end apart: 13 -> 12, of which waited for: 7 -> 5; matrix products, arithmetic and copies ran while one was open for 3% -> 5% of each run, Pallas kernels for 0% -> 0%
where the time goes in v1:
time: 344 us; the launch traced here: 342 us
  local copies, waits for them, and re-layouts  144 us (42%)
  starting transfers between devices  46.1 us (13%)
  blocking collectives  45.4 us (13%)
  other arithmetic  42.1 us (12%)
  Pallas kernels  35.8 us (10%)
  matrix products  14.9 us (4%)
  waiting for transfers between devices  12.4 us (4%)
    all_to_all x1, blocking collectives, gather_all(): lax.all_to_all(jnp.broadcast_to(block, (count,) + block.shape[1:]), ('gx'...  45.4 us
    ppermute x6, starting transfers between devices, padded_2(): lax.ppermute(lax.slice_in_dim(block, block.shape[dim] - width, None, axis...  38 us
    pallas_call x1, Pallas kernels, sweep(): pl.pallas_call(sweep_kernel, grid=(steps // block,), in_specs=[big, big,...  35.8 us
    transpose x9, local copies, waits for them, and re-layouts, tiles_and_sides(): sides.append(jnp.transpose(s, (1, 0, 2)).reshape(72, LANES))  19.8 us
    slice x6, local copies, waits for them, and re-layouts, padded_2(): lax.slice_in_dim(block, block.shape[dim] - width, None, axis=dim)  13.6 us
    scatter-add x1, local copies, waits for them, and re-layouts, collect_rims(): incoming.at[:, :OV, cols_dev - OV:].add(returned[:, :OV, rightmost:])  12 us
    unnamed x96, local copies, waits for them, and re-layouts  11.5 us
    scatter-add x1, local copies, waits for them, and re-layouts, collect_rims(): incoming.at[:, rows_dev - OV:, cols_dev - OV:]  10.8 us
  transfers between devices with their start and end apart: 12, of which 5 were waited for; matrix products, arithmetic and copies ran while one was open for 5% of the time, Pallas kernels for 0%

profile of v1, /device:TPU:0, one launch (start us, length us, event | category | flops | bytes accessed | tf_op | source)
XLA Modules:
  0.0 342.1 jit_solution(17872463501769611442)
XLA Ops:
  4.1 3.4 %fusion.40 = (f32[70,64,3]{2,1,0:T(8,128)}, f32[70,64,3]{2,1,0:T(8,128)}) fusion(f32[70,64,256]{2,1,0:T(8,128)S(1)} %broadcast_dynamic-update-slice_fusion), kind=kLoop, calls=%fused_computation.122 | loop fusion | bytes 215040 | tf_op jit(solution)/shard_map/slice | solution.py:79
  7.7 2.9 copy.77
  11.8 2.9 copy.78
  16.0 3.1 copy.79
  20.1 3.2 copy.80
  25.7 3.7 %collective-permute-start.3 = (f32[70,3,262]{2,1,0:T(4,128)S(1)}, f32[70,3,262]{2,1,0:T(4,128)S(1)}, u32[]{:S(2)}, u32[]{:S(2)}) collective-permute-start(f32[70,3,262]{2,1,0:T(4,128)S(1)} %get-tuple-element.113), channel_id=1, source_target_pairs={{0,1},{1,2},{2,3},{3,4},{4,5},{5,6},{6,7},{8,9},{9,10},{10,11},{11... | collective-permute-start | bytes 660248 | tf_op jit(solution)/shard_map/ppermute | solution.py:78
  31.1 6.2 %collective-permute-done.3 = f32[70,3,262]{2,1,0:T(4,128)S(1)} collective-permute-done((f32[70,3,262]{2,1,0:T(4,128)S(1)}, f32[70,3,262]{2,1,0:T(4,128)S(1)}, u32[]{:S(2)}, u32[]{:S(2)}) %collective-permute-start.3) | collective-permute-done | bytes 220112 | tf_op jit(solution)/shard_map/ppermute | solution.py:78
  37.3 4.7 %collective-permute-done.2 = f32[70,3,262]{2,1,0:T(4,128)S(1)} collective-permute-done((f32[70,3,262]{2,1,0:T(4,128)S(1)}, f32[70,3,262]{2,1,0:T(4,128)S(1)}, u32[]{:S(2)}, u32[]{:S(2)}) %collective-permute-start.2) | collective-permute-done | bytes 220112 | tf_op jit(solution)/shard_map/ppermute | solution.py:81
  43.9 3.1 pad_maximum_fusion
  50.6 3.1 slice_bitcast_fusion.4
  64.7 2.6 pad_bitcast_fusion
  75.0 3.4 fusion.26
  90.3 35.8 %sweep.1 = (f32[32,2,72,128]{3,2,1,0:T(8,128)S(1)}, f32[2,72,128]{2,1,0:T(8,128)S(1)}) custom-call(f32[32,2,72,128]{3,2,1,0:T(8,128)S(1)} %copy.94.pT, f32[32,2,72,128]{3,2,1,0:T(8,128)} %copy.95.sT, f32[5,2,72,128]{3,2,1,0:T(8,128)S(1)} %pad_maximum_fusion.20.cT, f32[2,72,128]{2,1,0:T(8,128)S(1)} %get-tuple-element.148.pX, ...), custom_call_target="tpu_custom_call" | custom-call | tf_op jit(solution)/shard_map/sweep/pallas_call | solution.py:181
  128.0 3.0 copy.98
  133.2 2.9 fusion.4
  144.7 5.0 %collective-permute-start.4 = (f32[33,68,2]{1,2,0:T(2,128)}, f32[33,68,2]{1,2,0:T(2,128)}, u32[]{:S(2)}, u32[]{:S(2)}) collective-permute-start(f32[33,68,2]{1,2,0:T(2,128)} %copy.99), channel_id=1, source_target_pairs={{0,8},{8,16},{16,24},{24,32},{32,40},{40,48},{48,56},{56,64},{64,7... | collective-permute-start | bytes 53864 | tf_op jit(solution)/shard_map/ppermute | solution.py:78
  157.9 17.3 %collective-permute-start.6 = (f32[33,2,264]{2,1,0:T(2,128)}, f32[33,2,264]{2,1,0:T(2,128)}, u32[]{:S(2)}, u32[]{:S(2)}) collective-permute-start(f32[33,2,264]{2,1,0:T(2,128)} %get-tuple-element.117), channel_id=1, source_target_pairs={{0,1},{1,2},{2,3},{3,4},{4,5},{5,6},{6,7},{8,9},{9,10},{10,11},{11... | collective-permute-start | bytes 209096 | tf_op jit(solution)/shard_map/ppermute | solution.py:78
  184.5 7.1 %scatter-add.30 = f32[33,64,256]{2,1,0:T(8,128)} dynamic-update-slice(f32[33,64,256]{2,1,0:T(8,128)} %copy-done.9, f32[33,64,2]{2,1,0:T(8,128)} %slice_add_fusion.2, s32[]{:T(128)} %constant.251.clone.1, s32[]{:T(128)} %constant.251.clone.1, s32[]{:T(128)} %constant.251.clone.1) | dynamic-update-slice | bytes 33796 | tf_op jit(solution)/shard_map/scatter-add | solution.py:226
  191.6 2.9 slice_add_fusion.1
  194.5 9.3 %scatter-add.31 = f32[33,64,256]{2,1,0:T(8,128)} dynamic-update-slice(f32[33,64,256]{2,1,0:T(8,128)} %scatter-add.30, f32[33,64,2]{2,1,0:T(8,128)} %slice_add_fusion.1, s32[]{:T(128)} %constant.251.clone.1, s32[]{:T(128)} %constant.251.clone.1, s32[]{:T(128)} %constant.253.clone.1) | dynamic-update-slice | bytes 33796 | tf_op jit(solution)/shard_map/scatter-add | solution.py:227
  204.7 3.6 %scatter-add.34 = f32[33,64,256]{2,1,0:T(8,128)} dynamic-update-slice(f32[33,64,256]{2,1,0:T(8,128)} %scatter-add.31, f32[33,2,2]{2,1,0:T(2,128)S(1)} %slice_add_fusion.5, s32[]{:T(128)} %constant.251.clone.1, s32[]{:T(128)} %constant.251.clone.1, s32[]{:T(128)} %constant.251.clone.1) | dynamic-update-slice | bytes 1060 | tf_op jit(solution)/shard_map/scatter-add | solution.py:230
  208.4 2.9 add_select_fusion
  211.2 12.0 %scatter-add.35 = f32[33,64,256]{2,1,0:T(8,128)} dynamic-update-slice(f32[33,64,256]{2,1,0:T(8,128)} %scatter-add.34, f32[33,2,2]{2,1,0:T(2,128)S(1)} %add_select_fusion, s32[]{:T(128)} %constant.251.clone.1, s32[]{:T(128)} %bitcast.30, s32[]{:T(128)} %bitcast.31) | dynamic-update-slice | bytes 1060 | tf_op jit(solution)/shard_map/scatter-add | solution.py:231
  227.5 10.8 %scatter-add.39 = f32[33,64,256]{2,1,0:T(8,128)} dynamic-update-slice(f32[33,64,256]{2,1,0:T(8,128)} %scatter-add.36, f32[33,2,2]{2,1,0:T(2,128)S(1)} %slice_add_fusion.3, s32[]{:T(128)} %constant.251.clone.1, s32[]{:T(128)} %constant.252.clone.1, s32[]{:T(128)} %constant.253.clone.1) | dynamic-update-slice | bytes 1060 | tf_op jit(solution)/shard_map/scatter-add | solution.py:233
  247.4 6.2 %collective-permute-start.9 = (f32[32,64,1]{1,0,2:T(8,128)S(1)}, f32[32,64,1]{1,0,2:T(8,128)S(1)}, u32[]{:S(2)}, u32[]{:S(2)}) collective-permute-start(f32[32,64,1]{1,0,2:T(8,128)S(1)} %copy.108), channel_id=1, source_target_pairs={{0,8},{8,16},{16,24},{24,32},{32,40},{40,48},{48,56},{56,64},{64,7... | collective-permute-start | bytes 24584 | tf_op jit(solution)/shard_map/ppermute | solution.py:78
  259.2 4.5 %collective-permute-start.11 = (f32[32,1,258]{2,1,0:T(1,128)S(1)}, f32[32,1,258]{2,1,0:T(1,128)S(1)}, u32[]{:S(2)}, u32[]{:S(2)}) collective-permute-start(f32[32,1,258]{2,1,0:T(1,128)S(1)} %get-tuple-element.121), channel_id=1, source_target_pairs={{0,1},{1,2},{2,3},{3,4},{4,5},{5,6},{6,7},{8,9},{9,10},{10,11},{11... | collective-permute-start | bytes 99080 | tf_op jit(solution)/shard_map/ppermute | solution.py:78
  267.1 2.9 fusion.10
  271.3 3.7 %fusion.2 = f32[64,32]{1,0:T(8,128)S(1)} fusion(f32[32,16384]{1,0:T(8,128)S(1)} %bitcast.81, s32[16384]{0:T(1024)S(1)} %bitcast.90), kind=kOutput, calls=%fused_computation.3 | convolution fusion | flops 404750336 | bytes 2170880 | tf_op jit(solution)/shard_map/dot_general | solution.py:316
  275.6 45.4 %all_to_all.5 = f32[128,1,2048]{2,1,0:T(1,128)} all-to-all(f32[128,1,2048]{2,1,0:T(1,128)S(1)} %broadcast_in_dim.52), channel_id=1, replica_groups=mesh['gx'=16,'gy'=8] {'gx','gy'}, dimensions={0} | all-to-all | bytes 2097152 | tf_op jit(solution)/shard_map/all_to_all | solution.py:240
  321.0 3.7 %reduce.21 = f32[128,2048]{1,0:T(8,128)S(1)} reduce(f32[128,1,2048]{2,1,0:T(1,128)} %all_to_all.5, f32[]{:T(128)} %constant.271), dimensions={1}, to_apply=%all_to_all.3.reduce_sub_computation | reduce | bytes 2097156 | tf_op jit(solution)/shard_map/all_to_all | solution.py:240
  324.7 2.8 reshape.294
  327.4 8.8 %fusion.46 = f32[32,64]{1,0:T(8,128)S(1)} fusion(f32[8192,32]{1,0:T(8,128)} %reshape.294, f32[64,8192]{1,0:T(8,128)S(1)} %copy-done), kind=kOutput, calls=%fused_computation.128 | convolution fusion | flops 201326592 | bytes 3153920 | tf_op jit(solution)/shard_map/dot_general | solution.py:323
  (194 shorter events, 108.4 us)
Async XLA Ops:
  0.0 327.4 %copy-start = (f32[64,8192]{1,0:T(8,128)S(1)}, f32[64,8192]{1,0:T(8,128)}, u32[]{:S(2)}) copy-start(f32[64,8192]{1,0:T(8,128)} %param.35) | copy-start | bytes 6291460
  4.1 3.6 %copy-start.1 = (f32[70,64,256]{2,1,0:T(8,128)}, f32[70,64,256]{2,1,0:T(8,128)S(1)}, u32[]{:S(2)}) copy-start(f32[70,64,256]{2,1,0:T(8,128)S(1)} %broadcast_dynamic-update-slice_fusion) | copy-start | bytes 13762564
  10.5 5.5 %collective-permute-start = (f32[70,64,3]{0,1,2:T(8,128)S(1)}, f32[70,64,3]{0,1,2:T(8,128)S(1)}, u32[]{:S(2)}, u32[]{:S(2)}) collective-permute-start(f32[70,64,3]{0,1,2:T(8,128)S(1)} %copy.77), channel_id=1, source_target_pairs={{0,8},{8,16},{16,24},{24,32},{32,40},{40,48},{48,56},{56,64},{64,7... | collective-permute-start | bytes 161288 | tf_op jit(solution)/shard_map/ppermute | solution.py:78
  14.7 5.4 %collective-permute-start.1 = (f32[70,64,3]{0,1,2:T(8,128)S(1)}, f32[70,64,3]{0,1,2:T(8,128)S(1)}, u32[]{:S(2)}, u32[]{:S(2)}) collective-permute-start(f32[70,64,3]{0,1,2:T(8,128)S(1)} %copy.78), channel_id=1, source_target_pairs={{8,0},{16,8},{24,16},{32,24},{40,32},{48,40},{56,48},{64,56},{72,6... | collective-permute-start | bytes 161288 | tf_op jit(solution)/shard_map/ppermute | solution.py:81
  20.1 21.9 %slice-start = ((s8[4587520]{0:T(1024)(128)(4,1)}), s8[393216]{0:T(1024)(128)(4,1)S(1)}, s32[]{:S(2)}) async-start(s8[4587520]{0:T(1024)(128)(4,1)} %bitcast.76), calls=%async_computation.1 | async-start | bytes 786432
  23.3 18.7 %slice-start.1 = ((s8[4587520]{0:T(1024)(128)(4,1)}), s8[4194304]{0:T(1024)(128)(4,1)S(1)}, s32[]{:S(2)}) async-start(s8[4587520]{0:T(1024)(128)(4,1)} %bitcast.76), calls=%async_computation.2 | async-start | bytes 8388608
  23.3 18.7 %copy-start.5 = (f32[70,64,3]{2,1,0:T(8,128)S(1)}, f32[70,64,3]{2,1,0:T(8,128)}, u32[]{:S(2)}) copy-start(f32[70,64,3]{2,1,0:T(8,128)} %copy.79) | copy-start | bytes 161284
  23.3 18.7 %copy-start.7 = (f32[70,64,3]{2,1,0:T(8,128)S(1)}, f32[70,64,3]{2,1,0:T(8,128)}, u32[]{:S(2)}) copy-start(f32[70,64,3]{2,1,0:T(8,128)} %copy.80) | copy-start | bytes 161284
  25.7 11.6 %collective-permute-start.3 = (f32[70,3,262]{2,1,0:T(4,128)S(1)}, f32[70,3,262]{2,1,0:T(4,128)S(1)}, u32[]{:S(2)}, u32[]{:S(2)}) collective-permute-start(f32[70,3,262]{2,1,0:T(4,128)S(1)} %get-tuple-element.113), channel_id=1, source_target_pairs={{0,1},{1,2},{2,3},{3,4},{4,5},{5,6},{6,7},{8,9},{9,10},{10,11},{11... | collective-permute-start | bytes 660248 | tf_op jit(solution)/shard_map/ppermute | solution.py:78
  29.4 12.6 %collective-permute-start.2 = (f32[70,3,262]{2,1,0:T(4,128)S(1)}, f32[70,3,262]{2,1,0:T(4,128)S(1)}, u32[]{:S(2)}, u32[]{:S(2)}) collective-permute-start(f32[70,3,262]{2,1,0:T(4,128)S(1)} %get-tuple-element.112), channel_id=1, source_target_pairs={{1,0},{2,1},{3,2},{4,3},{5,4},{6,5},{7,6},{9,8},{10,9},{11,10},{12... | collective-permute-start | bytes 660248 | tf_op jit(solution)/shard_map/ppermute | solution.py:81
  37.3 10.2 %copy-start.19 = (f32[70,3,262]{2,1,0:T(4,128)}, f32[70,3,262]{2,1,0:T(4,128)S(1)}, u32[]{:S(2)}) copy-start(f32[70,3,262]{2,1,0:T(4,128)S(1)} %collective-permute-done.3) | copy-start | bytes 660244
  48.2 5.4 %copy-start.11 = (f32[32,72,262]{2,1,0:T(8,128)}, f32[32,72,262]{2,1,0:T(8,128)S(1)}, u32[]{:S(2)}) copy-start(f32[32,72,262]{2,1,0:T(8,128)S(1)} %get-tuple-element.143) | copy-start | bytes 7243780
  64.7 10.3 %copy-start.40 = (pred[4]{0:T(512)(128)(4,1)S(1)}, pred[4]{0:T(512)(128)(4,1)}, u32[]{:S(2)}) copy-start(pred[4]{0:T(512)(128)(4,1)} %constant.250.clone.1) | copy-start | bytes 16
  75.0 3.4 copy-start.16
  75.0 3.4 copy-start.17
  138.7 11.0 %copy-start.41 = (s32[3]{0:T(128)S(1)}, s32[3]{0:T(128)}, u32[]{:S(2)}) copy-start(s32[3]{0:T(128)} %constant.255.clone.1) | copy-start | bytes 40
  138.7 11.7 %copy-start.29 = (s32[64,256]{1,0:T(8,128)S(1)}, s32[64,256]{1,0:T(8,128)}, u32[]{:S(2)}) copy-start(s32[64,256]{1,0:T(8,128)} %param.33) | copy-start | bytes 196612
  143.4 9.3 %collective-permute-start.5 = (f32[33,68,2]{1,2,0:T(2,128)}, f32[33,68,2]{1,2,0:T(2,128)S(1)}, u32[]{:S(2)}, u32[]{:S(2)}) collective-permute-start(f32[33,68,2]{1,2,0:T(2,128)} %copy.100), channel_id=1, source_target_pairs={{8,0},{16,8},{24,16},{32,24},{40,32},{48,40},{56,48},{64,56},{72,6... | collective-permute-start | bytes 53864 | tf_op jit(solution)/shard_map/ppermute | solution.py:81
  144.7 5.7 %collective-permute-start.4 = (f32[33,68,2]{1,2,0:T(2,128)}, f32[33,68,2]{1,2,0:T(2,128)}, u32[]{:S(2)}, u32[]{:S(2)}) collective-permute-start(f32[33,68,2]{1,2,0:T(2,128)} %copy.99), channel_id=1, source_target_pairs={{0,8},{8,16},{16,24},{24,32},{32,40},{40,48},{48,56},{56,64},{64,7... | collective-permute-start | bytes 53864 | tf_op jit(solution)/shard_map/ppermute | solution.py:78
  156.6 24.4 %collective-permute-start.7 = (f32[33,2,264]{2,1,0:T(2,128)}, f32[33,2,264]{2,1,0:T(2,128)}, u32[]{:S(2)}, u32[]{:S(2)}) collective-permute-start(f32[33,2,264]{2,1,0:T(2,128)} %get-tuple-element.116), channel_id=1, source_target_pairs={{1,0},{2,1},{3,2},{4,3},{5,4},{6,5},{7,6},{9,8},{10,9},{11,10},{12... | collective-permute-start | bytes 209096 | tf_op jit(solution)/shard_map/ppermute | solution.py:81
  157.9 21.7 %collective-permute-start.6 = (f32[33,2,264]{2,1,0:T(2,128)}, f32[33,2,264]{2,1,0:T(2,128)}, u32[]{:S(2)}, u32[]{:S(2)}) collective-permute-start(f32[33,2,264]{2,1,0:T(2,128)} %get-tuple-element.117), channel_id=1, source_target_pairs={{0,1},{1,2},{2,3},{3,4},{4,5},{5,6},{6,7},{8,9},{9,10},{10,11},{11... | collective-permute-start | bytes 209096 | tf_op jit(solution)/shard_map/ppermute | solution.py:78
  179.6 3.8 %copy-start.18 = (f32[33,64,2]{2,1,0:T(8,128)S(1)}, f32[33,64,2]{2,1,0:T(8,128)}, u32[]{:S(2)}) copy-start(f32[33,64,2]{2,1,0:T(8,128)} %copy.103) | copy-start | bytes 50692
  242.8 10.9 %copy-start.38 = (s32[64,256]{1,0:T(8,128)S(1)}, s32[64,256]{1,0:T(8,128)}, u32[]{:S(2)}) copy-start(s32[64,256]{1,0:T(8,128)} %param.34) | copy-start | bytes 196612
  246.1 8.7 %collective-permute-start.8 = (f32[32,64,1]{1,0,2:T(8,128)S(1)}, f32[32,64,1]{1,0,2:T(8,128)S(1)}, u32[]{:S(2)}, u32[]{:S(2)}) collective-permute-start(f32[32,64,1]{1,0,2:T(8,128)S(1)} %copy.106), channel_id=1, source_target_pairs={{8,0},{16,8},{24,16},{32,24},{40,32},{48,40},{56,48},{64,56},{72,6... | collective-permute-start | bytes 24584 | tf_op jit(solution)/shard_map/ppermute | solution.py:81
  247.4 7.0 %collective-permute-start.9 = (f32[32,64,1]{1,0,2:T(8,128)S(1)}, f32[32,64,1]{1,0,2:T(8,128)S(1)}, u32[]{:S(2)}, u32[]{:S(2)}) collective-permute-start(f32[32,64,1]{1,0,2:T(8,128)S(1)} %copy.108), channel_id=1, source_target_pairs={{0,8},{8,16},{16,24},{24,32},{32,40},{40,48},{48,56},{56,64},{64,7... | collective-permute-start | bytes 24584 | tf_op jit(solution)/shard_map/ppermute | solution.py:78
  256.3 7.5 %copy-start.6 = (f32[70,64,3]{2,1,0:T(8,128)S(1)}, f32[70,64,3]{2,1,0:T(8,128)}, u32[]{:S(2)}) copy-start(f32[70,64,3]{2,1,0:T(8,128)} %copy.79) | copy-start | bytes 161284
  256.3 7.5 %copy-start.20 = (f32[70,3,262]{2,1,0:T(4,128)S(1)}, f32[70,3,262]{2,1,0:T(4,128)}, u32[]{:S(2)}) copy-start(f32[70,3,262]{2,1,0:T(4,128)} %copy-done.19) | copy-start | bytes 660244
  256.3 7.6 %copy-start.22 = (f32[64,256]{1,0:T(8,128)S(1)}, f32[64,256]{1,0:T(8,128)}, u32[]{:S(2)}) copy-start(f32[64,256]{1,0:T(8,128)} %get-tuple-element.109) | copy-start | bytes 196612
  256.3 7.6 %copy-start.24 = (f32[64,256]{1,0:T(8,128)S(1)}, f32[64,256]{1,0:T(8,128)}, u32[]{:S(2)}) copy-start(f32[64,256]{1,0:T(8,128)} %param.29) | copy-start | bytes 196612
  256.3 7.6 %copy-start.26 = (f32[64,256]{1,0:T(8,128)S(1)}, f32[64,256]{1,0:T(8,128)}, u32[]{:S(2)}) copy-start(f32[64,256]{1,0:T(8,128)} %param.30) | copy-start | bytes 196612
  257.9 7.1 %collective-permute-start.10 = (f32[32,1,258]{2,1,0:T(1,128)S(1)}, f32[32,1,258]{2,1,0:T(1,128)S(1)}, u32[]{:S(2)}, u32[]{:S(2)}) collective-permute-start(f32[32,1,258]{2,1,0:T(1,128)S(1)} %get-tuple-element.120), channel_id=1, source_target_pairs={{1,0},{2,1},{3,2},{4,3},{5,4},{6,5},{7,6},{9,8},{10,9},{11,10},{12... | collective-permute-start | bytes 99080 | tf_op jit(solution)/shard_map/ppermute | solution.py:81
  259.2 6.3 %collective-permute-start.11 = (f32[32,1,258]{2,1,0:T(1,128)S(1)}, f32[32,1,258]{2,1,0:T(1,128)S(1)}, u32[]{:S(2)}, u32[]{:S(2)}) collective-permute-start(f32[32,1,258]{2,1,0:T(1,128)S(1)} %get-tuple-element.121), channel_id=1, source_target_pairs={{0,1},{1,2},{2,3},{3,4},{4,5},{5,6},{6,7},{8,9},{9,10},{10,11},{11... | collective-permute-start | bytes 99080 | tf_op jit(solution)/shard_map/ppermute | solution.py:78
  (25 other events, 36.2 us)

commit v2 on v1

v2 whole, which is shorter than its diff:
```python
import functools
import math

import jax
import jax.numpy as jnp
import numpy as np
from jax import lax
from jax.experimental import pallas as pl
from jax.experimental.pallas import tpu as pltpu
from jax.sharding import PartitionSpec as P

DEG = 8
OV = 2
STRIDE = 9
LANES = 128
SUB = 8


cheb_theta = 1.0
cheb_delta = 0.95


def horner_coefficients():
    t8 = np.array([1.0, -32.0, 160.0, -256.0, 128.0])
    u_scale = 1.0 / cheb_delta**2
    at_one = sum(c * u_scale**k for k, c in enumerate(t8))
    g = -np.array([c * u_scale**k for k, c in enumerate(t8)]) / at_one
    g[0] += 1.0
    q = np.zeros(4)
    total = 0.0
    for k in range(4):
        total += g[k]
        q[k] = total
    return q


Q_COEF = horner_coefficients()


def sub_ids():
    return lax.broadcasted_iota(jnp.int32, (SUB, LANES), 0)


def lane_ids():
    return lax.broadcasted_iota(jnp.int32, (SUB, LANES), 1)


def row_ids_of(j):
    return lax.broadcasted_iota(jnp.int32, (SUB, LANES), 0) * STRIDE + j


def east_of(x):
    return pltpu.roll(x, LANES - 1, 1)


def west_of(x):
    return pltpu.roll(x, 1, 1)


def south_list(xs):
    return xs[1:] + [pltpu.roll(xs[0], SUB - 1, 0)]


def north_list(xs):
    return [pltpu.roll(xs[-1], 1, 0)] + xs[:-1]


def off_diagonal(xs, east, south):
    from_north = north_list([s * x for s, x in zip(south, xs)])
    from_south = [s * x for s, x in zip(south, south_list(xs))]
    out = []
    for j, x in enumerate(xs):
        out.append((west_of(east[j] * x) + east[j] * east_of(x)) + (from_north[j] + from_south[j]))
    return out


GROUPS = 9
PLANES = 6
MIB = 1024 * 1024
START, STORAGE, LEAKAGE, EAST, SOUTH, WEIGHT = range(PLANES)


def tile_of(k):
    return slice(k * LANES, (k + 1) * LANES)


def rows_of(g):
    return slice(g * SUB, (g + 1) * SUB)


def rows(j):
    return pl.ds(j, SUB, stride=STRIDE)


def rolled(x, amount):
    return pltpu.roll(x, lax.rem(amount + 4 * LANES, LANES), 1)


def half_turn(x):
    return pltpu.roll(x, SUB // 2, 0)


def whole(shape):
    return pl.BlockSpec(shape, lambda i: (0,) * len(shape))


def pack_kernel(flags, prev, source, start, storage, leakage, east, south, weight, coef, to_left, to_right, to_up, to_down):
    step0 = pl.program_id(0)
    steps = prev.shape[0]
    total = steps * pl.num_programs(0)
    lanes, sub = lane_ids(), sub_ids()

    def sides(array, slot, get):
        here = (lanes >= slot) & (lanes < slot + 3)
        for g in range(SUB):
            to_left[array, rows_of(g), :] = jnp.where(here, rolled(get(g, 0), slot), to_left[array, rows_of(g), :])
            to_right[array, rows_of(g), :] = jnp.where(here, rolled(get(g, 1), slot + 3), to_right[array, rows_of(g), :])

    def slabs(slab, get_even, get_odd):
        for k in range(2):
            to_up[slab, :, tile_of(k)] = jnp.where(sub < 4, get_even(0, k), half_turn(get_odd(0, k)))
            to_down[slab, :, tile_of(k)] = jnp.where(sub < 4, half_turn(get_odd(SUB - 1, k)), get_even(SUB - 1, k))

    @pl.when(step0 == 0)
    def _():
        for array in range(3):
            to_left[array] = jnp.zeros_like(to_left[array])
            to_right[array] = jnp.zeros_like(to_right[array])
        for p, ref in enumerate((start, storage, leakage, east, south, weight)):
            for g in range(SUB):
                for k in range(2):
                    value = ref[rows_of(g), tile_of(k)].astype(jnp.float32)
                    if p == EAST and k == 1:
                        value = jnp.where((lanes == LANES - 1) & (flags[1] == 0), 0.0, value)
                    if p == SOUTH and g == SUB - 1:
                        value = jnp.where((sub == SUB - 1) & (flags[3] == 0), 0.0, value)
                    coef[p, rows_of(g), tile_of(k)] = value
        plane = lambda p: lambda g, k: coef[p, rows_of(g), tile_of(k)]
        for p in range(PLANES):
            sides(2, 4 * p, plane(p))
        for q in range(PLANES // 2):
            slabs(total + q, plane(2 * q), plane(2 * q + 1))

    def pair(q, _):
        for array, ref in ((0, prev), (1, source)):
            plane = lambda i: lambda g, k: ref[i, rows_of(g), tile_of(k)]
            for o in range(2):
                sides(array, 4 * (step0 * steps + 2 * q + o), plane(2 * q + o))
            slabs(array * (total // 2) + step0 * (steps // 2) + q, plane(2 * q), plane(2 * q + 1))
        return 0

    lax.fori_loop(0, steps // 2, pair, 0)


def pack(flags, prev, source, planes):
    steps, nr, nc = prev.shape
    block = 8
    big = pl.BlockSpec((block, nr, nc), lambda i: (i, 0, 0))
    shapes = [(PLANES, nr, nc), (3, nr, LANES), (3, nr, LANES), (steps + PLANES // 2, SUB, nc), (steps + PLANES // 2, SUB, nc)]
    return pl.pallas_call(
        pack_kernel,
        grid=(steps // block,),
        in_specs=[pl.BlockSpec(memory_space=pltpu.SMEM), big, big] + [whole((nr, nc))] * PLANES,
        out_specs=[whole(s) for s in shapes],
        out_shape=[jax.ShapeDtypeStruct(s, jnp.float32) for s in shapes],
        compiler_params=pltpu.CompilerParams(vmem_limit_bytes=16 * MIB),
        name="pack",
    )(flags, prev, source, *planes)


def windows_of(left, right, halo_left, halo_right, lanes):
    return (
        jnp.where(lanes < LANES - 3, left, halo_left),
        jnp.where(lanes < LANES // 2, right, left),
        jnp.where(lanes < 3, halo_right, right),
    )


def halo_rows(below, above, odd, sub):
    if odd:
        return half_turn(jnp.where(sub < 4, above, below))
    return jnp.where(sub < 4, below, above)


def sweep_kernel(prev, source, coefs, xL, xR, cA, cB, yA, yB, out, rims, yU, yD, tiles, ctiles, halo, coef, carry):
    step0 = pl.program_id(0)
    steps = prev.shape[0]
    total = steps * pl.num_programs(0)
    lanes, sub = lane_ids(), sub_ids()

    def window_set(j, left, right, array, slot):
        return windows_of(
            left, right, rolled(halo[0, array, rows(j), :], LANES - 3 - slot), rolled(halo[1, array, rows(j), :], -slot), lanes
        )

    breaks = (LANES - 4, LANES // 2 - 1, 2)
    outer = (LANES - 3, -1, 2)

    @pl.when(step0 == 0)
    def _():
        for array in range(3):
            for side, ref in ((0, xL), (1, xR)):
                for g in range(SUB):
                    halo[side, array, rows_of(g), :] = ref[array, rows_of(g), :]
                halo[side, array, rows_of(SUB), :] = jnp.where(sub < 4, cB[side, array], cA[side, array])
        for p in range(5):
            slab = total + p // 2
            for k in range(2):
                for g in range(SUB):
                    ctiles[p, k, rows_of(g), :] = coefs[p, rows_of(g), tile_of(k)]
                ctiles[p, k, rows_of(SUB), :] = halo_rows(yB[slab, :, tile_of(k)], yA[slab, :, tile_of(k)], p % 2, sub)
        planes = [
            [window_set(j, ctiles[p, 0, rows(j), :], ctiles[p, 1, rows(j), :], 2, 4 * p) for j in range(STRIDE)]
            for p in range(5)
        ]
        for w in range(3):
            start, storage, leakage, east, south = [[planes[p][j][w] for j in range(STRIDE)] for p in range(5)]
            east = [jnp.where(lanes == breaks[w], 0.0, e) for e in east]
            north = north_list(south)
            diag, scale = [], []
            for j in range(STRIDE):
                d = storage[j] + leakage[j] + east[j] + west_of(east[j]) + south[j] + north[j]
                row = row_ids_of(j)
                inner = ((row < 66) | (row > 69)) & (lanes != outer[w]) & (d > 0.0)
                diag.append(d)
                scale.append(jnp.where(inner, 1.0 / jnp.sqrt(jnp.where(inner, d, 1.0)), 0.0))
            scale_south = south_list(scale)
            for j in range(STRIDE):
                carry[w, j] = start[j]
                coef[0, w, j] = east[j] * scale[j] * east_of(scale[j])
                coef[1, w, j] = south[j] * scale[j] * scale_south[j]
                coef[2, w, j] = storage[j]
                coef[3, w, j] = diag[j]
                coef[4, w, j] = east[j]
                coef[5, w, j] = south[j]
                coef[6, w, j] = scale[j]
                coef[7, w, j] = scale[j] * np.float32(Q_COEF[3])
        for side in range(2):
            rims[side] = jnp.zeros_like(rims[side])

    def step(i, t, odd):
        for array, ref in ((0, prev), (1, source)):
            slab = array * (total // 2) + t // 2
            for k in range(2):
                for g in range(SUB):
                    tiles[odd, array, k, rows_of(g), :] = ref[i, rows_of(g), tile_of(k)]
                tiles[odd, array, k, rows_of(SUB), :] = halo_rows(yB[slab, :, tile_of(k)], yA[slab, :, tile_of(k)], odd, sub)
        x0s, srcs = [
            [window_set(j, tiles[odd, a, 0, rows(j), :], tiles[odd, a, 1, rows(j), :], a, 4 * t) for j in range(STRIDE)]
            for a in range(2)
        ]
        result = []
        for w in range(3):
            x0 = [x0s[j][w] for j in range(STRIDE)]
            full = off_diagonal(x0, [coef[4, w, j] for j in range(STRIDE)], [coef[5, w, j] for j in range(STRIDE)])
            z = [
                coef[6, w, j] * ((srcs[j][w] + coef[2, w, j] * carry[w, j]) + (full[j] - coef[3, w, j] * x0[j]))
                for j in range(STRIDE)
            ]
            east = [coef[0, w, j] for j in range(STRIDE)]
            south = [coef[1, w, j] for j in range(STRIDE)]
            base = [a + b for a, b in zip(z, off_diagonal(z, east, south))]
            y = base
            for k in (2, 1, 0):
                y = off_diagonal(off_diagonal(y, east, south), east, south)
                ratio = np.float32(Q_COEF[k] / Q_COEF[3])
                y = [a + ratio * b for a, b in zip(y, base)]
            result.append([x0[j] + coef[7, w, j] * y[j] for j in range(STRIDE)])
        slot = 4 * t
        here = (lanes >= slot) & (lanes < slot + 3)
        for j in range(STRIDE):
            a, b, c = result[0][j], result[1][j], result[2][j]
            left = jnp.where(lanes < 96, a, b)
            right = jnp.where(lanes < 32, b, c)
            out[i, 0, rows(j), :] = left
            out[i, 1, rows(j), :] = right
            fresh = windows_of(left, right, a, c, lanes)
            for w in range(3):
                carry[w, j] = fresh[w]
            rims[0, rows(j), :] = jnp.where(here, rolled(a, slot + 2), rims[0, rows(j), :])
            rims[1, rows(j), :] = jnp.where(here, rolled(c, slot + 1), rims[1, rows(j), :])

    def pair(q, _):
        for odd in range(2):
            step(2 * q + odd, step0 * steps + 2 * q + odd, odd)
        kept = (sub < 2) | (sub > 5)
        slab = step0 * (steps // 2) + q
        for k in range(2):
            down, up = [], []
            for odd in range(2):
                first, last, beyond = [out[2 * q + odd, k, rows_of(g), :] for g in (0, SUB - 1, SUB)]
                down.append(jnp.where(sub < 4, beyond, last))
                up.append(jnp.where(sub < 4, first, beyond))
            yD[slab, :, tile_of(k)] = jnp.where(kept, down[0], half_turn(down[1]))
            yU[slab, :, tile_of(k)] = jnp.where(kept, up[0], half_turn(up[1]))
        return 0

    lax.fori_loop(0, steps // 2, pair, 0)

    @pl.when(step0 == pl.num_programs(0) - 1)
    def _():
        for side in range(2):
            first, last, beyond = [rims[side, rows_of(g), :] for g in (0, SUB - 1, SUB)]
            yD[total // 2, :, tile_of(side)] = jnp.where(sub < 4, beyond, last)
            yU[total // 2, :, tile_of(side)] = jnp.where(sub < 4, first, beyond)


def sweep(prev, source, coefs, xL, xR, cA, cB, yA, yB):
    steps, nr, nc = prev.shape
    block = 4
    big = pl.BlockSpec((block, nr, nc), lambda i: (i, 0, 0))
    ext = GROUPS * SUB
    consts = (coefs, xL, xR, cA, cB, yA, yB)
    rest = [(2, ext, LANES), (steps // 2 + 1, SUB, nc), (steps // 2 + 1, SUB, nc)]
    return pl.pallas_call(
        sweep_kernel,
        grid=(steps // block,),
        in_specs=[big, big] + [whole(a.shape) for a in consts],
        out_specs=[pl.BlockSpec((block, 2, ext, LANES), lambda i: (i, 0, 0, 0))] + [whole(s) for s in rest],
        out_shape=[jax.ShapeDtypeStruct(s, jnp.float32) for s in [(steps, 2, ext, LANES)] + rest],
        scratch_shapes=[
            pltpu.VMEM((2, 2, 2, ext, LANES), jnp.float32),
            pltpu.VMEM((5, 2, ext, LANES), jnp.float32),
            pltpu.VMEM((2, 3, ext, LANES), jnp.float32),
            pltpu.VMEM((8, 3, STRIDE, SUB, LANES), jnp.float32),
            pltpu.VMEM((3, STRIDE, SUB, LANES), jnp.float32),
        ],
        compiler_params=pltpu.CompilerParams(vmem_limit_bytes=16 * MIB),
        name="sweep",
    )(prev, source, *consts)


def split3(x):
    hi = x.astype(jnp.bfloat16)
    left = x - hi.astype(jnp.float32)
    mid = left.astype(jnp.bfloat16)
    low = (left - mid.astype(jnp.float32)).astype(jnp.bfloat16)
    return hi, mid, low


def settle_kernel(
    flags, local, source, coefs, xL, xR, yA, yB, rims, rL, rR, kA, kB, sA, sB, ids, settled, coarse, pack, ring, edge, before, resid
):
    step0 = pl.program_id(0)
    steps = local.shape[0]
    total = steps * pl.num_programs(0)
    lanes, sub = lane_ids(), sub_ids()
    has_left, has_right, has_up, has_down = [(flags[k] != 0) for k in range(4)]
    as_one = lambda mask: jnp.where(mask, 1.0, 0.0)
    only = lambda mask, x: jnp.where(mask, x, 0.0)

    def column(ref, g, lane):
        return jnp.broadcast_to(ref[2, rows_of(g), lane : lane + 1], (SUB, LANES))

    def halo_plane(p, k):
        slab = total + p // 2
        return halo_rows(yB[slab, :, tile_of(k)], yA[slab, :, tile_of(k)], p % 2, sub)

    @pl.when(step0 == 0)
    def _():
        across = lambda k: as_one((lanes < 2) & has_left) if k == 0 else as_one((lanes > LANES - 3) & has_right)
        for g in range(GROUPS):
            if g < SUB:
                down = only(sub < 2, as_one(has_up)) if g == 0 else only(sub > 5, as_one(has_down)) if g == SUB - 1 else 0.0 * as_one(sub < 0)
            else:
                down = as_one(sub >= 0)
            for k in range(2):
                copies = (1.0 + across(k)) * (1.0 + down) - 1.0
                weight = coefs[WEIGHT, rows_of(g), tile_of(k)] if g < SUB else halo_plane(WEIGHT, k)
                ring[0, k, g] = weight / (weight + copies)
                ring[1, k, g] = 1.0 / (weight + copies)
            for side, got, xref, lane, keep, back in ((0, rL, xL, 4 * WEIGHT + 2, 0, LANES - 1), (1, rR, xR, 4 * WEIGHT, 2, 1)):
                arrived = got[rows_of(g), :]
                fwd_above, fwd_below = sA[:, tile_of(side)], sB[:, tile_of(side)]
                if g == 0:
                    extra = only(sub < 2, fwd_above)
                elif g == SUB - 1:
                    extra = only(sub > 5, fwd_below)
                elif g == SUB:
                    extra = only(sub == SUB - 1, fwd_above) + only(sub == 0, fwd_below)
                else:
                    extra = jnp.zeros((SUB, LANES), jnp.float32)
                value = arrived + extra
                if g < SUB:
                    mine = rims[side, rows_of(g), :]
                    if g == 0:
                        mine = mine + only(sub < 2, kA[total // 2, :, tile_of(side)])
                    if g == SUB - 1:
                        mine = mine + only(sub > 5, kB[total // 2, :, tile_of(side)])
                    weight = column(xref, g, lane)
                    copies = 2.0 * (1.0 + down) - 1.0
                    outer = (weight * arrived + (pltpu.roll(mine, back, 1) + extra)) / (weight + copies)
                    value = jnp.where(lax.rem(lanes, 4) == keep, outer, value)
                edge[side, g] = value
        for k in range(2):
            for g in range(SUB):
                own = lambda p: coefs[p, rows_of(g), tile_of(k)]
                neighbour = column(xL, g, 4 * EAST + 2) if k == 0 else coefs[EAST, rows_of(g), tile_of(0)]
                west = west_of(jnp.where(lanes == LANES - 1, neighbour, own(EAST)))
                above = halo_plane(SOUTH, k) if g == 0 else coefs[SOUTH, rows_of(g - 1), tile_of(k)]
                north = pltpu.roll(jnp.where(sub == SUB - 1, above, own(SOUTH)), 1, 0)
                pack[0, k, g] = west
                pack[1, k, g] = north
                pack[2, k, g] = own(STORAGE) + own(LEAKAGE) + own(EAST) + west + own(SOUTH) + north
                before[k, g] = own(START)

    def step(i, t, odd):
        slab = t // 2
        mid = []
        for k in range(2):
            from_above, from_below = kA[slab, :, tile_of(k)], kB[slab, :, tile_of(k)]
            if odd:
                from_above, from_below = half_turn(from_above), half_turn(from_below)
            values = []
            for g in range(GROUPS):
                side = rolled(edge[k, g], -4 * t - 1 if k == 0 else LANES - 2 - 4 * t)
                extra = only(lanes < 2 if k == 0 else lanes > LANES - 3, side)
                here = local[i, k, rows_of(g), :]
                if g == 0:
                    extra = extra + only(sub < 2, from_above)
                elif g == SUB - 1:
                    extra = extra + only(sub > 5, from_below)
                elif g == SUB:
                    extra = extra + here
                    here = jnp.where(sub < 4, from_below, from_above)
                values.append((ring[0, k, g] * here + ring[1, k, g] * extra, side))
            mid.append(values)
        for k in range(2):
            for g in range(SUB):
                x = mid[k][g][0]
                if k == 0:
                    west = jnp.where(lanes == LANES - 1, mid[0][g][1], x)
                    east = jnp.where(lanes == 0, mid[1][g][0], x)
                else:
                    west = jnp.where(lanes == LANES - 1, mid[0][g][0], x)
                    east = jnp.where(lanes == 0, mid[1][g][1], x)
                north = jnp.where(sub == SUB - 1, mid[k][(g + GROUPS - 1) % GROUPS][0], x)
                south = jnp.where(sub == 0, mid[k][g + 1][0], x)
                around = (coefs[EAST, rows_of(g), tile_of(k)] * east_of(east) + pack[0, k, g] * west_of(west)) + (
                    coefs[SOUTH, rows_of(g), tile_of(k)] * pltpu.roll(south, SUB - 1, 0) + pack[1, k, g] * pltpu.roll(north, 1, 0)
                )
                value = (source[i, rows_of(g), tile_of(k)] + coefs[STORAGE, rows_of(g), tile_of(k)] * before[k, g]) - (
                    pack[2, k, g] * x - around
                )
                resid[k, pl.ds(t * 64 + g * SUB, SUB), :] = value
                before[k, g] = x
                settled[i, rows_of(g), tile_of(k)] = x

    def pair(q, _):
        for odd in range(2):
            step(2 * q + odd, step0 * steps + 2 * q + odd, odd)
        return 0

    lax.fori_loop(0, steps // 2, pair, 0)

    @pl.when(step0 == pl.num_programs(0) - 1)
    def _():
        aggs = lax.broadcasted_iota(jnp.int32, (64, 2 * LANES), 0)

        def one_row(r, acc):
            picked = jnp.broadcast_to(ids[pl.ds(r, 1), :] - flags[4], (64, 2 * LANES))
            hot = jnp.where(picked == aggs, 1.0, 0.0).astype(jnp.bfloat16)
            values = jnp.concatenate([resid[k, pl.ds(r, total, stride=64), :] for k in range(2)], axis=1)
            parts = jnp.concatenate(split3(values), axis=0)
            return acc + lax.dot_general(parts, hot, (((1,), (1,)), ((), ())), preferred_element_type=jnp.float32)

        def rows4(r, acc):
            for o in range(4):
                acc = one_row(4 * r + o, acc)
            return acc

        acc = lax.fori_loop(0, 16, rows4, jnp.zeros((3 * total, 64), jnp.float32))
        sums = acc[:total] + acc[total : 2 * total] + acc[2 * total :]
        block = jnp.concatenate([sums[: total // 2], sums[total // 2 :]], axis=1)
        coarse[...] = jnp.broadcast_to(block[None], coarse.shape)


def settle(flags, local, source, coefs, xL, xR, yA, yB, rims, rL, rR, kA, kB, sA, sB, ids, count):
    steps, nr, nc = source.shape
    block = 4
    ext = GROUPS * SUB
    big = pl.BlockSpec((block, nr, nc), lambda i: (i, 0, 0))
    consts = (coefs, xL, xR, yA, yB, rims, rL, rR, kA, kB, sA, sB, ids)
    shapes = [(steps, nr, nc), (count, steps // 2, LANES)]
    return pl.pallas_call(
        settle_kernel,
        grid=(steps // block,),
        in_specs=[
            pl.BlockSpec(memory_space=pltpu.SMEM),
            pl.BlockSpec((block, 2, ext, LANES), lambda i: (i, 0, 0, 0)),
            big,
        ]
        + [whole(a.shape) for a in consts],
        out_specs=[big, whole(shapes[1])],
        out_shape=[jax.ShapeDtypeStruct(s, jnp.float32) for s in shapes],
        scratch_shapes=[
            pltpu.VMEM((3, 2, SUB, SUB, LANES), jnp.float32),
            pltpu.VMEM((2, 2, GROUPS, SUB, LANES), jnp.float32),
            pltpu.VMEM((2, GROUPS, SUB, LANES), jnp.float32),
            pltpu.VMEM((2, SUB, SUB, LANES), jnp.float32),
            pltpu.VMEM((2, steps * nr, LANES), jnp.float32),
        ],
        compiler_params=pltpu.CompilerParams(vmem_limit_bytes=20 * MIB),
        name="settle",
    )(flags, local, source, *consts)


def finish_kernel(flags, every, inverse, settled, ids, out, table, stacked):
    step0 = pl.program_id(0)
    steps = settled.shape[0]
    half = every.shape[1]
    lanes = lane_ids()

    @pl.when(step0 == 0)
    def _():
        for d in range(every.shape[0] // 2):
            for g in range(half // SUB):
                a, b = every[2 * d, rows_of(g), :], every[2 * d + 1, rows_of(g), :]
                stacked[rows_of(g), tile_of(d)] = jnp.where(lanes < LANES // 2, a, pltpu.roll(b, LANES // 2, 1))
                stacked[half + g * SUB : half + (g + 1) * SUB, tile_of(d)] = jnp.where(
                    lanes < LANES // 2, pltpu.roll(a, LANES // 2, 1), b
                )
        product = lax.dot_general(
            stacked[...],
            inverse[...],
            (((1,), (1,)), ((), ())),
            precision=lax.Precision.HIGHEST,
            preferred_element_type=jnp.float32,
        )
        table[...] = jnp.concatenate([product, product], axis=1)

    def step(i, _):
        t = step0 * steps + i
        row = jnp.broadcast_to(table[pl.ds(t, 1), :], (SUB, LANES))
        for g in range(SUB):
            for k in range(2):
                picked = ids[rows_of(g), tile_of(k)] - flags[4]
                out[i, rows_of(g), tile_of(k)] = settled[i, rows_of(g), tile_of(k)] + jnp.take_along_axis(row, picked, axis=1)
        return 0

    lax.fori_loop(0, steps, step, 0)


def finish(flags, every, inverse, settled, ids):
    steps, nr, nc = settled.shape
    block = 8
    big = pl.BlockSpec((block, nr, nc), lambda i: (i, 0, 0))
    return pl.pallas_call(
        finish_kernel,
        grid=(steps // block,),
        in_specs=[pl.BlockSpec(memory_space=pltpu.SMEM), whole(every.shape), whole(inverse.shape), big, whole(ids.shape)],
        out_specs=big,
        out_shape=jax.ShapeDtypeStruct(settled.shape, jnp.float32),
        scratch_shapes=[pltpu.VMEM((steps, LANES), jnp.float32), pltpu.VMEM((steps, inverse.shape[1]), jnp.float32)],
        compiler_params=pltpu.CompilerParams(vmem_limit_bytes=20 * MIB),
        name="finish",
    )(flags, every, inverse, settled, ids)


def neighbours(low, high, axis):
    count = lax.axis_size(axis)
    forward = [(i, i + 1) for i in range(count - 1)]
    backward = [(target, source) for source, target in forward]
    return lax.ppermute(high, axis, forward), lax.ppermute(low, axis, backward)


def gather_all(block, axes):
    count = block.shape[0]
    every = lax.all_to_all(block.reshape(count, 1, -1), axes, 0, 0)
    return every.reshape(block.shape)


def shards(
    prev_wave,
    source,
    start_state,
    storage,
    leakage,
    cond_east,
    cond_south,
    owner_weight,
    aggregate,
    coarse_inverse,
):
    gx, gy = lax.axis_index("gx"), lax.axis_index("gy")
    nx, ny = lax.axis_size("gx"), lax.axis_size("gy")
    flags = jnp.stack([gx, nx - 1 - gx, gy, ny - 1 - gy, (gx * ny + gy) * coarse_inverse.shape[0]]).astype(jnp.int32)
    planes = (start_state, storage, leakage, cond_east, cond_south, owner_weight)
    coefs, to_left, to_right, to_up, to_down = pack(flags, prev_wave, source, planes)
    xL, xR = neighbours(to_left, to_right, "gx")
    yA, yB = neighbours(to_up, to_down, "gy")
    both = jnp.stack([xL, xR])
    cA, cB = neighbours(both[:, :, :SUB], both[:, :, -SUB:], "gy")
    local, rims, yU, yD = sweep(prev_wave, source, coefs, xL, xR, cA, cB, yA, yB)
    rL, rR = neighbours(rims[0], rims[1], "gx")
    kA, kB = neighbours(yU, yD, "gy")
    up = jnp.concatenate([jnp.concatenate([r[0:4], r[68:72]], 0) for r in (rL, rR)], 1)
    down = jnp.concatenate([jnp.concatenate([r[64:68], r[60:64]], 0) for r in (rL, rR)], 1)
    sA, sB = neighbours(up, down, "gy")
    settled, coarse = settle(
        flags, local, source, coefs, xL, xR, yA, yB, rims, rL, rR, kA, kB, sA, sB, aggregate, nx * ny
    )
    every = gather_all(coarse, ("gx", "gy"))
    return finish(flags, every, coarse_inverse, settled, aggregate)


def solution(mesh):
    return jax.shard_map(
        shards,
        mesh=mesh,
        in_specs=(
            P(None, "gy", "gx"),
            P(None, "gy", "gx"),
            P("gy", "gx"),
            P("gy", "gx"),
            P("gy", "gx"),
            P("gy", "gx"),
            P("gy", "gx"),
            P("gy", "gx"),
            P("gy", "gx"),
            P(("gx", "gy"), None),
        ),
        out_specs=P(None, "gy", "gx"),
        check_vma=False,
    )
```

time: 344 us -> 137 us (0.40)
  local copies, waits for them, and re-layouts: 144 us -> 8.33 us
  other arithmetic: 42.1 us -> 0.02 us
  matrix products: 14.9 us -> 0 us
  starting transfers between devices: 46.1 us -> 31.3 us
  Pallas kernels: 35.8 us -> 44.2 us
  blocking collectives: 45.4 us -> 41.6 us
    scatter-add x8 -> x0, local copies, waits for them, and re-layouts: 46.3 us -> none  [the longest x1 12 us: collect_rims(): incoming.at[:, :OV, cols_dev - OV:].add(returned[:, :OV, rightmost:])]
    slice x22 -> x2, local copies, waits for them, and re-layouts: 28.8 us -> 0.01 us  [shards(): r[0:4]]
    transpose x9 -> x0, local copies, waits for them, and re-layouts: 19.8 us -> none  [tiles_and_sides(): sides.append(jnp.transpose(s, (1, 0, 2)).reshape(72, LANES))]
    another operation x12 -> x1, local copies, waits for them, and re-layouts: 15.4 us -> 0.08 us  [shards(): jnp.stack([gx, nx - 1 - gx, gy, ny - 1 - gy, (gx * ny + gy) * coarse_inve...]
    dot_general x3 -> x0, matrix products: 14.9 us -> none  [the longest x1 8.8 us: shards(): jnp.dot(coarse_inverse, gather_all(own_coarse), precision=lax.Precision.H...]
    ppermute x12, starting transfers between devices: 46.1 us -> 31.3 us  [the longest x6 23.5 us: neighbours(): lax.ppermute(high, axis, forward)]
    ppermute x6 -> x0, local copies, waits for them, and re-layouts: 11.9 us -> none  [the longest x3 6.07 us: padded_2(): lax.ppermute(lax.slice_in_dim(block, 0, width, axis=dim), axis, backward)]
    add x8 -> x0, other arithmetic: 10.6 us -> none  [the longest x1 2.89 us: collect_rims(): incoming.at[:, :, cols_dev - OV:]]
  transfers between devices with their start and end apart: 12 -> 12, of which waited for: 5 -> 3; matrix products, arithmetic and copies ran while one was open for 5% -> 0% of each run, Pallas kernels for 0% -> 0%
where the time goes in v2:
time: 137 us; the launch traced here: 136 us
  Pallas kernels  44.2 us (32%)
  blocking collectives  41.6 us (30%)
  starting transfers between devices  31.3 us (23%)
  waiting for transfers between devices  10.2 us (7%)
  local copies, waits for them, and re-layouts  8.33 us (6%)
    all_to_all x1, blocking collectives, gather_all(): every = lax.all_to_all(block.reshape(count, 1, -1), axes, 0, 0)  41.6 us
    pallas_call x1, Pallas kernels, sweep(): pl.pallas_call(sweep_kernel, grid=(steps // block,), in_specs=[big, big]...  25.6 us
    ppermute x6, starting transfers between devices, neighbours(): lax.ppermute(high, axis, forward)  23.5 us
    ppermute x6, waiting for transfers between devices, neighbours(): lax.ppermute(low, axis, backward)  8.64 us
    pallas_call x1, Pallas kernels, settle(): pl.pallas_call(settle_kernel, grid=(steps // block,), in_specs=[pl.BlockS...  8.64 us
    unnamed x22, local copies, waits for them, and re-layouts  8.23 us
    ppermute x6, starting transfers between devices, neighbours(): lax.ppermute(low, axis, backward)  7.74 us
    pallas_call x1, Pallas kernels, finish(): pl.pallas_call(finish_kernel, grid=(steps // block,), in_specs=[pl.BlockS...  7.01 us
  transfers between devices with their start and end apart: 12, of which 3 were waited for; matrix products, arithmetic and copies ran while one was open for 0% of the time, Pallas kernels for 0%

profile of v2, /device:TPU:0, one launch (start us, length us, event | category | flops | bytes accessed | tf_op | source)
XLA Modules:
  0.0 135.8 jit_solution(16273356784258886455)
XLA Ops:
  0.0 0.1 stack.32.flags
  0.1 1.6 %copy-done = f32[32,64,256]{2,1,0:T(8,128)S(1)} copy-done((f32[32,64,256]{2,1,0:T(8,128)S(1)}, f32[32,64,256]{2,1,0:T(8,128)}, u32[]{:S(2)}) %copy-start) | copy-done | bytes 2097176
  1.7 1.6 %copy-done.2 = f32[32,64,256]{2,1,0:T(8,128)S(1)} copy-done((f32[32,64,256]{2,1,0:T(8,128)S(1)}, f32[32,64,256]{2,1,0:T(8,128)}, u32[]{:S(2)}) %copy-start.2) | copy-done | bytes 2097176
  3.3 0.8 copy-done.5
  4.1 0.8 copy-done.6
  5.0 0.8 copy-done.7
  5.8 0.8 copy-done.8
  6.6 0.8 copy-done.9
  7.5 0.8 copy-done.10
  8.3 3.0 %pack.1 = (f32[6,64,256]{2,1,0:T(8,128)S(1)}, f32[3,64,128]{2,1,0:T(8,128)S(1)}, f32[3,64,128]{2,1,0:T(8,128)S(1)}, f32[35,8,256]{2,1,0:T(8,128)S(1)}, f32[35,8,256]{2,1,0:T(8,128)S(1)}) custom-call(s32[5]{0:T(128)S(1)} %stack.32.flags, f32[32,64,256]{2,1,0:T(8,128)S(1)} %copy-done.2, f32[32,64,256]{2,1,0:T(8,128)S(1)} %copy-done, f32[64,256]{1,0:T(8,128)S(1)} %copy-done.5, ...), custom_call_target="tpu_custom_call" | custom-call | tf_op jit(solution)/shard_map/pack/pallas_call | solution.py:160
  11.3 3.5 %collective-permute-start.4 = (f32[35,8,256]{2,1,0:T(8,128)S(1)}, f32[35,8,256]{2,1,0:T(8,128)S(1)}, u32[]{:S(2)}, u32[]{:S(2)}) collective-permute-start(f32[35,8,256]{2,1,0:T(8,128)S(1)} %get-tuple-element.19), channel_id=1, source_target_pairs={{0,1},{1,2},{2,3},{3,4},{4,5},{5,6},{6,7},{8,9},{9,10},{10,11},{11... | collective-permute-start | bytes 860168 | tf_op jit(solution)/shard_map/ppermute | solution.py:564
  14.8 1.3 collective-permute-start.5
  16.1 1.5 %collective-permute-start = (f32[3,64,128]{2,1,0:T(8,128)S(1)}, f32[3,64,128]{2,1,0:T(8,128)S(1)}, u32[]{:S(2)}, u32[]{:S(2)}) collective-permute-start(f32[3,64,128]{2,1,0:T(8,128)S(1)} %get-tuple-element.17), channel_id=1, source_target_pairs={{0,8},{8,16},{16,24},{24,32},{32,40},{40,48},{48,56},{56,64},{64,7... | collective-permute-start | bytes 294920 | tf_op jit(solution)/shard_map/ppermute | solution.py:564
  17.6 1.3 collective-permute-start.1
  18.9 3.9 %collective-permute-done.1.xR = f32[3,64,128]{2,1,0:T(8,128)S(1)} collective-permute-done((f32[3,64,128]{2,1,0:T(8,128)S(1)}, f32[3,64,128]{2,1,0:T(8,128)S(1)}, u32[]{:S(2)}, u32[]{:S(2)}) %collective-permute-start.1) | collective-permute-done | bytes 98336 | tf_op jit(solution)/shard_map/ppermute | solution.py:564
  22.8 1.3 collective-permute-start.3
  24.1 5.2 %collective-permute-start.2 = (f32[2,3,8,128]{3,2,1,0:T(8,128)S(1)}, f32[2,3,8,128]{3,2,1,0:T(8,128)S(1)}, u32[]{:S(2)}, u32[]{:S(2)}) collective-permute-start(f32[2,3,8,128]{3,2,1,0:T(8,128)S(1)} %get-tuple-element.28), channel_id=1, source_target_pairs={{0,1},{1,2},{2,3},{3,4},{4,5},{5,6},{6,7},{8,9},{9,10},{10,11},{11... | collective-permute-start | bytes 73736 | tf_op jit(solution)/shard_map/ppermute | solution.py:564
  29.3 1.5 %collective-permute-done.2.cA = f32[2,3,8,128]{3,2,1,0:T(8,128)S(1)} collective-permute-done((f32[2,3,8,128]{3,2,1,0:T(8,128)S(1)}, f32[2,3,8,128]{3,2,1,0:T(8,128)S(1)}, u32[]{:S(2)}, u32[]{:S(2)}) %collective-permute-start.2) | collective-permute-done | bytes 24608 | tf_op jit(solution)/shard_map/ppermute | solution.py:564
  30.8 0.0 copy-start.4
  30.8 25.6 %sweep.1 = (f32[32,2,72,128]{3,2,1,0:T(8,128)S(1)}, f32[2,72,128]{2,1,0:T(8,128)S(1)}, f32[17,8,256]{2,1,0:T(8,128)S(1)}, f32[17,8,256]{2,1,0:T(8,128)S(1)}) custom-call(f32[32,64,256]{2,1,0:T(8,128)S(1)} %copy-done.2, f32[32,64,256]{2,1,0:T(8,128)S(1)} %copy-done.1, f32[6,64,256]{2,1,0:T(8,128)S(1)} %get-tuple-element.16.coefs, ...), custom_call_target="tpu_custom_call" | custom-call | tf_op jit(solution)/shard_map/sweep/pallas_call | solution.py:315
  56.4 1.3 collective-permute-start.7
  57.7 4.9 %collective-permute-start.6 = (f32[72,128]{1,0:T(8,128)S(1)}, f32[72,128]{1,0:T(8,128)S(1)}, u32[]{:S(2)}, u32[]{:S(2)}) collective-permute-start(f32[72,128]{1,0:T(8,128)S(1)} %get-tuple-element.30), channel_id=1, source_target_pairs={{0,8},{8,16},{16,24},{24,32},{32,40},{40,48},{48,56},{56,64},{64,7... | collective-permute-start | bytes 110600 | tf_op jit(solution)/shard_map/ppermute | solution.py:564
  62.6 3.9 %collective-permute-start.8 = (f32[17,8,256]{2,1,0:T(8,128)S(1)}, f32[17,8,256]{2,1,0:T(8,128)S(1)}, u32[]{:S(2)}, u32[]{:S(2)}) collective-permute-start(f32[17,8,256]{2,1,0:T(8,128)S(1)} %get-tuple-element.23), channel_id=1, source_target_pairs={{0,1},{1,2},{2,3},{3,4},{4,5},{5,6},{6,7},{8,9},{9,10},{10,11},{11... | collective-permute-start | bytes 417800 | tf_op jit(solution)/shard_map/ppermute | solution.py:564
  66.5 1.3 collective-permute-start.9
  67.9 4.5 %collective-permute-start.10 = (f32[8,256]{1,0:T(8,128)S(1)}, f32[8,256]{1,0:T(8,128)S(1)}, u32[]{:S(2)}, u32[]{:S(2)}) collective-permute-start(f32[8,256]{1,0:T(8,128)S(1)} %maximum_maximum_fusion), channel_id=1, source_target_pairs={{0,1},{1,2},{2,3},{3,4},{4,5},{5,6},{6,7},{8,9},{9,10},{10,11},{11... | collective-permute-start | bytes 24584 | tf_op jit(solution)/shard_map/ppermute | solution.py:564
  72.5 1.3 collective-permute-start.11
  73.8 0.0 collective-permute-done.10.sA
  73.8 4.8 %collective-permute-done.11.sB = f32[8,256]{1,0:T(8,128)S(1)} collective-permute-done((f32[8,256]{1,0:T(8,128)S(1)}, f32[8,256]{1,0:T(8,128)S(1)}, u32[]{:S(2)}, u32[]{:S(2)}) %collective-permute-start.11) | collective-permute-done | bytes 8224 | tf_op jit(solution)/shard_map/ppermute | solution.py:564
  78.6 8.6 %settle.1 = (f32[32,64,256]{2,1,0:T(8,128)S(1)}, f32[128,16,128]{2,1,0:T(8,128)S(1)}) custom-call(s32[5]{0:T(128)S(1)} %stack.32.flags, f32[32,2,72,128]{3,2,1,0:T(8,128)S(1)} %get-tuple-element.21.local, f32[32,64,256]{2,1,0:T(8,128)S(1)} %copy-done.1, f32[6,64,256]{2,1,0:T(8,128)S(1)} %get-tuple-element.16.coefs, ...), custom_call_target="tpu_custom_call" | custom-call | tf_op jit(solution)/shard_map/settle/pallas_call | solution.py:485
  87.2 0.0 copy-start.3
  87.2 41.6 %all_to_all.5 = f32[128,1,2048]{2,1,0:T(1,128)S(1)} all-to-all(f32[128,1,2048]{2,1,0:T(1,128)S(1)} %bitcast.14), channel_id=1, replica_groups=mesh['gx'=16,'gy'=8] {'gx','gy'}, dimensions={0} | all-to-all | bytes 2097152 | tf_op jit(solution)/shard_map/all_to_all | solution.py:569
  128.8 7.0 %finish.1 = f32[32,64,256]{2,1,0:T(8,128)} custom-call(s32[5]{0:T(128)S(1)} %stack.32.flags, f32[128,16,128]{2,1,0:T(8,128)S(1)} %bitcast.13, f32[64,8192]{1,0:T(8,128)S(1)} %copy-done.3, f32[32,64,256]{2,1,0:T(8,128)S(1)} %get-tuple-element.26.settled, s32[64,256]{1,0:T(8,128)S(1)} %copy-done.4), custom_call_target="tpu_custom_call" | custom-call | tf_op jit(solution)/shard_map/finish/pallas_call | solution.py:548
  (26 shorter events, 0.1 us)
Async XLA Ops:
  0.1 1.6 %copy-start = (f32[32,64,256]{2,1,0:T(8,128)S(1)}, f32[32,64,256]{2,1,0:T(8,128)}, u32[]{:S(2)}) copy-start(f32[32,64,256]{2,1,0:T(8,128)} %source.5) | copy-start | bytes 6291460
  1.7 1.6 %copy-start.2 = (f32[32,64,256]{2,1,0:T(8,128)S(1)}, f32[32,64,256]{2,1,0:T(8,128)}, u32[]{:S(2)}) copy-start(f32[32,64,256]{2,1,0:T(8,128)} %prev.3) | copy-start | bytes 6291460
  3.3 0.8 copy-start.5
  4.1 0.8 copy-start.6
  4.9 0.8 copy-start.7
  5.8 0.8 copy-start.8
  6.6 0.8 copy-start.9
  7.5 0.8 copy-start.10
  8.3 22.4 %copy-start.1 = (f32[32,64,256]{2,1,0:T(8,128)S(1)}, f32[32,64,256]{2,1,0:T(8,128)}, u32[]{:S(2)}) copy-start(f32[32,64,256]{2,1,0:T(8,128)} %source.5) | copy-start | bytes 6291460
  11.3 19.4 %collective-permute-start.4 = (f32[35,8,256]{2,1,0:T(8,128)S(1)}, f32[35,8,256]{2,1,0:T(8,128)S(1)}, u32[]{:S(2)}, u32[]{:S(2)}) collective-permute-start(f32[35,8,256]{2,1,0:T(8,128)S(1)} %get-tuple-element.19), channel_id=1, source_target_pairs={{0,1},{1,2},{2,3},{3,4},{4,5},{5,6},{6,7},{8,9},{9,10},{10,11},{11... | collective-permute-start | bytes 860168 | tf_op jit(solution)/shard_map/ppermute | solution.py:564
  14.8 15.9 %collective-permute-start.5 = (f32[35,8,256]{2,1,0:T(8,128)S(1)}, f32[35,8,256]{2,1,0:T(8,128)S(1)}, u32[]{:S(2)}, u32[]{:S(2)}) collective-permute-start(f32[35,8,256]{2,1,0:T(8,128)S(1)} %get-tuple-element.20), channel_id=1, source_target_pairs={{1,0},{2,1},{3,2},{4,3},{5,4},{6,5},{7,6},{9,8},{10,9},{11,10},{12... | collective-permute-start | bytes 860168 | tf_op jit(solution)/shard_map/ppermute | solution.py:564
  16.1 2.8 %collective-permute-start = (f32[3,64,128]{2,1,0:T(8,128)S(1)}, f32[3,64,128]{2,1,0:T(8,128)S(1)}, u32[]{:S(2)}, u32[]{:S(2)}) collective-permute-start(f32[3,64,128]{2,1,0:T(8,128)S(1)} %get-tuple-element.17), channel_id=1, source_target_pairs={{0,8},{8,16},{16,24},{24,32},{32,40},{40,48},{48,56},{56,64},{64,7... | collective-permute-start | bytes 294920 | tf_op jit(solution)/shard_map/ppermute | solution.py:564
  17.6 5.2 %collective-permute-start.1 = (f32[3,64,128]{2,1,0:T(8,128)S(1)}, f32[3,64,128]{2,1,0:T(8,128)S(1)}, u32[]{:S(2)}, u32[]{:S(2)}) collective-permute-start(f32[3,64,128]{2,1,0:T(8,128)S(1)} %get-tuple-element.18), channel_id=1, source_target_pairs={{8,0},{16,8},{24,16},{32,24},{40,32},{48,40},{56,48},{64,56},{72,6... | collective-permute-start | bytes 294920 | tf_op jit(solution)/shard_map/ppermute | solution.py:564
  22.8 6.5 %collective-permute-start.3 = (f32[2,3,8,128]{3,2,1,0:T(8,128)S(1)}, f32[2,3,8,128]{3,2,1,0:T(8,128)S(1)}, u32[]{:S(2)}, u32[]{:S(2)}) collective-permute-start(f32[2,3,8,128]{3,2,1,0:T(8,128)S(1)} %get-tuple-element.27), channel_id=1, source_target_pairs={{1,0},{2,1},{3,2},{4,3},{5,4},{6,5},{7,6},{9,8},{10,9},{11,10},{12... | collective-permute-start | bytes 73736 | tf_op jit(solution)/shard_map/ppermute | solution.py:564
  24.1 6.7 %collective-permute-start.2 = (f32[2,3,8,128]{3,2,1,0:T(8,128)S(1)}, f32[2,3,8,128]{3,2,1,0:T(8,128)S(1)}, u32[]{:S(2)}, u32[]{:S(2)}) collective-permute-start(f32[2,3,8,128]{3,2,1,0:T(8,128)S(1)} %get-tuple-element.28), channel_id=1, source_target_pairs={{0,1},{1,2},{2,3},{3,4},{4,5},{5,6},{6,7},{8,9},{9,10},{10,11},{11... | collective-permute-start | bytes 73736 | tf_op jit(solution)/shard_map/ppermute | solution.py:564
  30.8 47.8 %copy-start.4 = (s32[64,256]{1,0:T(8,128)S(1)}, s32[64,256]{1,0:T(8,128)}, u32[]{:S(2)}) copy-start(s32[64,256]{1,0:T(8,128)} %ids.3) | copy-start | bytes 196612
  56.4 11.5 %collective-permute-start.7 = (f32[72,128]{1,0:T(8,128)S(1)}, f32[72,128]{1,0:T(8,128)S(1)}, u32[]{:S(2)}, u32[]{:S(2)}) collective-permute-start(f32[72,128]{1,0:T(8,128)S(1)} %get-tuple-element.29), channel_id=1, source_target_pairs={{8,0},{16,8},{24,16},{32,24},{40,32},{48,40},{56,48},{64,56},{72,6... | collective-permute-start | bytes 110600 | tf_op jit(solution)/shard_map/ppermute | solution.py:564
  57.7 10.2 %collective-permute-start.6 = (f32[72,128]{1,0:T(8,128)S(1)}, f32[72,128]{1,0:T(8,128)S(1)}, u32[]{:S(2)}, u32[]{:S(2)}) collective-permute-start(f32[72,128]{1,0:T(8,128)S(1)} %get-tuple-element.30), channel_id=1, source_target_pairs={{0,8},{8,16},{16,24},{24,32},{32,40},{40,48},{48,56},{56,64},{64,7... | collective-permute-start | bytes 110600 | tf_op jit(solution)/shard_map/ppermute | solution.py:564
  62.6 16.0 %collective-permute-start.8 = (f32[17,8,256]{2,1,0:T(8,128)S(1)}, f32[17,8,256]{2,1,0:T(8,128)S(1)}, u32[]{:S(2)}, u32[]{:S(2)}) collective-permute-start(f32[17,8,256]{2,1,0:T(8,128)S(1)} %get-tuple-element.23), channel_id=1, source_target_pairs={{0,1},{1,2},{2,3},{3,4},{4,5},{5,6},{6,7},{8,9},{9,10},{10,11},{11... | collective-permute-start | bytes 417800 | tf_op jit(solution)/shard_map/ppermute | solution.py:564
  66.5 12.0 %collective-permute-start.9 = (f32[17,8,256]{2,1,0:T(8,128)S(1)}, f32[17,8,256]{2,1,0:T(8,128)S(1)}, u32[]{:S(2)}, u32[]{:S(2)}) collective-permute-start(f32[17,8,256]{2,1,0:T(8,128)S(1)} %get-tuple-element.24), channel_id=1, source_target_pairs={{1,0},{2,1},{3,2},{4,3},{5,4},{6,5},{7,6},{9,8},{10,9},{11,10},{12... | collective-permute-start | bytes 417800 | tf_op jit(solution)/shard_map/ppermute | solution.py:564
  67.9 5.9 %collective-permute-start.10 = (f32[8,256]{1,0:T(8,128)S(1)}, f32[8,256]{1,0:T(8,128)S(1)}, u32[]{:S(2)}, u32[]{:S(2)}) collective-permute-start(f32[8,256]{1,0:T(8,128)S(1)} %maximum_maximum_fusion), channel_id=1, source_target_pairs={{0,1},{1,2},{2,3},{3,4},{4,5},{5,6},{6,7},{8,9},{9,10},{10,11},{11... | collective-permute-start | bytes 24584 | tf_op jit(solution)/shard_map/ppermute | solution.py:564
  72.5 6.1 %collective-permute-start.11 = (f32[8,256]{1,0:T(8,128)S(1)}, f32[8,256]{1,0:T(8,128)S(1)}, u32[]{:S(2)}, u32[]{:S(2)}) collective-permute-start(f32[8,256]{1,0:T(8,128)S(1)} %maximum_maximum_fusion.1), channel_id=1, source_target_pairs={{1,0},{2,1},{3,2},{4,3},{5,4},{6,5},{7,6},{9,8},{10,9},{11,10},{12... | collective-permute-start | bytes 24584 | tf_op jit(solution)/shard_map/ppermute | solution.py:564
  87.2 41.6 %copy-start.3 = (f32[64,8192]{1,0:T(8,128)S(1)}, f32[64,8192]{1,0:T(8,128)}, u32[]{:S(2)}) copy-start(f32[64,8192]{1,0:T(8,128)} %inverse.1) | copy-start | bytes 6291460

commit v3 on v2

--- a/solution.py
+++ b/solution.py
@@ -156,14 +156,15 @@
     steps, nr, nc = prev.shape
     block = 8
     big = pl.BlockSpec((block, nr, nc), lambda i: (i, 0, 0))
-    shapes = [(PLANES, nr, nc), (3, nr, LANES), (3, nr, LANES), (steps + PLANES // 2, SUB, nc), (steps + PLANES // 2, SUB, nc)]
+    row_slabs = (steps + PLANES // 2 + 3, SUB, nc)
+    shapes = [(PLANES, nr, nc), (3, nr, LANES), (3, nr, LANES), row_slabs, row_slabs]
     return pl.pallas_call(
         pack_kernel,
         grid=(steps // block,),
         in_specs=[pl.BlockSpec(memory_space=pltpu.SMEM), big, big] + [whole((nr, nc))] * PLANES,
         out_specs=[whole(s) for s in shapes],
         out_shape=[jax.ShapeDtypeStruct(s, jnp.float32) for s in shapes],
-        compiler_params=pltpu.CompilerParams(vmem_limit_bytes=16 * MIB),
+        compiler_params=pltpu.CompilerParams(vmem_limit_bytes=60 * MIB),
         name="pack",
     )(flags, prev, source, *planes)
 
@@ -182,7 +183,11 @@
     return jnp.where(sub < 4, below, above)
 
 
-def sweep_kernel(prev, source, coefs, xL, xR, cA, cB, yA, yB, out, rims, yU, yD, tiles, ctiles, halo, coef, carry):
+def present(x, flag):
+    return jnp.where(flag != 0, x, 0.0)
+
+
+def sweep_kernel(flags, prev, source, coefs, xL, xR, yA, yB, out, rims, yU, yD, tiles, ctiles, halo, coef, carry):
     step0 = pl.program_id(0)
     steps = prev.shape[0]
     total = steps * pl.num_programs(0)
@@ -200,15 +205,21 @@
     def _():
         for array in range(3):
             for side, ref in ((0, xL), (1, xR)):
-                for g in range(SUB):
-                    halo[side, array, rows_of(g), :] = ref[array, rows_of(g), :]
-                halo[side, array, rows_of(SUB), :] = jnp.where(sub < 4, cB[side, array], cA[side, array])
+                slab = total + PLANES // 2 + array
+                below, above = yB[slab, :, tile_of(side)], yA[slab, :, tile_of(side)]
+                if array == 2:
+                    below, above = present(below, flags[3]), present(above, flags[2])
+                parts = [ref[array, rows_of(g), :] for g in range(SUB)] + [jnp.where(sub < 4, below, above)]
+                for g in range(GROUPS):
+                    halo[side, array, rows_of(g), :] = present(parts[g], flags[side]) if array == 2 else parts[g]
         for p in range(5):
             slab = total + p // 2
             for k in range(2):
                 for g in range(SUB):
                     ctiles[p, k, rows_of(g), :] = coefs[p, rows_of(g), tile_of(k)]
-                ctiles[p, k, rows_of(SUB), :] = halo_rows(yB[slab, :, tile_of(k)], yA[slab, :, tile_of(k)], p % 2, sub)
+                ctiles[p, k, rows_of(SUB), :] = halo_rows(
+                    present(yB[slab, :, tile_of(k)], flags[3]), present(yA[slab, :, tile_of(k)], flags[2]), p % 2, sub
+                )
         planes = [
             [window_set(j, ctiles[p, 0, rows(j), :], ctiles[p, 1, rows(j), :], 2, 4 * p) for j in range(STRIDE)]
             for p in range(5)
@@ -249,23 +260,25 @@
             [window_set(j, tiles[odd, a, 0, rows(j), :], tiles[odd, a, 1, rows(j), :], a, 4 * t) for j in range(STRIDE)]
             for a in range(2)
         ]
-        result = []
-        for w in range(3):
-            x0 = [x0s[j][w] for j in range(STRIDE)]
-            full = off_diagonal(x0, [coef[4, w, j] for j in range(STRIDE)], [coef[5, w, j] for j in range(STRIDE)])
-            z = [
-                coef[6, w, j] * ((srcs[j][w] + coef[2, w, j] * carry[w, j]) + (full[j] - coef[3, w, j] * x0[j]))
+        every = range(3)
+        x0 = [[x0s[j][w] for j in range(STRIDE)] for w in every]
+        table = lambda n, w: [coef[n, w, j] for j in range(STRIDE)]
+        full = [off_diagonal(x0[w], table(4, w), table(5, w)) for w in every]
+        z = [
+            [
+                coef[6, w, j] * ((srcs[j][w] + coef[2, w, j] * carry[w, j]) + (full[w][j] - coef[3, w, j] * x0[w][j]))
                 for j in range(STRIDE)
             ]
-            east = [coef[0, w, j] for j in range(STRIDE)]
-            south = [coef[1, w, j] for j in range(STRIDE)]
-            base = [a + b for a, b in zip(z, off_diagonal(z, east, south))]
-            y = base
-            for k in (2, 1, 0):
-                y = off_diagonal(off_diagonal(y, east, south), east, south)
-                ratio = np.float32(Q_COEF[k] / Q_COEF[3])
-                y = [a + ratio * b for a, b in zip(y, base)]
-            result.append([x0[j] + coef[7, w, j] * y[j] for j in range(STRIDE)])
+            for w in every
+        ]
+        apply = lambda v: [off_diagonal(v[w], table(0, w), table(1, w)) for w in every]
+        base = [[a + b for a, b in zip(p, q)] for p, q in zip(z, apply(z))]
+        y = base
+        for k in (2, 1, 0):
+            y = apply(apply(y))
+            ratio = np.float32(Q_COEF[k] / Q_COEF[3])
+            y = [[a + ratio * b for a, b in zip(p, q)] for p, q in zip(y, base)]
+        result = [[x0[w][j] + coef[7, w, j] * y[w][j] for j in range(STRIDE)] for w in every]
         slot = 4 * t
         here = (lanes >= slot) & (lanes < slot + 3)
         for j in range(STRIDE):
@@ -305,17 +318,17 @@
             yU[total // 2, :, tile_of(side)] = jnp.where(sub < 4, first, beyond)
 
 
-def sweep(prev, source, coefs, xL, xR, cA, cB, yA, yB):
+def sweep(flags, prev, source, coefs, xL, xR, yA, yB):
     steps, nr, nc = prev.shape
     block = 4
     big = pl.BlockSpec((block, nr, nc), lambda i: (i, 0, 0))
     ext = GROUPS * SUB
-    consts = (coefs, xL, xR, cA, cB, yA, yB)
-    rest = [(2, ext, LANES), (steps // 2 + 1, SUB, nc), (steps // 2 + 1, SUB, nc)]
+    consts = (coefs, xL, xR, yA, yB)
+    rest = [(2, ext, LANES), (steps // 2 + 2, SUB, nc), (steps // 2 + 2, SUB, nc)]
     return pl.pallas_call(
         sweep_kernel,
         grid=(steps // block,),
-        in_specs=[big, big] + [whole(a.shape) for a in consts],
+        in_specs=[pl.BlockSpec(memory_space=pltpu.SMEM), big, big] + [whole(a.shape) for a in consts],
         out_specs=[pl.BlockSpec((block, 2, ext, LANES), lambda i: (i, 0, 0, 0))] + [whole(s) for s in rest],
         out_shape=[jax.ShapeDtypeStruct(s, jnp.float32) for s in [(steps, 2, ext, LANES)] + rest],
         scratch_shapes=[
@@ -327,7 +340,7 @@
         ],
         compiler_params=pltpu.CompilerParams(vmem_limit_bytes=16 * MIB),
         name="sweep",
-    )(prev, source, *consts)
+    )(flags, prev, source, *consts)
 
 
 def split3(x):
@@ -339,7 +352,7 @@
 
 
 def settle_kernel(
-    flags, local, source, coefs, xL, xR, yA, yB, rims, rL, rR, kA, kB, sA, sB, ids, settled, coarse, pack, ring, edge, before, resid
+    flags, local, source, coefs, xL, xR, yA, yB, rims, rL, rR, kA, kB, ids, settled, coarse, pack, ring, edge, before, resid
 ):
     step0 = pl.program_id(0)
     steps = local.shape[0]
@@ -354,7 +367,9 @@
 
     def halo_plane(p, k):
         slab = total + p // 2
-        return halo_rows(yB[slab, :, tile_of(k)], yA[slab, :, tile_of(k)], p % 2, sub)
+        return halo_rows(
+            present(yB[slab, :, tile_of(k)], flags[3]), present(yA[slab, :, tile_of(k)], flags[2]), p % 2, sub
+        )
 
     @pl.when(step0 == 0)
     def _():
@@ -370,8 +385,9 @@
                 ring[0, k, g] = weight / (weight + copies)
                 ring[1, k, g] = 1.0 / (weight + copies)
             for side, got, xref, lane, keep, back in ((0, rL, xL, 4 * WEIGHT + 2, 0, LANES - 1), (1, rR, xR, 4 * WEIGHT, 2, 1)):
-                arrived = got[rows_of(g), :]
-                fwd_above, fwd_below = sA[:, tile_of(side)], sB[:, tile_of(side)]
+                arrived = present(got[rows_of(g), :], flags[side])
+                fwd_above = present(kA[total // 2 + 1, :, tile_of(side)], flags[side] * flags[2])
+                fwd_below = present(kB[total // 2 + 1, :, tile_of(side)], flags[side] * flags[3])
                 if g == 0:
                     extra = only(sub < 2, fwd_above)
                 elif g == SUB - 1:
@@ -384,9 +400,9 @@
                 if g < SUB:
                     mine = rims[side, rows_of(g), :]
                     if g == 0:
-                        mine = mine + only(sub < 2, kA[total // 2, :, tile_of(side)])
+                        mine = mine + only((sub < 2) & has_up, kA[total // 2, :, tile_of(side)])
                     if g == SUB - 1:
-                        mine = mine + only(sub > 5, kB[total // 2, :, tile_of(side)])
+                        mine = mine + only((sub > 5) & has_down, kB[total // 2, :, tile_of(side)])
                     weight = column(xref, g, lane)
                     copies = 2.0 * (1.0 + down) - 1.0
                     outer = (weight * arrived + (pltpu.roll(mine, back, 1) + extra)) / (weight + copies)
@@ -395,7 +411,7 @@
         for k in range(2):
             for g in range(SUB):
                 own = lambda p: coefs[p, rows_of(g), tile_of(k)]
-                neighbour = column(xL, g, 4 * EAST + 2) if k == 0 else coefs[EAST, rows_of(g), tile_of(0)]
+                neighbour = present(column(xL, g, 4 * EAST + 2), flags[0]) if k == 0 else coefs[EAST, rows_of(g), tile_of(0)]
                 west = west_of(jnp.where(lanes == LANES - 1, neighbour, own(EAST)))
                 above = halo_plane(SOUTH, k) if g == 0 else coefs[SOUTH, rows_of(g - 1), tile_of(k)]
                 north = pltpu.roll(jnp.where(sub == SUB - 1, above, own(SOUTH)), 1, 0)
@@ -417,9 +433,9 @@
                 extra = only(lanes < 2 if k == 0 else lanes > LANES - 3, side)
                 here = local[i, k, rows_of(g), :]
                 if g == 0:
-                    extra = extra + only(sub < 2, from_above)
+                    extra = extra + only((sub < 2) & has_up, from_above)
                 elif g == SUB - 1:
-                    extra = extra + only(sub > 5, from_below)
+                    extra = extra + only((sub > 5) & has_down, from_below)
                 elif g == SUB:
                     extra = extra + here
                     here = jnp.where(sub < 4, from_below, from_above)
@@ -472,16 +488,16 @@
         acc = lax.fori_loop(0, 16, rows4, jnp.zeros((3 * total, 64), jnp.float32))
         sums = acc[:total] + acc[total : 2 * total] + acc[2 * total :]
         block = jnp.concatenate([sums[: total // 2], sums[total // 2 :]], axis=1)
-        coarse[...] = jnp.broadcast_to(block[None], coarse.shape)
-
-
-def settle(flags, local, source, coefs, xL, xR, yA, yB, rims, rL, rR, kA, kB, sA, sB, ids, count):
+        coarse[0] = block
+
+
+def settle(flags, local, source, coefs, xL, xR, yA, yB, rims, rL, rR, kA, kB, ids):
     steps, nr, nc = source.shape
     block = 4
     ext = GROUPS * SUB
     big = pl.BlockSpec((block, nr, nc), lambda i: (i, 0, 0))
-    consts = (coefs, xL, xR, yA, yB, rims, rL, rR, kA, kB, sA, sB, ids)
-    shapes = [(steps, nr, nc), (count, steps // 2, LANES)]
+    consts = (coefs, xL, xR, yA, yB, rims, rL, rR, kA, kB, ids)
+    shapes = [(steps, nr, nc), (1, steps // 2, LANES)]
     return pl.pallas_call(
         settle_kernel,
         grid=(steps // block,),
@@ -515,7 +531,7 @@
     def _():
         for d in range(every.shape[0] // 2):
             for g in range(half // SUB):
-                a, b = every[2 * d, rows_of(g), :], every[2 * d + 1, rows_of(g), :]
+                a, b = [every[2 * d + o, rows_of(g), :] for o in range(2)]
                 stacked[rows_of(g), tile_of(d)] = jnp.where(lanes < LANES // 2, a, pltpu.roll(b, LANES // 2, 1))
                 stacked[half + g * SUB : half + (g + 1) * SUB, tile_of(d)] = jnp.where(
                     lanes < LANES // 2, pltpu.roll(a, LANES // 2, 1), b
@@ -559,15 +575,16 @@
 
 def neighbours(low, high, axis):
     count = lax.axis_size(axis)
-    forward = [(i, i + 1) for i in range(count - 1)]
+    forward = [(i, (i + 1) % count) for i in range(count)]
     backward = [(target, source) for source, target in forward]
     return lax.ppermute(high, axis, forward), lax.ppermute(low, axis, backward)
 
 
-def gather_all(block, axes):
-    count = block.shape[0]
-    every = lax.all_to_all(block.reshape(count, 1, -1), axes, 0, 0)
-    return every.reshape(block.shape)
+def gather_all(block):
+    count = lax.axis_size("gx") * lax.axis_size("gy")
+    block = block.reshape(1, 1, -1)
+    every = lax.all_to_all(jnp.broadcast_to(block, (count,) + block.shape[1:]), ("gx", "gy"), 0, 0)
+    return every.reshape(count, -1, LANES)
 
 
 def shards(
@@ -588,19 +605,20 @@
     planes = (start_state, storage, leakage, cond_east, cond_south, owner_weight)
     coefs, to_left, to_right, to_up, to_down = pack(flags, prev_wave, source, planes)
     xL, xR = neighbours(to_left, to_right, "gx")
+    wide = lambda first, second: jnp.concatenate([first, second], -1)
+    slab = to_up.shape[0] - 3
+    to_up = to_up.at[slab:].set(wide(xL[:, :SUB], xR[:, :SUB]))
+    to_down = to_down.at[slab:].set(wide(xL[:, -SUB:], xR[:, -SUB:]))
     yA, yB = neighbours(to_up, to_down, "gy")
-    both = jnp.stack([xL, xR])
-    cA, cB = neighbours(both[:, :, :SUB], both[:, :, -SUB:], "gy")
-    local, rims, yU, yD = sweep(prev_wave, source, coefs, xL, xR, cA, cB, yA, yB)
+    local, rims, yU, yD = sweep(flags, prev_wave, source, coefs, xL, xR, yA, yB)
     rL, rR = neighbours(rims[0], rims[1], "gx")
+    half = SUB // 2
+    around = wide(rL, rR)
+    yU = yU.at[-1].set(jnp.concatenate([around[:half], around[-half:]], 0))
+    yD = yD.at[-1].set(jnp.concatenate([around[-SUB : -half], around[-SUB - half : -SUB]], 0))
     kA, kB = neighbours(yU, yD, "gy")
-    up = jnp.concatenate([jnp.concatenate([r[0:4], r[68:72]], 0) for r in (rL, rR)], 1)
-    down = jnp.concatenate([jnp.concatenate([r[64:68], r[60:64]], 0) for r in (rL, rR)], 1)
-    sA, sB = neighbours(up, down, "gy")
-    settled, coarse = settle(
-        flags, local, source, coefs, xL, xR, yA, yB, rims, rL, rR, kA, kB, sA, sB, aggregate, nx * ny
-    )
-    every = gather_all(coarse, ("gx", "gy"))
+    settled, coarse = settle(flags, local, source, coefs, xL, xR, yA, yB, rims, rL, rR, kA, kB, aggregate)
+    every = gather_all(coarse)
     return finish(flags, every, coarse_inverse, settled, aggregate)
 
 

time: 137 us -> 113 us (0.82)
  blocking collectives: 41.6 us -> 24.9 us
  starting transfers between devices: 31.3 us -> 16.7 us
  waiting for transfers between devices: 10.2 us -> 20.9 us
  local copies, waits for them, and re-layouts: 8.33 us -> 3.79 us
    ppermute x6 -> x4, starting transfers between devices: 23.5 us -> 2.09 us  [neighbours(): lax.ppermute(high, axis, forward)]
    all_to_all x1, blocking collectives: 41.6 us -> 24.9 us  [gather_all(): lax.all_to_all(jnp.broadcast_to(block, (count,) + block.shape[1:]), ('gx'...]
    ppermute x6 -> x4, waiting for transfers between devices: 1.53 us -> 11.1 us  [neighbours(): lax.ppermute(high, axis, forward)]
    ppermute x6 -> x4, starting transfers between devices: 7.74 us -> 14.6 us  [neighbours(): lax.ppermute(low, axis, backward)]
    unnamed x22 -> x13, local copies, waits for them, and re-layouts: 8.23 us -> 2.61 us
    pallas_call x1, Pallas kernels: 3 us -> 5.64 us  [pack(): pl.pallas_call(pack_kernel, grid=(steps // block,), in_specs=[pl.BlockSpe...]
    pallas_call x1, Pallas kernels: 25.6 us -> 24.1 us  [sweep(): pl.pallas_call(sweep_kernel, grid=(steps // block,), in_specs=[pl.BlockSp...]
    ppermute x6 -> x4, waiting for transfers between devices: 8.64 us -> 9.83 us  [neighbours(): lax.ppermute(low, axis, backward)]
  transfers between devices with their start and end apart: 12 -> 8, of which waited for: 3 -> 8; matrix products, arithmetic and copies ran while one was open for 0% -> 1% of each run, Pallas kernels for 0% -> 0%
where the time goes in v3:
time: 113 us
  Pallas kernels  45 us (40%)
  blocking collectives  24.9 us (22%)
  waiting for transfers between devices  20.9 us (18%)
  starting transfers between devices  16.7 us (15%)
  local copies, waits for them, and re-layouts  3.79 us (3%)
  other arithmetic  1.24 us (1%)
    all_to_all x1, blocking collectives, gather_all(): lax.all_to_all(jnp.broadcast_to(block, (count,) + block.shape[1:]), ('gx'...  24.9 us
    pallas_call x1, Pallas kernels, sweep(): pl.pallas_call(sweep_kernel, grid=(steps // block,), in_specs=[pl.BlockSp...  24.1 us
    ppermute x4, starting transfers between devices, neighbours(): lax.ppermute(low, axis, backward)  14.6 us
    ppermute x4, waiting for transfers between devices, neighbours(): lax.ppermute(high, axis, forward)  11.1 us
    ppermute x4, waiting for transfers between devices, neighbours(): lax.ppermute(low, axis, backward)  9.83 us
    pallas_call x1, Pallas kernels, settle(): pl.pallas_call(settle_kernel, grid=(steps // block,), in_specs=[pl.BlockS...  8.34 us
    pallas_call x1, Pallas kernels, finish(): pl.pallas_call(finish_kernel, grid=(steps // block,), in_specs=[pl.BlockS...  6.98 us
    pallas_call x1, Pallas kernels, pack(): pl.pallas_call(pack_kernel, grid=(steps // block,), in_specs=[pl.BlockSpe...  5.64 us
  transfers between devices with their start and end apart: 8, of which 8 were waited for; matrix products, arithmetic and copies ran while one was open for 1% of the time, Pallas kernels for 0%

profile of v3, /device:TPU:0, one launch (start us, length us, event | category | flops | bytes accessed | tf_op | source)
XLA Modules:
  0.0 112.6 jit_solution(11603601792622699373)
XLA Ops:
  0.0 0.6 stack.23.flags
  0.6 0.0 copy-start
  0.6 5.6 %pack.1 = (f32[6,64,256]{2,1,0:T(8,128)}, f32[3,64,128]{2,1,0:T(8,128)}, f32[3,64,128]{2,1,0:T(8,128)}, f32[38,8,256]{2,1,0:T(8,128)}, f32[38,8,256]{2,1,0:T(8,128)}) custom-call(s32[5]{0:T(128)} %stack.23.flags, f32[32,64,256]{2,1,0:T(8,128)} %prev.3, f32[32,64,256]{2,1,0:T(8,128)} %source.5, f32[64,256]{1,0:T(8,128)} %start.1, f32[64,256]{1,0:T(8,128)} %storage.1, ...), custom_call_target="tpu_custom_call" | custom-call | tf_op jit(solution)/shard_map/pack/pallas_call | solution.py:161
  6.3 0.0 collective-permute-start
  6.3 6.3 %collective-permute-start.1 = (f32[3,64,128]{2,1,0:T(8,128)}, f32[3,64,128]{2,1,0:T(8,128)S(1)}, u32[]{:S(2)}, u32[]{:S(2)}) collective-permute-start(f32[3,64,128]{2,1,0:T(8,128)} %get-tuple-element.66), channel_id=1, source_target_pairs={{8,0},{16,8},{24,16},{32,24},{40,32},{48,40},{56,48},{64,56},{72,6... | collective-permute-start | bytes 294920 | tf_op jit(solution)/shard_map/ppermute | solution.py:580
  12.5 2.4 %collective-permute-done.xL = f32[3,64,128]{2,1,0:T(8,128)S(1)} collective-permute-done((f32[3,64,128]{2,1,0:T(8,128)}, f32[3,64,128]{2,1,0:T(8,128)S(1)}, u32[]{:S(2)}, u32[]{:S(2)}) %collective-permute-start) | collective-permute-done | bytes 98336 | tf_op jit(solution)/shard_map/ppermute | solution.py:580
  15.0 0.1 collective-permute-done.1.xR
  15.1 0.6 maximum_dynamic-update-slice_fusion.1
  15.7 2.9 %collective-permute-start.3 = (f32[38,8,256]{2,1,0:T(8,128)}, f32[38,8,256]{2,1,0:T(8,128)S(1)}, u32[]{:S(2)}, u32[]{:S(2)}) collective-permute-start(f32[38,8,256]{2,1,0:T(8,128)} %maximum_dynamic-update-slice_fusion.1), channel_id=1, source_target_pairs={{1,0},{2,1},{3,2},{4,3},{5,4},{6,5},{7,6},{0,7},{9,8},{10,9},{11,1... | collective-permute-start | bytes 933896 | tf_op jit(solution)/shard_map/ppermute | solution.py:580
  18.6 0.6 maximum_dynamic-update-slice_fusion
  19.2 0.0 collective-permute-start.2
  19.2 5.2 %collective-permute-done.3.yB = f32[38,8,256]{2,1,0:T(8,128)S(1)} collective-permute-done((f32[38,8,256]{2,1,0:T(8,128)}, f32[38,8,256]{2,1,0:T(8,128)S(1)}, u32[]{:S(2)}, u32[]{:S(2)}) %collective-permute-start.3) | collective-permute-done | bytes 311328 | tf_op jit(solution)/shard_map/ppermute | solution.py:580
  24.4 4.8 %collective-permute-done.2.yA = f32[38,8,256]{2,1,0:T(8,128)S(1)} collective-permute-done((f32[38,8,256]{2,1,0:T(8,128)}, f32[38,8,256]{2,1,0:T(8,128)S(1)}, u32[]{:S(2)}, u32[]{:S(2)}) %collective-permute-start.2) | collective-permute-done | bytes 311328 | tf_op jit(solution)/shard_map/ppermute | solution.py:580
  29.2 0.0 copy-done
  29.2 0.0 copy-done.5
  29.2 1.6 %copy-done.1 = f32[32,64,256]{2,1,0:T(8,128)S(1)} copy-done((f32[32,64,256]{2,1,0:T(8,128)S(1)}, f32[32,64,256]{2,1,0:T(8,128)}, u32[]{:S(2)}) %copy-start.1) | copy-done | bytes 2097176
  30.8 1.0 copy-done.3
  31.8 24.1 %sweep.1 = (f32[32,2,72,128]{3,2,1,0:T(8,128)S(1)}, f32[2,72,128]{2,1,0:T(8,128)S(1)}, f32[18,8,256]{2,1,0:T(8,128)S(1)}, f32[18,8,256]{2,1,0:T(8,128)S(1)}) custom-call(s32[5]{0:T(128)S(1)} %copy-done.5, f32[32,64,256]{2,1,0:T(8,128)S(1)} %copy-done.1, f32[32,64,256]{2,1,0:T(8,128)S(1)} %copy-done, f32[6,64,256]{2,1,0:T(8,128)S(1)} %copy-done.3, ...), custom_call_target="tpu_custom_call" | custom-call | tf_op jit(solution)/shard_map/sweep/pallas_call | solution.py:328
  55.9 0.1 collective-permute-start.4
  56.0 5.3 %collective-permute-start.5 = (f32[72,128]{1,0:T(8,128)S(1)}, f32[72,128]{1,0:T(8,128)S(1)}, u32[]{:S(2)}, u32[]{:S(2)}) collective-permute-start(f32[72,128]{1,0:T(8,128)S(1)} %get-tuple-element.83), channel_id=1, source_target_pairs={{8,0},{16,8},{24,16},{32,24},{40,32},{48,40},{56,48},{64,56},{72,6... | collective-permute-start | bytes 110600 | tf_op jit(solution)/shard_map/ppermute | solution.py:580
  61.3 1.6 %collective-permute-done.4.rL = f32[72,128]{1,0:T(8,128)S(1)} collective-permute-done((f32[72,128]{1,0:T(8,128)S(1)}, f32[72,128]{1,0:T(8,128)S(1)}, u32[]{:S(2)}, u32[]{:S(2)}) %collective-permute-start.4) | collective-permute-done | bytes 36896 | tf_op jit(solution)/shard_map/ppermute | solution.py:580
  63.0 1.4 %collective-permute-done.5.rR = f32[72,128]{1,0:T(8,128)S(1)} collective-permute-done((f32[72,128]{1,0:T(8,128)S(1)}, f32[72,128]{1,0:T(8,128)S(1)}, u32[]{:S(2)}, u32[]{:S(2)}) %collective-permute-start.5) | collective-permute-done | bytes 36896 | tf_op jit(solution)/shard_map/ppermute | solution.py:580
  64.4 0.1 collective-permute-start.7
  64.5 2.0 %collective-permute-start.6 = (f32[18,8,256]{2,1,0:T(8,128)S(1)}, f32[18,8,256]{2,1,0:T(8,128)S(1)}, u32[]{:S(2)}, u32[]{:S(2)}) collective-permute-start(f32[18,8,256]{2,1,0:T(8,128)S(1)} %fusion), channel_id=1, source_target_pairs={{0,1},{1,2},{2,3},{3,4},{4,5},{5,6},{6,7},{7,0},{8,9},{9,10},{10,1... | collective-permute-start | bytes 442376 | tf_op jit(solution)/shard_map/ppermute | solution.py:580
  66.6 3.1 %collective-permute-done.7.kB = f32[18,8,256]{2,1,0:T(8,128)S(1)} collective-permute-done((f32[18,8,256]{2,1,0:T(8,128)S(1)}, f32[18,8,256]{2,1,0:T(8,128)S(1)}, u32[]{:S(2)}, u32[]{:S(2)}) %collective-permute-start.7) | collective-permute-done | bytes 147488 | tf_op jit(solution)/shard_map/ppermute | solution.py:580
  69.7 2.2 %collective-permute-done.6.kA = f32[18,8,256]{2,1,0:T(8,128)S(1)} collective-permute-done((f32[18,8,256]{2,1,0:T(8,128)S(1)}, f32[18,8,256]{2,1,0:T(8,128)S(1)}, u32[]{:S(2)}, u32[]{:S(2)}) %collective-permute-start.6) | collective-permute-done | bytes 147488 | tf_op jit(solution)/shard_map/ppermute | solution.py:580
  71.9 0.0 copy-done.4
  71.9 8.3 %settle.1 = (f32[32,64,256]{2,1,0:T(8,128)S(1)}, f32[1,16,128]{2,1,0:T(8,128)S(1)}) custom-call(s32[5]{0:T(128)S(1)} %copy-done.5, f32[32,2,72,128]{3,2,1,0:T(8,128)S(1)} %get-tuple-element.69.local, f32[32,64,256]{2,1,0:T(8,128)S(1)} %copy-done, f32[6,64,256]{2,1,0:T(8,128)S(1)} %copy-done.3, f32[3,64,128]{2,1,0:T(8,128)S(1)} %collective-permute-done.xL, ...), custom_call_target="tpu_custom_call" | custom-call | tf_op jit(solution)/shard_map/settle/pallas_call | solution.py:501
  80.2 0.5 broadcast_in_dim.8
  80.8 24.9 %all_to_all.5 = f32[128,1,2048]{2,1,0:T(1,128)S(1)} all-to-all(f32[128,1,2048]{2,1,0:T(1,128)S(1)} %broadcast_in_dim.8), channel_id=1, replica_groups=mesh['gx'=16,'gy'=8] {'gx','gy'}, dimensions={0} | all-to-all | bytes 2097152 | tf_op jit(solution)/shard_map/all_to_all | solution.py:586
  105.6 0.0 copy-done.2
  105.6 7.0 %finish.1 = f32[32,64,256]{2,1,0:T(8,128)} custom-call(s32[5]{0:T(128)S(1)} %copy-done.5, f32[128,16,128]{2,1,0:T(8,128)S(1)} %bitcast.19, f32[64,8192]{1,0:T(8,128)S(1)} %copy-done.2, f32[32,64,256]{2,1,0:T(8,128)S(1)} %get-tuple-element.74.settled, s32[64,256]{1,0:T(8,128)S(1)} %copy-done.4), custom_call_target="tpu_custom_call" | custom-call | tf_op jit(solution)/shard_map/finish/pallas_call | solution.py:564
  (13 shorter events, 0.1 us)
Async XLA Ops:
  0.6 28.6 %copy-start = (f32[32,64,256]{2,1,0:T(8,128)S(1)}, f32[32,64,256]{2,1,0:T(8,128)}, u32[]{:S(2)}) copy-start(f32[32,64,256]{2,1,0:T(8,128)} %source.5) | copy-start | bytes 6291460
  0.6 28.6 %copy-start.5 = (s32[5]{0:T(128)S(1)}, s32[5]{0:T(128)}, u32[]{:S(2)}) copy-start(s32[5]{0:T(128)} %stack.23.flags) | copy-start | bytes 64
  6.3 8.7 %collective-permute-start = (f32[3,64,128]{2,1,0:T(8,128)}, f32[3,64,128]{2,1,0:T(8,128)S(1)}, u32[]{:S(2)}, u32[]{:S(2)}) collective-permute-start(f32[3,64,128]{2,1,0:T(8,128)} %get-tuple-element.65), channel_id=1, source_target_pairs={{0,8},{8,16},{16,24},{24,32},{32,40},{40,48},{48,56},{56,64},{64,7... | collective-permute-start | bytes 294920 | tf_op jit(solution)/shard_map/ppermute | solution.py:580
  6.3 8.8 %collective-permute-start.1 = (f32[3,64,128]{2,1,0:T(8,128)}, f32[3,64,128]{2,1,0:T(8,128)S(1)}, u32[]{:S(2)}, u32[]{:S(2)}) collective-permute-start(f32[3,64,128]{2,1,0:T(8,128)} %get-tuple-element.66), channel_id=1, source_target_pairs={{8,0},{16,8},{24,16},{32,24},{40,32},{48,40},{56,48},{64,56},{72,6... | collective-permute-start | bytes 294920 | tf_op jit(solution)/shard_map/ppermute | solution.py:580
  15.7 8.7 %collective-permute-start.3 = (f32[38,8,256]{2,1,0:T(8,128)}, f32[38,8,256]{2,1,0:T(8,128)S(1)}, u32[]{:S(2)}, u32[]{:S(2)}) collective-permute-start(f32[38,8,256]{2,1,0:T(8,128)} %maximum_dynamic-update-slice_fusion.1), channel_id=1, source_target_pairs={{1,0},{2,1},{3,2},{4,3},{5,4},{6,5},{7,6},{0,7},{9,8},{10,9},{11,1... | collective-permute-start | bytes 933896 | tf_op jit(solution)/shard_map/ppermute | solution.py:580
  19.2 10.0 %collective-permute-start.2 = (f32[38,8,256]{2,1,0:T(8,128)}, f32[38,8,256]{2,1,0:T(8,128)S(1)}, u32[]{:S(2)}, u32[]{:S(2)}) collective-permute-start(f32[38,8,256]{2,1,0:T(8,128)} %maximum_dynamic-update-slice_fusion), channel_id=1, source_target_pairs={{0,1},{1,2},{2,3},{3,4},{4,5},{5,6},{6,7},{7,0},{8,9},{9,10},{10,1... | collective-permute-start | bytes 933896 | tf_op jit(solution)/shard_map/ppermute | solution.py:580
  29.2 1.6 %copy-start.1 = (f32[32,64,256]{2,1,0:T(8,128)S(1)}, f32[32,64,256]{2,1,0:T(8,128)}, u32[]{:S(2)}) copy-start(f32[32,64,256]{2,1,0:T(8,128)} %prev.3) | copy-start | bytes 6291460
  30.8 1.0 copy-start.3
  31.8 40.0 %copy-start.4 = (s32[64,256]{1,0:T(8,128)S(1)}, s32[64,256]{1,0:T(8,128)}, u32[]{:S(2)}) copy-start(s32[64,256]{1,0:T(8,128)} %ids.3) | copy-start | bytes 196612
  55.9 7.1 %collective-permute-start.4 = (f32[72,128]{1,0:T(8,128)S(1)}, f32[72,128]{1,0:T(8,128)S(1)}, u32[]{:S(2)}, u32[]{:S(2)}) collective-permute-start(f32[72,128]{1,0:T(8,128)S(1)} %get-tuple-element.84), channel_id=1, source_target_pairs={{0,8},{8,16},{16,24},{24,32},{32,40},{40,48},{48,56},{56,64},{64,7... | collective-permute-start | bytes 110600 | tf_op jit(solution)/shard_map/ppermute | solution.py:580
  56.0 8.4 %collective-permute-start.5 = (f32[72,128]{1,0:T(8,128)S(1)}, f32[72,128]{1,0:T(8,128)S(1)}, u32[]{:S(2)}, u32[]{:S(2)}) collective-permute-start(f32[72,128]{1,0:T(8,128)S(1)} %get-tuple-element.83), channel_id=1, source_target_pairs={{8,0},{16,8},{24,16},{32,24},{40,32},{48,40},{56,48},{64,56},{72,6... | collective-permute-start | bytes 110600 | tf_op jit(solution)/shard_map/ppermute | solution.py:580
  64.4 5.2 %collective-permute-start.7 = (f32[18,8,256]{2,1,0:T(8,128)S(1)}, f32[18,8,256]{2,1,0:T(8,128)S(1)}, u32[]{:S(2)}, u32[]{:S(2)}) collective-permute-start(f32[18,8,256]{2,1,0:T(8,128)S(1)} %fusion.1), channel_id=1, source_target_pairs={{1,0},{2,1},{3,2},{4,3},{5,4},{6,5},{7,6},{0,7},{9,8},{10,9},{11,1... | collective-permute-start | bytes 442376 | tf_op jit(solution)/shard_map/ppermute | solution.py:580
  64.5 7.3 %collective-permute-start.6 = (f32[18,8,256]{2,1,0:T(8,128)S(1)}, f32[18,8,256]{2,1,0:T(8,128)S(1)}, u32[]{:S(2)}, u32[]{:S(2)}) collective-permute-start(f32[18,8,256]{2,1,0:T(8,128)S(1)} %fusion), channel_id=1, source_target_pairs={{0,1},{1,2},{2,3},{3,4},{4,5},{5,6},{6,7},{7,0},{8,9},{9,10},{10,1... | collective-permute-start | bytes 442376 | tf_op jit(solution)/shard_map/ppermute | solution.py:580
  80.2 25.4 %copy-start.2 = (f32[64,8192]{1,0:T(8,128)S(1)}, f32[64,8192]{1,0:T(8,128)}, u32[]{:S(2)}) copy-start(f32[64,8192]{1,0:T(8,128)} %inverse.1) | copy-start | bytes 6291460

commit v4 on v3

--- a/solution.py
+++ b/solution.py
@@ -104,69 +104,164 @@
     return pl.BlockSpec(shape, lambda i: (0,) * len(shape))
 
 
-def pack_kernel(flags, prev, source, start, storage, leakage, east, south, weight, coef, to_left, to_right, to_up, to_down):
+def edge_rows_kernel(
+    flags, prev, source, start, storage, leakage, east, south, weight, coef, to_up, to_down, waves, planes, numbers, sems
+):
+    total = prev.shape[0]
+    lanes, sub = lane_ids(), sub_ids()
+    copies = []
+
+    def fetch(source_ref, target_ref):
+        copies.append(pltpu.make_async_copy(source_ref, target_ref, sems.at[len(copies)]))
+        copies[-1].start()
+
+    for end, g in ((0, 0), (1, SUB - 1)):
+        for array, ref in ((0, prev), (1, source)):
+            fetch(ref.at[:, rows_of(g), :], waves.at[array, end])
+    for p, ref in enumerate((start, storage, leakage, east, south)):
+        fetch(ref, planes.at[p])
+    fetch(weight, numbers)
+    for copy in copies:
+        copy.wait()
+
+    def slabs(slab, even, odd):
+        for k in range(2):
+            to_up[slab, :, tile_of(k)] = jnp.where(sub < 4, even(0, k), half_turn(odd(0, k)))
+            to_down[slab, :, tile_of(k)] = jnp.where(sub < 4, half_turn(odd(1, k)), even(1, k))
+
+    for p in range(PLANES):
+        for g in range(SUB):
+            for k in range(2):
+                ref = numbers if p == WEIGHT else planes.at[p]
+                value = ref[rows_of(g), tile_of(k)].astype(jnp.float32)
+                if p == EAST and k == 1:
+                    value = jnp.where((lanes == LANES - 1) & (flags[1] == 0), 0.0, value)
+                if p == SOUTH and g == SUB - 1:
+                    value = jnp.where((sub == SUB - 1) & (flags[3] == 0), 0.0, value)
+                coef[p, rows_of(g), tile_of(k)] = value
+
+    plane = lambda p: lambda end, k: coef[p, rows_of(end * (SUB - 1)), tile_of(k)]
+    for q in range(PLANES // 2):
+        slabs(total + q, plane(2 * q), plane(2 * q + 1))
+
+    def pair(q, _):
+        for array in range(2):
+            wave = lambda i: lambda end, k: waves[array, end, i, :, tile_of(k)]
+            slabs(array * (total // 2) + q, wave(2 * q), wave(2 * q + 1))
+        return 0
+
+    lax.fori_loop(0, total // 2, pair, 0)
+
+
+def edge_rows(flags, prev, source, planes):
+    steps, nr, nc = prev.shape
+    out = jax.ShapeDtypeStruct((steps + PLANES // 2, SUB, nc), jnp.float32)
+    vmem = pl.BlockSpec(memory_space=pltpu.VMEM)
+    return pl.pallas_call(
+        edge_rows_kernel,
+        in_specs=[pl.BlockSpec(memory_space=pltpu.SMEM)] + [pl.BlockSpec(memory_space=pltpu.HBM)] * (2 + PLANES),
+        out_specs=[vmem, vmem, vmem],
+        out_shape=[jax.ShapeDtypeStruct((PLANES, nr, nc), jnp.float32), out, out],
+        scratch_shapes=[
+            pltpu.VMEM((2, 2, steps, SUB, nc), jnp.float32),
+            pltpu.VMEM((PLANES - 1, nr, nc), jnp.float32),
+            pltpu.VMEM((nr, nc), jnp.int32),
+            pltpu.SemaphoreType.DMA((PLANES + 4,)),
+        ],
+        compiler_params=pltpu.CompilerParams(vmem_limit_bytes=60 * MIB),
+        name="rows",
+    )(flags, prev, source, *planes)
+
+
+def put_sides(left, right, array, slot, g, value_left, value_right):
+    lanes = lane_ids()
+    here = (lanes >= slot) & (lanes < slot + 3)
+    left[array, rows_of(g), :] = jnp.where(here, rolled(value_left, slot), left[array, rows_of(g), :])
+    right[array, rows_of(g), :] = jnp.where(here, rolled(value_right, slot + 3), right[array, rows_of(g), :])
+
+
+def pack_kernel(prev, source, coef, to_left, to_right):
     step0 = pl.program_id(0)
     steps = prev.shape[0]
-    total = steps * pl.num_programs(0)
-    lanes, sub = lane_ids(), sub_ids()
-
-    def sides(array, slot, get):
-        here = (lanes >= slot) & (lanes < slot + 3)
-        for g in range(SUB):
-            to_left[array, rows_of(g), :] = jnp.where(here, rolled(get(g, 0), slot), to_left[array, rows_of(g), :])
-            to_right[array, rows_of(g), :] = jnp.where(here, rolled(get(g, 1), slot + 3), to_right[array, rows_of(g), :])
-
-    def slabs(slab, get_even, get_odd):
-        for k in range(2):
-            to_up[slab, :, tile_of(k)] = jnp.where(sub < 4, get_even(0, k), half_turn(get_odd(0, k)))
-            to_down[slab, :, tile_of(k)] = jnp.where(sub < 4, half_turn(get_odd(SUB - 1, k)), get_even(SUB - 1, k))
 
     @pl.when(step0 == 0)
     def _():
         for array in range(3):
             to_left[array] = jnp.zeros_like(to_left[array])
             to_right[array] = jnp.zeros_like(to_right[array])
-        for p, ref in enumerate((start, storage, leakage, east, south, weight)):
+        for p in range(PLANES):
             for g in range(SUB):
-                for k in range(2):
-                    value = ref[rows_of(g), tile_of(k)].astype(jnp.float32)
-                    if p == EAST and k == 1:
-                        value = jnp.where((lanes == LANES - 1) & (flags[1] == 0), 0.0, value)
-                    if p == SOUTH and g == SUB - 1:
-                        value = jnp.where((sub == SUB - 1) & (flags[3] == 0), 0.0, value)
-                    coef[p, rows_of(g), tile_of(k)] = value
-        plane = lambda p: lambda g, k: coef[p, rows_of(g), tile_of(k)]
-        for p in range(PLANES):
-            sides(2, 4 * p, plane(p))
-        for q in range(PLANES // 2):
-            slabs(total + q, plane(2 * q), plane(2 * q + 1))
-
-    def pair(q, _):
+                put_sides(to_left, to_right, 2, 4 * p, g, *[coef[p, rows_of(g), tile_of(k)] for k in range(2)])
+
+    def step(i, _):
         for array, ref in ((0, prev), (1, source)):
-            plane = lambda i: lambda g, k: ref[i, rows_of(g), tile_of(k)]
-            for o in range(2):
-                sides(array, 4 * (step0 * steps + 2 * q + o), plane(2 * q + o))
-            slabs(array * (total // 2) + step0 * (steps // 2) + q, plane(2 * q), plane(2 * q + 1))
+            for g in range(SUB):
+                values = [ref[i, rows_of(g), tile_of(k)] for k in range(2)]
+                put_sides(to_left, to_right, array, 4 * (step0 * steps + i), g, *values)
         return 0
 
-    lax.fori_loop(0, steps // 2, pair, 0)
-
-
-def pack(flags, prev, source, planes):
+    lax.fori_loop(0, steps, step, 0)
+
+
+def pack(prev, source, coefs):
     steps, nr, nc = prev.shape
     block = 8
     big = pl.BlockSpec((block, nr, nc), lambda i: (i, 0, 0))
-    row_slabs = (steps + PLANES // 2 + 3, SUB, nc)
-    shapes = [(PLANES, nr, nc), (3, nr, LANES), (3, nr, LANES), row_slabs, row_slabs]
+    shape = (3, nr, LANES)
     return pl.pallas_call(
         pack_kernel,
         grid=(steps // block,),
-        in_specs=[pl.BlockSpec(memory_space=pltpu.SMEM), big, big] + [whole((nr, nc))] * PLANES,
-        out_specs=[whole(s) for s in shapes],
-        out_shape=[jax.ShapeDtypeStruct(s, jnp.float32) for s in shapes],
-        compiler_params=pltpu.CompilerParams(vmem_limit_bytes=60 * MIB),
+        in_specs=[big, big, whole(coefs.shape)],
+        out_specs=[whole(shape)] * 2,
+        out_shape=[jax.ShapeDtypeStruct(shape, jnp.float32)] * 2,
+        compiler_params=pltpu.CompilerParams(vmem_limit_bytes=16 * MIB),
+        cost_estimate=pl.CostEstimate(flops=20_000_000, bytes_accessed=16_000_000, transcendentals=0),
         name="pack",
-    )(flags, prev, source, *planes)
+    )(prev, source, coefs)
+
+
+def corners_kernel(flags, left, right, yA, yB, to_left, to_right):
+    total = yA.shape[0] - PLANES // 2
+    sub = sub_ids()
+    for array in range(3):
+        for ref, out in ((left, to_left), (right, to_right)):
+            out[array, : SUB * SUB, :] = ref[array]
+            out[array, rows_of(SUB), :] = jnp.zeros((SUB, LANES), jnp.float32)
+
+    def both(slab, array, slot):
+        for odd in range(2):
+            values = [halo_rows(yB[slab, :, tile_of(k)], yA[slab, :, tile_of(k)], odd, sub) for k in range(2)]
+            put_sides(to_left, to_right, array, slot + 4 * odd, SUB, *values)
+
+    for q in range(PLANES // 2):
+        for odd in range(2):
+            values = [
+                halo_rows(
+                    present(yB[total + q, :, tile_of(k)], flags[3]), present(yA[total + q, :, tile_of(k)], flags[2]), odd, sub
+                )
+                for k in range(2)
+            ]
+            put_sides(to_left, to_right, 2, 4 * (2 * q + odd), SUB, *values)
+
+    def pair(q, _):
+        for array in range(2):
+            both(array * (total // 2) + q, array, 8 * q)
+        return 0
+
+    lax.fori_loop(0, total // 2, pair, 0)
+
+
+def corners(flags, left, right, yA, yB):
+    vmem = pl.BlockSpec(memory_space=pltpu.VMEM)
+    out = jax.ShapeDtypeStruct((3, GROUPS * SUB, LANES), jnp.float32)
+    return pl.pallas_call(
+        corners_kernel,
+        in_specs=[pl.BlockSpec(memory_space=pltpu.SMEM)] + [vmem] * 4,
+        out_specs=[vmem, vmem],
+        out_shape=[out, out],
+        compiler_params=pltpu.CompilerParams(vmem_limit_bytes=8 * MIB),
+        name="corners",
+    )(flags, left, right, yA, yB)
 
 
 def windows_of(left, right, halo_left, halo_right, lanes):
@@ -205,13 +300,9 @@
     def _():
         for array in range(3):
             for side, ref in ((0, xL), (1, xR)):
-                slab = total + PLANES // 2 + array
-                below, above = yB[slab, :, tile_of(side)], yA[slab, :, tile_of(side)]
-                if array == 2:
-                    below, above = present(below, flags[3]), present(above, flags[2])
-                parts = [ref[array, rows_of(g), :] for g in range(SUB)] + [jnp.where(sub < 4, below, above)]
                 for g in range(GROUPS):
-                    halo[side, array, rows_of(g), :] = present(parts[g], flags[side]) if array == 2 else parts[g]
+                    value = ref[array, rows_of(g), :]
+                    halo[side, array, rows_of(g), :] = present(value, flags[side]) if array == 2 else value
         for p in range(5):
             slab = total + p // 2
             for k in range(2):
@@ -603,17 +694,15 @@
     nx, ny = lax.axis_size("gx"), lax.axis_size("gy")
     flags = jnp.stack([gx, nx - 1 - gx, gy, ny - 1 - gy, (gx * ny + gy) * coarse_inverse.shape[0]]).astype(jnp.int32)
     planes = (start_state, storage, leakage, cond_east, cond_south, owner_weight)
-    coefs, to_left, to_right, to_up, to_down = pack(flags, prev_wave, source, planes)
+    coefs, to_up, to_down = edge_rows(flags, prev_wave, source, planes)
+    yA, yB = neighbours(to_up, to_down, "gy")
+    to_left, to_right = pack(prev_wave, source, coefs)
+    to_left, to_right = corners(flags, to_left, to_right, yA, yB)
     xL, xR = neighbours(to_left, to_right, "gx")
-    wide = lambda first, second: jnp.concatenate([first, second], -1)
-    slab = to_up.shape[0] - 3
-    to_up = to_up.at[slab:].set(wide(xL[:, :SUB], xR[:, :SUB]))
-    to_down = to_down.at[slab:].set(wide(xL[:, -SUB:], xR[:, -SUB:]))
-    yA, yB = neighbours(to_up, to_down, "gy")
     local, rims, yU, yD = sweep(flags, prev_wave, source, coefs, xL, xR, yA, yB)
     rL, rR = neighbours(rims[0], rims[1], "gx")
     half = SUB // 2
-    around = wide(rL, rR)
+    around = jnp.concatenate([rL, rR], -1)
     yU = yU.at[-1].set(jnp.concatenate([around[:half], around[-half:]], 0))
     yD = yD.at[-1].set(jnp.concatenate([around[-SUB : -half], around[-SUB - half : -SUB]], 0))
     kA, kB = neighbours(yU, yD, "gy")

time: 113 us -> 110 us (0.973)
  waiting for transfers between devices: 20.9 us -> 11.9 us
  starting transfers between devices: 16.7 us -> 20.1 us
  Pallas kernels: 45 us -> 48.2 us
  other arithmetic: 1.24 us -> 0.02 us
    ppermute x4, waiting for transfers between devices: 9.83 us -> 2.74 us  [neighbours(): lax.ppermute(low, axis, backward)]
    ppermute x4, starting transfers between devices: 14.6 us -> 18.4 us  [neighbours(): lax.ppermute(low, axis, backward)]
    pallas_call x1 -> x3, Pallas kernels: 5.64 us -> 8.72 us  [the longest x1 3.54 us: pack(): pl.pallas_call(pack_kernel, grid=(steps // block,), in_specs=[big, big, w...]
    ppermute x4, waiting for transfers between devices: 11.1 us -> 9.13 us  [neighbours(): lax.ppermute(high, axis, forward)]
    scatter x2 -> x0, other arithmetic: 1.22 us -> none  [the longest x1 0.61 us: shards(): to_up = to_up.at[slab:].set(wide(xL[:, :SUB], xR[:, :SUB]))]
    unnamed x13 -> x17, local copies, waits for them, and re-layouts: 2.61 us -> 2.62 us
  transfers between devices with their start and end apart: 8 -> 8, of which waited for: 8 -> 6; matrix products, arithmetic and copies ran while one was open for 1% -> 0% of each run, Pallas kernels for 0% -> 3%
where the time goes in v4:
time: 110 us; the launch traced here: 109 us
  Pallas kernels  48.2 us (44%)
  blocking collectives  25.2 us (23%)
  starting transfers between devices  20.1 us (18%)
  waiting for transfers between devices  11.9 us (11%)
  local copies, waits for them, and re-layouts  3.81 us (3%)
    all_to_all x1, blocking collectives, gather_all(): lax.all_to_all(jnp.broadcast_to(block, (count,) + block.shape[1:]), ('gx'...  25.2 us
    pallas_call x1, Pallas kernels, sweep(): pl.pallas_call(sweep_kernel, grid=(steps // block,), in_specs=[pl.BlockSp...  24.1 us
    ppermute x4, starting transfers between devices, neighbours(): lax.ppermute(low, axis, backward)  18.4 us
    ppermute x4, waiting for transfers between devices, neighbours(): lax.ppermute(high, axis, forward)  9.13 us
    pallas_call x1, Pallas kernels, settle(): pl.pallas_call(settle_kernel, grid=(steps // block,), in_specs=[pl.BlockS...  8.45 us
    pallas_call x1, Pallas kernels, finish(): pl.pallas_call(finish_kernel, grid=(steps // block,), in_specs=[pl.BlockS...  7.01 us
    pallas_call x1, Pallas kernels, pack(): pl.pallas_call(pack_kernel, grid=(steps // block,), in_specs=[big, big, w...  3.54 us
    pallas_call x1, Pallas kernels, edge_rows(): pl.pallas_call(edge_rows_kernel, in_specs=[pl.BlockSpec(memory_space=pltp...  3.21 us
  transfers between devices with their start and end apart: 8, of which 6 were waited for; matrix products, arithmetic and copies ran while one was open for 0% of the time, Pallas kernels for 3%

profile of v4, /device:TPU:0, one launch (start us, length us, event | category | flops | bytes accessed | tf_op | source)
XLA Modules:
  0.0 109.4 jit_solution(15923982392594576477)
XLA Ops:
  0.0 0.6 stack.23.flags
  0.6 3.2 %rows.1 = (f32[6,64,256]{2,1,0:T(8,128)}, f32[35,8,256]{2,1,0:T(8,128)}, f32[35,8,256]{2,1,0:T(8,128)}) custom-call(s32[5]{0:T(128)} %stack.23.flags, f32[32,64,256]{2,1,0:T(8,128)} %prev.5, f32[32,64,256]{2,1,0:T(8,128)} %source.7, f32[64,256]{1,0:T(8,128)} %start.1, f32[64,256]{1,0:T(8,128)} %storage.1, f32[64,256]{1,0:T(8,128)} %leakage.1, ...), custom_call_target="tpu_custom_call" | custom-call | tf_op jit(solution)/shard_map/rows/pallas_call | solution.py:160
  3.9 1.6 %collective-permute-start = (f32[35,8,256]{2,1,0:T(8,128)}, f32[35,8,256]{2,1,0:T(8,128)S(1)}, u32[]{:S(2)}, u32[]{:S(2)}) collective-permute-start(f32[35,8,256]{2,1,0:T(8,128)} %get-tuple-element.45), channel_id=1, source_target_pairs={{0,1},{1,2},{2,3},{3,4},{4,5},{5,6},{6,7},{7,0},{8,9},{9,10},{10,1... | collective-permute-start | bytes 860168 | tf_op jit(solution)/shard_map/ppermute | solution.py:671
  5.5 2.6 %collective-permute-start.1 = (f32[35,8,256]{2,1,0:T(8,128)}, f32[35,8,256]{2,1,0:T(8,128)S(1)}, u32[]{:S(2)}, u32[]{:S(2)}) collective-permute-start(f32[35,8,256]{2,1,0:T(8,128)} %get-tuple-element.46), channel_id=1, source_target_pairs={{1,0},{2,1},{3,2},{4,3},{5,4},{6,5},{7,6},{0,7},{9,8},{10,9},{11,1... | collective-permute-start | bytes 860168 | tf_op jit(solution)/shard_map/ppermute | solution.py:671
  8.1 0.0 copy-done
  8.1 1.6 %copy-done.1 = f32[32,64,256]{2,1,0:T(8,128)S(1)} copy-done((f32[32,64,256]{2,1,0:T(8,128)S(1)}, f32[32,64,256]{2,1,0:T(8,128)}, u32[]{:S(2)}) %copy-start.1) | copy-done | bytes 2097176
  9.7 1.0 copy-done.3
  10.7 3.5 %pack.1 = (f32[3,64,128]{2,1,0:T(8,128)S(1)}, f32[3,64,128]{2,1,0:T(8,128)S(1)}) custom-call(f32[32,64,256]{2,1,0:T(8,128)S(1)} %copy-done.1, f32[32,64,256]{2,1,0:T(8,128)S(1)} %copy-done, f32[6,64,256]{2,1,0:T(8,128)S(1)} %copy-done.3), custom_call_target="tpu_custom_call" | custom-call | flops 20000000 | bytes 16000000 | tf_op jit(solution)/shard_map/pack/pallas_call | solution.py:211
  14.2 0.6 collective-permute-done.yA
  14.8 0.0 collective-permute-done.1.yB
  14.8 0.0 copy-done.7
  14.8 2.0 %corners.1 = (f32[3,72,128]{2,1,0:T(8,128)S(1)}, f32[3,72,128]{2,1,0:T(8,128)S(1)}) custom-call(s32[5]{0:T(128)S(1)} %copy-done.7, f32[3,64,128]{2,1,0:T(8,128)S(1)} %get-tuple-element.43.left, f32[3,64,128]{2,1,0:T(8,128)S(1)} %get-tuple-element.44.right, f32[35,8,256]{2,1,0:T(8,128)S(1)} %collective-permute-done.yA, ...), custom_call_target="tpu_custom_call" | custom-call | tf_op jit(solution)/shard_map/corners/pallas_call | solution.py:257
  16.8 0.0 collective-permute-start.2
  16.8 0.0 copy-start.4
  16.9 0.0 copy-start.6
  16.9 5.4 %collective-permute-start.3 = (f32[3,72,128]{2,1,0:T(8,128)S(1)}, f32[3,72,128]{2,1,0:T(8,128)S(1)}, u32[]{:S(2)}, u32[]{:S(2)}) collective-permute-start(f32[3,72,128]{2,1,0:T(8,128)S(1)} %get-tuple-element.48), channel_id=1, source_target_pairs={{8,0},{16,8},{24,16},{32,24},{40,32},{48,40},{56,48},{64,56},{72,6... | collective-permute-start | bytes 331784 | tf_op jit(solution)/shard_map/ppermute | solution.py:671
  22.2 2.4 %collective-permute-done.2.xL = f32[3,72,128]{2,1,0:T(8,128)S(1)} collective-permute-done((f32[3,72,128]{2,1,0:T(8,128)S(1)}, f32[3,72,128]{2,1,0:T(8,128)S(1)}, u32[]{:S(2)}, u32[]{:S(2)}) %collective-permute-start.2) | collective-permute-done | bytes 110624 | tf_op jit(solution)/shard_map/ppermute | solution.py:671
  24.6 0.0 collective-permute-done.3.xR
  24.6 24.1 %sweep.1 = (f32[32,2,72,128]{3,2,1,0:T(8,128)S(1)}, f32[2,72,128]{2,1,0:T(8,128)S(1)}, f32[18,8,256]{2,1,0:T(8,128)S(1)}, f32[18,8,256]{2,1,0:T(8,128)S(1)}) custom-call(s32[5]{0:T(128)S(1)} %copy-done.7, f32[32,64,256]{2,1,0:T(8,128)S(1)} %copy-done.2, f32[32,64,256]{2,1,0:T(8,128)S(1)} %copy-done, f32[6,64,256]{2,1,0:T(8,128)S(1)} %copy-done.3, ...), custom_call_target="tpu_custom_call" | custom-call | tf_op jit(solution)/shard_map/sweep/pallas_call | solution.py:419
  48.7 0.1 collective-permute-start.4
  48.8 5.5 %collective-permute-start.5 = (f32[72,128]{1,0:T(8,128)S(1)}, f32[72,128]{1,0:T(8,128)S(1)}, u32[]{:S(2)}, u32[]{:S(2)}) collective-permute-start(f32[72,128]{1,0:T(8,128)S(1)} %get-tuple-element.59), channel_id=1, source_target_pairs={{8,0},{16,8},{24,16},{32,24},{40,32},{48,40},{56,48},{64,56},{72,6... | collective-permute-start | bytes 110600 | tf_op jit(solution)/shard_map/ppermute | solution.py:671
  54.3 1.6 %collective-permute-done.4.rL = f32[72,128]{1,0:T(8,128)S(1)} collective-permute-done((f32[72,128]{1,0:T(8,128)S(1)}, f32[72,128]{1,0:T(8,128)S(1)}, u32[]{:S(2)}, u32[]{:S(2)}) %collective-permute-start.4) | collective-permute-done | bytes 36896 | tf_op jit(solution)/shard_map/ppermute | solution.py:671
  55.8 0.1 collective-permute-done.5.rR
  55.9 5.0 %collective-permute-start.7 = (f32[18,8,256]{2,1,0:T(8,128)S(1)}, f32[18,8,256]{2,1,0:T(8,128)S(1)}, u32[]{:S(2)}, u32[]{:S(2)}) collective-permute-start(f32[18,8,256]{2,1,0:T(8,128)S(1)} %fusion.1), channel_id=1, source_target_pairs={{1,0},{2,1},{3,2},{4,3},{5,4},{6,5},{7,6},{0,7},{9,8},{10,9},{11,1... | collective-permute-start | bytes 442376 | tf_op jit(solution)/shard_map/ppermute | solution.py:671
  60.9 0.0 collective-permute-start.6
  60.9 2.7 %collective-permute-done.7.kB = f32[18,8,256]{2,1,0:T(8,128)S(1)} collective-permute-done((f32[18,8,256]{2,1,0:T(8,128)S(1)}, f32[18,8,256]{2,1,0:T(8,128)S(1)}, u32[]{:S(2)}, u32[]{:S(2)}) %collective-permute-start.7) | collective-permute-done | bytes 147488 | tf_op jit(solution)/shard_map/ppermute | solution.py:671
  63.6 4.6 %collective-permute-done.6.kA = f32[18,8,256]{2,1,0:T(8,128)S(1)} collective-permute-done((f32[18,8,256]{2,1,0:T(8,128)S(1)}, f32[18,8,256]{2,1,0:T(8,128)S(1)}, u32[]{:S(2)}, u32[]{:S(2)}) %collective-permute-start.6) | collective-permute-done | bytes 147488 | tf_op jit(solution)/shard_map/ppermute | solution.py:671
  68.1 8.4 %settle.1 = (f32[32,64,256]{2,1,0:T(8,128)S(1)}, f32[1,16,128]{2,1,0:T(8,128)S(1)}) custom-call(s32[5]{0:T(128)S(1)} %copy-done.7, f32[32,2,72,128]{3,2,1,0:T(8,128)S(1)} %get-tuple-element.49.local, f32[32,64,256]{2,1,0:T(8,128)S(1)} %copy-done, f32[6,64,256]{2,1,0:T(8,128)S(1)} %copy-done.4, f32[3,72,128]{2,1,0:T(8,128)S(1)} %collective-permute-done.2.xL, ...), custom_call_target="tpu_custom_call" | custom-call | tf_op jit(solution)/shard_map/settle/pallas_call | solution.py:592
  76.6 0.5 broadcast_in_dim.8
  77.1 25.2 %all_to_all.5 = f32[128,1,2048]{2,1,0:T(1,128)S(1)} all-to-all(f32[128,1,2048]{2,1,0:T(1,128)S(1)} %broadcast_in_dim.8), channel_id=1, replica_groups=mesh['gx'=16,'gy'=8] {'gx','gy'}, dimensions={0} | all-to-all | bytes 2097152 | tf_op jit(solution)/shard_map/all_to_all | solution.py:677
  102.3 0.0 copy-done.5
  102.3 7.0 %finish.1 = f32[32,64,256]{2,1,0:T(8,128)} custom-call(s32[5]{0:T(128)S(1)} %copy-done.7, f32[128,16,128]{2,1,0:T(8,128)S(1)} %bitcast.19, f32[64,8192]{1,0:T(8,128)S(1)} %copy-done.5, f32[32,64,256]{2,1,0:T(8,128)S(1)} %get-tuple-element.54.settled, s32[64,256]{1,0:T(8,128)S(1)} %copy-done.6), custom_call_target="tpu_custom_call" | custom-call | tf_op jit(solution)/shard_map/finish/pallas_call | solution.py:655
  (15 shorter events, 0.1 us)
Async XLA Ops:
  0.6 7.4 %copy-start = (f32[32,64,256]{2,1,0:T(8,128)S(1)}, f32[32,64,256]{2,1,0:T(8,128)}, u32[]{:S(2)}) copy-start(f32[32,64,256]{2,1,0:T(8,128)} %source.7) | copy-start | bytes 6291460
  3.9 11.0 %collective-permute-start = (f32[35,8,256]{2,1,0:T(8,128)}, f32[35,8,256]{2,1,0:T(8,128)S(1)}, u32[]{:S(2)}, u32[]{:S(2)}) collective-permute-start(f32[35,8,256]{2,1,0:T(8,128)} %get-tuple-element.45), channel_id=1, source_target_pairs={{0,1},{1,2},{2,3},{3,4},{4,5},{5,6},{6,7},{7,0},{8,9},{9,10},{10,1... | collective-permute-start | bytes 860168 | tf_op jit(solution)/shard_map/ppermute | solution.py:671
  5.5 9.3 %collective-permute-start.1 = (f32[35,8,256]{2,1,0:T(8,128)}, f32[35,8,256]{2,1,0:T(8,128)S(1)}, u32[]{:S(2)}, u32[]{:S(2)}) collective-permute-start(f32[35,8,256]{2,1,0:T(8,128)} %get-tuple-element.46), channel_id=1, source_target_pairs={{1,0},{2,1},{3,2},{4,3},{5,4},{6,5},{7,6},{0,7},{9,8},{10,9},{11,1... | collective-permute-start | bytes 860168 | tf_op jit(solution)/shard_map/ppermute | solution.py:671
  8.1 1.6 %copy-start.1 = (f32[32,64,256]{2,1,0:T(8,128)S(1)}, f32[32,64,256]{2,1,0:T(8,128)}, u32[]{:S(2)}) copy-start(f32[32,64,256]{2,1,0:T(8,128)} %prev.5) | copy-start | bytes 6291460
  9.7 1.0 copy-start.3
  10.6 4.2 %copy-start.7 = (s32[5]{0:T(128)S(1)}, s32[5]{0:T(128)}, u32[]{:S(2)}) copy-start(s32[5]{0:T(128)} %stack.23.flags) | copy-start | bytes 64
  10.6 14.0 %copy-start.2 = (f32[32,64,256]{2,1,0:T(8,128)S(1)}, f32[32,64,256]{2,1,0:T(8,128)}, u32[]{:S(2)}) copy-start(f32[32,64,256]{2,1,0:T(8,128)} %prev.5) | copy-start | bytes 6291460
  16.8 7.8 %collective-permute-start.2 = (f32[3,72,128]{2,1,0:T(8,128)S(1)}, f32[3,72,128]{2,1,0:T(8,128)S(1)}, u32[]{:S(2)}, u32[]{:S(2)}) collective-permute-start(f32[3,72,128]{2,1,0:T(8,128)S(1)} %get-tuple-element.47), channel_id=1, source_target_pairs={{0,8},{8,16},{16,24},{24,32},{32,40},{40,48},{48,56},{56,64},{64,7... | collective-permute-start | bytes 331784 | tf_op jit(solution)/shard_map/ppermute | solution.py:671
  16.8 51.3 %copy-start.4 = (f32[6,64,256]{2,1,0:T(8,128)S(1)}, f32[6,64,256]{2,1,0:T(8,128)}, u32[]{:S(2)}) copy-start(f32[6,64,256]{2,1,0:T(8,128)} %get-tuple-element.42.coef.coefs) | copy-start | bytes 1179652
  16.9 51.3 %copy-start.6 = (s32[64,256]{1,0:T(8,128)S(1)}, s32[64,256]{1,0:T(8,128)}, u32[]{:S(2)}) copy-start(s32[64,256]{1,0:T(8,128)} %ids.3) | copy-start | bytes 196612
  16.9 7.8 %collective-permute-start.3 = (f32[3,72,128]{2,1,0:T(8,128)S(1)}, f32[3,72,128]{2,1,0:T(8,128)S(1)}, u32[]{:S(2)}, u32[]{:S(2)}) collective-permute-start(f32[3,72,128]{2,1,0:T(8,128)S(1)} %get-tuple-element.48), channel_id=1, source_target_pairs={{8,0},{16,8},{24,16},{32,24},{40,32},{48,40},{56,48},{64,56},{72,6... | collective-permute-start | bytes 331784 | tf_op jit(solution)/shard_map/ppermute | solution.py:671
  48.7 7.1 %collective-permute-start.4 = (f32[72,128]{1,0:T(8,128)S(1)}, f32[72,128]{1,0:T(8,128)S(1)}, u32[]{:S(2)}, u32[]{:S(2)}) collective-permute-start(f32[72,128]{1,0:T(8,128)S(1)} %get-tuple-element.60), channel_id=1, source_target_pairs={{0,8},{8,16},{16,24},{24,32},{32,40},{40,48},{48,56},{56,64},{64,7... | collective-permute-start | bytes 110600 | tf_op jit(solution)/shard_map/ppermute | solution.py:671
  48.8 7.1 %collective-permute-start.5 = (f32[72,128]{1,0:T(8,128)S(1)}, f32[72,128]{1,0:T(8,128)S(1)}, u32[]{:S(2)}, u32[]{:S(2)}) collective-permute-start(f32[72,128]{1,0:T(8,128)S(1)} %get-tuple-element.59), channel_id=1, source_target_pairs={{8,0},{16,8},{24,16},{32,24},{40,32},{48,40},{56,48},{64,56},{72,6... | collective-permute-start | bytes 110600 | tf_op jit(solution)/shard_map/ppermute | solution.py:671
  55.9 7.6 %collective-permute-start.7 = (f32[18,8,256]{2,1,0:T(8,128)S(1)}, f32[18,8,256]{2,1,0:T(8,128)S(1)}, u32[]{:S(2)}, u32[]{:S(2)}) collective-permute-start(f32[18,8,256]{2,1,0:T(8,128)S(1)} %fusion.1), channel_id=1, source_target_pairs={{1,0},{2,1},{3,2},{4,3},{5,4},{6,5},{7,6},{0,7},{9,8},{10,9},{11,1... | collective-permute-start | bytes 442376 | tf_op jit(solution)/shard_map/ppermute | solution.py:671
  60.9 7.3 %collective-permute-start.6 = (f32[18,8,256]{2,1,0:T(8,128)S(1)}, f32[18,8,256]{2,1,0:T(8,128)S(1)}, u32[]{:S(2)}, u32[]{:S(2)}) collective-permute-start(f32[18,8,256]{2,1,0:T(8,128)S(1)} %fusion), channel_id=1, source_target_pairs={{0,1},{1,2},{2,3},{3,4},{4,5},{5,6},{6,7},{7,0},{8,9},{9,10},{10,1... | collective-permute-start | bytes 442376 | tf_op jit(solution)/shard_map/ppermute | solution.py:671
  76.6 25.7 %copy-start.5 = (f32[64,8192]{1,0:T(8,128)S(1)}, f32[64,8192]{1,0:T(8,128)}, u32[]{:S(2)}) copy-start(f32[64,8192]{1,0:T(8,128)} %inverse.1) | copy-start | bytes 6291460

commit v5 on v4

--- a/solution.py
+++ b/solution.py
@@ -645,7 +645,7 @@
                 out[i, rows_of(g), tile_of(k)] = settled[i, rows_of(g), tile_of(k)] + jnp.take_along_axis(row, picked, axis=1)
         return 0
 
-    lax.fori_loop(0, steps, step, 0)
+    lax.fori_loop(0, steps, step, 0, unroll=True)
 
 
 def finish(flags, every, inverse, settled, ids):

time: 110 us -> 108 us (0.982)
  Pallas kernels: 48.2 us -> 46.6 us
    pallas_call x1, Pallas kernels: 7.01 us -> 5.38 us  [finish(): pl.pallas_call(finish_kernel, grid=(steps // block,), in_specs=[pl.BlockS...]
where the time goes in v5:
time: 108 us
  Pallas kernels  46.6 us (43%)
  blocking collectives  25.2 us (23%)
  starting transfers between devices  20.1 us (19%)
  waiting for transfers between devices  11.9 us (11%)
  local copies, waits for them, and re-layouts  3.81 us (4%)
    all_to_all x1, blocking collectives, gather_all(): lax.all_to_all(jnp.broadcast_to(block, (count,) + block.shape[1:]), ('gx'...  25.2 us
    pallas_call x1, Pallas kernels, sweep(): pl.pallas_call(sweep_kernel, grid=(steps // block,), in_specs=[pl.BlockSp...  24.1 us
    ppermute x4, starting transfers between devices, neighbours(): lax.ppermute(low, axis, backward)  18.4 us
    ppermute x4, waiting for transfers between devices, neighbours(): lax.ppermute(high, axis, forward)  9.13 us
    pallas_call x1, Pallas kernels, settle(): pl.pallas_call(settle_kernel, grid=(steps // block,), in_specs=[pl.BlockS...  8.45 us
    pallas_call x1, Pallas kernels, finish(): pl.pallas_call(finish_kernel, grid=(steps // block,), in_specs=[pl.BlockS...  5.38 us
    pallas_call x1, Pallas kernels, pack(): pl.pallas_call(pack_kernel, grid=(steps // block,), in_specs=[big, big, w...  3.54 us
    pallas_call x1, Pallas kernels, edge_rows(): pl.pallas_call(edge_rows_kernel, in_specs=[pl.BlockSpec(memory_space=pltp...  3.21 us
  transfers between devices with their start and end apart: 8, of which 6 were waited for; matrix products, arithmetic and copies ran while one was open for 0% of the time, Pallas kernels for 3%

profile of v5, /device:TPU:0, one launch (start us, length us, event | category | flops | bytes accessed | tf_op | source)
XLA Modules:
  0.0 107.7 jit_solution(18131592663230730616)
XLA Ops:
  0.0 0.6 stack.23.flags
  0.6 3.2 %rows.1 = (f32[6,64,256]{2,1,0:T(8,128)}, f32[35,8,256]{2,1,0:T(8,128)}, f32[35,8,256]{2,1,0:T(8,128)}) custom-call(s32[5]{0:T(128)} %stack.23.flags, f32[32,64,256]{2,1,0:T(8,128)} %prev.5, f32[32,64,256]{2,1,0:T(8,128)} %source.7, f32[64,256]{1,0:T(8,128)} %start.1, f32[64,256]{1,0:T(8,128)} %storage.1, f32[64,256]{1,0:T(8,128)} %leakage.1, ...), custom_call_target="tpu_custom_call" | custom-call | tf_op jit(solution)/shard_map/rows/pallas_call | solution.py:160
  3.9 1.6 %collective-permute-start = (f32[35,8,256]{2,1,0:T(8,128)}, f32[35,8,256]{2,1,0:T(8,128)S(1)}, u32[]{:S(2)}, u32[]{:S(2)}) collective-permute-start(f32[35,8,256]{2,1,0:T(8,128)} %get-tuple-element.45), channel_id=1, source_target_pairs={{0,1},{1,2},{2,3},{3,4},{4,5},{5,6},{6,7},{7,0},{8,9},{9,10},{10,1... | collective-permute-start | bytes 860168 | tf_op jit(solution)/shard_map/ppermute | solution.py:671
  5.5 2.6 %collective-permute-start.1 = (f32[35,8,256]{2,1,0:T(8,128)}, f32[35,8,256]{2,1,0:T(8,128)S(1)}, u32[]{:S(2)}, u32[]{:S(2)}) collective-permute-start(f32[35,8,256]{2,1,0:T(8,128)} %get-tuple-element.46), channel_id=1, source_target_pairs={{1,0},{2,1},{3,2},{4,3},{5,4},{6,5},{7,6},{0,7},{9,8},{10,9},{11,1... | collective-permute-start | bytes 860168 | tf_op jit(solution)/shard_map/ppermute | solution.py:671
  8.1 0.0 copy-done
  8.1 1.6 %copy-done.1 = f32[32,64,256]{2,1,0:T(8,128)S(1)} copy-done((f32[32,64,256]{2,1,0:T(8,128)S(1)}, f32[32,64,256]{2,1,0:T(8,128)}, u32[]{:S(2)}) %copy-start.1) | copy-done | bytes 2097176
  9.7 1.0 copy-done.3
  10.7 3.5 %pack.1 = (f32[3,64,128]{2,1,0:T(8,128)S(1)}, f32[3,64,128]{2,1,0:T(8,128)S(1)}) custom-call(f32[32,64,256]{2,1,0:T(8,128)S(1)} %copy-done.1, f32[32,64,256]{2,1,0:T(8,128)S(1)} %copy-done, f32[6,64,256]{2,1,0:T(8,128)S(1)} %copy-done.3), custom_call_target="tpu_custom_call" | custom-call | flops 20000000 | bytes 16000000 | tf_op jit(solution)/shard_map/pack/pallas_call | solution.py:211
  14.2 0.6 collective-permute-done.yA
  14.8 0.0 collective-permute-done.1.yB
  14.8 0.0 copy-done.7
  14.8 2.0 %corners.1 = (f32[3,72,128]{2,1,0:T(8,128)S(1)}, f32[3,72,128]{2,1,0:T(8,128)S(1)}) custom-call(s32[5]{0:T(128)S(1)} %copy-done.7, f32[3,64,128]{2,1,0:T(8,128)S(1)} %get-tuple-element.43.left, f32[3,64,128]{2,1,0:T(8,128)S(1)} %get-tuple-element.44.right, f32[35,8,256]{2,1,0:T(8,128)S(1)} %collective-permute-done.yA, ...), custom_call_target="tpu_custom_call" | custom-call | tf_op jit(solution)/shard_map/corners/pallas_call | solution.py:257
  16.8 0.0 collective-permute-start.2
  16.8 0.0 copy-start.4
  16.9 0.0 copy-start.6
  16.9 5.4 %collective-permute-start.3 = (f32[3,72,128]{2,1,0:T(8,128)S(1)}, f32[3,72,128]{2,1,0:T(8,128)S(1)}, u32[]{:S(2)}, u32[]{:S(2)}) collective-permute-start(f32[3,72,128]{2,1,0:T(8,128)S(1)} %get-tuple-element.48), channel_id=1, source_target_pairs={{8,0},{16,8},{24,16},{32,24},{40,32},{48,40},{56,48},{64,56},{72,6... | collective-permute-start | bytes 331784 | tf_op jit(solution)/shard_map/ppermute | solution.py:671
  22.2 2.4 %collective-permute-done.2.xL = f32[3,72,128]{2,1,0:T(8,128)S(1)} collective-permute-done((f32[3,72,128]{2,1,0:T(8,128)S(1)}, f32[3,72,128]{2,1,0:T(8,128)S(1)}, u32[]{:S(2)}, u32[]{:S(2)}) %collective-permute-start.2) | collective-permute-done | bytes 110624 | tf_op jit(solution)/shard_map/ppermute | solution.py:671
  24.6 0.0 collective-permute-done.3.xR
  24.6 24.1 %sweep.1 = (f32[32,2,72,128]{3,2,1,0:T(8,128)S(1)}, f32[2,72,128]{2,1,0:T(8,128)S(1)}, f32[18,8,256]{2,1,0:T(8,128)S(1)}, f32[18,8,256]{2,1,0:T(8,128)S(1)}) custom-call(s32[5]{0:T(128)S(1)} %copy-done.7, f32[32,64,256]{2,1,0:T(8,128)S(1)} %copy-done.2, f32[32,64,256]{2,1,0:T(8,128)S(1)} %copy-done, f32[6,64,256]{2,1,0:T(8,128)S(1)} %copy-done.3, ...), custom_call_target="tpu_custom_call" | custom-call | tf_op jit(solution)/shard_map/sweep/pallas_call | solution.py:419
  48.7 0.1 collective-permute-start.4
  48.8 5.5 %collective-permute-start.5 = (f32[72,128]{1,0:T(8,128)S(1)}, f32[72,128]{1,0:T(8,128)S(1)}, u32[]{:S(2)}, u32[]{:S(2)}) collective-permute-start(f32[72,128]{1,0:T(8,128)S(1)} %get-tuple-element.59), channel_id=1, source_target_pairs={{8,0},{16,8},{24,16},{32,24},{40,32},{48,40},{56,48},{64,56},{72,6... | collective-permute-start | bytes 110600 | tf_op jit(solution)/shard_map/ppermute | solution.py:671
  54.3 1.6 %collective-permute-done.4.rL = f32[72,128]{1,0:T(8,128)S(1)} collective-permute-done((f32[72,128]{1,0:T(8,128)S(1)}, f32[72,128]{1,0:T(8,128)S(1)}, u32[]{:S(2)}, u32[]{:S(2)}) %collective-permute-start.4) | collective-permute-done | bytes 36896 | tf_op jit(solution)/shard_map/ppermute | solution.py:671
  55.8 0.1 collective-permute-done.5.rR
  55.9 5.0 %collective-permute-start.7 = (f32[18,8,256]{2,1,0:T(8,128)S(1)}, f32[18,8,256]{2,1,0:T(8,128)S(1)}, u32[]{:S(2)}, u32[]{:S(2)}) collective-permute-start(f32[18,8,256]{2,1,0:T(8,128)S(1)} %fusion.1), channel_id=1, source_target_pairs={{1,0},{2,1},{3,2},{4,3},{5,4},{6,5},{7,6},{0,7},{9,8},{10,9},{11,1... | collective-permute-start | bytes 442376 | tf_op jit(solution)/shard_map/ppermute | solution.py:671
  60.9 0.0 collective-permute-start.6
  60.9 2.7 %collective-permute-done.7.kB = f32[18,8,256]{2,1,0:T(8,128)S(1)} collective-permute-done((f32[18,8,256]{2,1,0:T(8,128)S(1)}, f32[18,8,256]{2,1,0:T(8,128)S(1)}, u32[]{:S(2)}, u32[]{:S(2)}) %collective-permute-start.7) | collective-permute-done | bytes 147488 | tf_op jit(solution)/shard_map/ppermute | solution.py:671
  63.6 4.6 %collective-permute-done.6.kA = f32[18,8,256]{2,1,0:T(8,128)S(1)} collective-permute-done((f32[18,8,256]{2,1,0:T(8,128)S(1)}, f32[18,8,256]{2,1,0:T(8,128)S(1)}, u32[]{:S(2)}, u32[]{:S(2)}) %collective-permute-start.6) | collective-permute-done | bytes 147488 | tf_op jit(solution)/shard_map/ppermute | solution.py:671
  68.1 8.4 %settle.1 = (f32[32,64,256]{2,1,0:T(8,128)S(1)}, f32[1,16,128]{2,1,0:T(8,128)S(1)}) custom-call(s32[5]{0:T(128)S(1)} %copy-done.7, f32[32,2,72,128]{3,2,1,0:T(8,128)S(1)} %get-tuple-element.49.local, f32[32,64,256]{2,1,0:T(8,128)S(1)} %copy-done, f32[6,64,256]{2,1,0:T(8,128)S(1)} %copy-done.4, f32[3,72,128]{2,1,0:T(8,128)S(1)} %collective-permute-done.2.xL, ...), custom_call_target="tpu_custom_call" | custom-call | tf_op jit(solution)/shard_map/settle/pallas_call | solution.py:592
  76.6 0.5 broadcast_in_dim.8
  77.1 25.2 %all_to_all.5 = f32[128,1,2048]{2,1,0:T(1,128)S(1)} all-to-all(f32[128,1,2048]{2,1,0:T(1,128)S(1)} %broadcast_in_dim.8), channel_id=1, replica_groups=mesh['gx'=16,'gy'=8] {'gx','gy'}, dimensions={0} | all-to-all | bytes 2097152 | tf_op jit(solution)/shard_map/all_to_all | solution.py:677
  102.3 0.0 copy-done.5
  102.3 5.4 %finish.1 = f32[32,64,256]{2,1,0:T(8,128)} custom-call(s32[5]{0:T(128)S(1)} %copy-done.7, f32[128,16,128]{2,1,0:T(8,128)S(1)} %bitcast.19, f32[64,8192]{1,0:T(8,128)S(1)} %copy-done.5, f32[32,64,256]{2,1,0:T(8,128)S(1)} %get-tuple-element.54.settled, s32[64,256]{1,0:T(8,128)S(1)} %copy-done.6), custom_call_target="tpu_custom_call" | custom-call | tf_op jit(solution)/shard_map/finish/pallas_call | solution.py:655
  (15 shorter events, 0.1 us)
Async XLA Ops:
  0.6 7.4 %copy-start = (f32[32,64,256]{2,1,0:T(8,128)S(1)}, f32[32,64,256]{2,1,0:T(8,128)}, u32[]{:S(2)}) copy-start(f32[32,64,256]{2,1,0:T(8,128)} %source.7) | copy-start | bytes 6291460
  3.9 11.0 %collective-permute-start = (f32[35,8,256]{2,1,0:T(8,128)}, f32[35,8,256]{2,1,0:T(8,128)S(1)}, u32[]{:S(2)}, u32[]{:S(2)}) collective-permute-start(f32[35,8,256]{2,1,0:T(8,128)} %get-tuple-element.45), channel_id=1, source_target_pairs={{0,1},{1,2},{2,3},{3,4},{4,5},{5,6},{6,7},{7,0},{8,9},{9,10},{10,1... | collective-permute-start | bytes 860168 | tf_op jit(solution)/shard_map/ppermute | solution.py:671
  5.5 9.3 %collective-permute-start.1 = (f32[35,8,256]{2,1,0:T(8,128)}, f32[35,8,256]{2,1,0:T(8,128)S(1)}, u32[]{:S(2)}, u32[]{:S(2)}) collective-permute-start(f32[35,8,256]{2,1,0:T(8,128)} %get-tuple-element.46), channel_id=1, source_target_pairs={{1,0},{2,1},{3,2},{4,3},{5,4},{6,5},{7,6},{0,7},{9,8},{10,9},{11,1... | collective-permute-start | bytes 860168 | tf_op jit(solution)/shard_map/ppermute | solution.py:671
  8.1 1.6 %copy-start.1 = (f32[32,64,256]{2,1,0:T(8,128)S(1)}, f32[32,64,256]{2,1,0:T(8,128)}, u32[]{:S(2)}) copy-start(f32[32,64,256]{2,1,0:T(8,128)} %prev.5) | copy-start | bytes 6291460
  9.7 1.0 copy-start.3
  10.6 4.2 %copy-start.7 = (s32[5]{0:T(128)S(1)}, s32[5]{0:T(128)}, u32[]{:S(2)}) copy-start(s32[5]{0:T(128)} %stack.23.flags) | copy-start | bytes 64
  10.6 14.0 %copy-start.2 = (f32[32,64,256]{2,1,0:T(8,128)S(1)}, f32[32,64,256]{2,1,0:T(8,128)}, u32[]{:S(2)}) copy-start(f32[32,64,256]{2,1,0:T(8,128)} %prev.5) | copy-start | bytes 6291460
  16.8 7.8 %collective-permute-start.2 = (f32[3,72,128]{2,1,0:T(8,128)S(1)}, f32[3,72,128]{2,1,0:T(8,128)S(1)}, u32[]{:S(2)}, u32[]{:S(2)}) collective-permute-start(f32[3,72,128]{2,1,0:T(8,128)S(1)} %get-tuple-element.47), channel_id=1, source_target_pairs={{0,8},{8,16},{16,24},{24,32},{32,40},{40,48},{48,56},{56,64},{64,7... | collective-permute-start | bytes 331784 | tf_op jit(solution)/shard_map/ppermute | solution.py:671
  16.8 51.3 %copy-start.4 = (f32[6,64,256]{2,1,0:T(8,128)S(1)}, f32[6,64,256]{2,1,0:T(8,128)}, u32[]{:S(2)}) copy-start(f32[6,64,256]{2,1,0:T(8,128)} %get-tuple-element.42.coef.coefs) | copy-start | bytes 1179652
  16.9 51.3 %copy-start.6 = (s32[64,256]{1,0:T(8,128)S(1)}, s32[64,256]{1,0:T(8,128)}, u32[]{:S(2)}) copy-start(s32[64,256]{1,0:T(8,128)} %ids.3) | copy-start | bytes 196612
  16.9 7.8 %collective-permute-start.3 = (f32[3,72,128]{2,1,0:T(8,128)S(1)}, f32[3,72,128]{2,1,0:T(8,128)S(1)}, u32[]{:S(2)}, u32[]{:S(2)}) collective-permute-start(f32[3,72,128]{2,1,0:T(8,128)S(1)} %get-tuple-element.48), channel_id=1, source_target_pairs={{8,0},{16,8},{24,16},{32,24},{40,32},{48,40},{56,48},{64,56},{72,6... | collective-permute-start | bytes 331784 | tf_op jit(solution)/shard_map/ppermute | solution.py:671
  48.7 7.1 %collective-permute-start.4 = (f32[72,128]{1,0:T(8,128)S(1)}, f32[72,128]{1,0:T(8,128)S(1)}, u32[]{:S(2)}, u32[]{:S(2)}) collective-permute-start(f32[72,128]{1,0:T(8,128)S(1)} %get-tuple-element.60), channel_id=1, source_target_pairs={{0,8},{8,16},{16,24},{24,32},{32,40},{40,48},{48,56},{56,64},{64,7... | collective-permute-start | bytes 110600 | tf_op jit(solution)/shard_map/ppermute | solution.py:671
  48.8 7.1 %collective-permute-start.5 = (f32[72,128]{1,0:T(8,128)S(1)}, f32[72,128]{1,0:T(8,128)S(1)}, u32[]{:S(2)}, u32[]{:S(2)}) collective-permute-start(f32[72,128]{1,0:T(8,128)S(1)} %get-tuple-element.59), channel_id=1, source_target_pairs={{8,0},{16,8},{24,16},{32,24},{40,32},{48,40},{56,48},{64,56},{72,6... | collective-permute-start | bytes 110600 | tf_op jit(solution)/shard_map/ppermute | solution.py:671
  55.9 7.6 %collective-permute-start.7 = (f32[18,8,256]{2,1,0:T(8,128)S(1)}, f32[18,8,256]{2,1,0:T(8,128)S(1)}, u32[]{:S(2)}, u32[]{:S(2)}) collective-permute-start(f32[18,8,256]{2,1,0:T(8,128)S(1)} %fusion.1), channel_id=1, source_target_pairs={{1,0},{2,1},{3,2},{4,3},{5,4},{6,5},{7,6},{0,7},{9,8},{10,9},{11,1... | collective-permute-start | bytes 442376 | tf_op jit(solution)/shard_map/ppermute | solution.py:671
  60.9 7.3 %collective-permute-start.6 = (f32[18,8,256]{2,1,0:T(8,128)S(1)}, f32[18,8,256]{2,1,0:T(8,128)S(1)}, u32[]{:S(2)}, u32[]{:S(2)}) collective-permute-start(f32[18,8,256]{2,1,0:T(8,128)S(1)} %fusion), channel_id=1, source_target_pairs={{0,1},{1,2},{2,3},{3,4},{4,5},{5,6},{6,7},{7,0},{8,9},{9,10},{10,1... | collective-permute-start | bytes 442376 | tf_op jit(solution)/shard_map/ppermute | solution.py:671
  76.6 25.7 %copy-start.5 = (f32[64,8192]{1,0:T(8,128)S(1)}, f32[64,8192]{1,0:T(8,128)}, u32[]{:S(2)}) copy-start(f32[64,8192]{1,0:T(8,128)} %inverse.1) | copy-start | bytes 6291460
